TPU v7x, 32 devices: a whole 2x2x4 slice. The times are simulated.
32 devices in a mesh: frag: 2 (over y), dev: 4 (over z), col: 4 (over x, core).
Axes of the slice: x: 2, y: 2, z: 4, core: 2. Of those that a mesh axis runs over, the one named last changes fastest.
Arguments:
- factor_ac: bfloat16 [3072, 32, 512], P(('frag', 'dev'), None, 'col'), parts along dimension 0, may hold values from -0.95703125 to 0.95703125
- factor_bd: bfloat16 [3072, 32, 512], P(('frag', 'col'), None, 'dev'), parts along dimension 0, may hold values from -0.95703125 to 0.95703125
- amplitudes: bfloat16 [1024, 512, 256], P(('frag', 'col'), 'dev'), parts along dimension 0, may hold values from -0.015625 to 0.015625
Outputs:
- ladder_residual: float32 [64, 32, 256], P(('frag', 'col'), 'dev'), parts along dimension 0
There are 2 independent parts, one for each index of `frag`. A program takes and returns all parts, laid end to end along the dimension named above; each array names one. Nothing has to cross between parts.
All inputs are finite; a program needn't handle non-finite values.
Results may differ from a plain program's by a relative error of at most 0.0029.
Values may be sent and summed in bfloat16 or wider, within the bound.
No kernel may reach another device: no remote copies, remote signals or barrier semaphores. Data moves between devices by JAX's collectives and lax.ppermute only.
A program may use at most 128 MiB of HBM per device.

v0:
```python
import jax
import jax.numpy as jnp
from jax import lax
from jax.sharding import PartitionSpec as P


def local(factor_ac, factor_bd, amplitudes):
    whole_bd = lax.all_gather(factor_bd, "col", axis=0, tiled=True)
    whole_ac = lax.all_gather(factor_ac, "dev", axis=0, tiled=True)
    integral = jnp.einsum("qac,qbd->abdc", whole_ac, whole_bd, preferred_element_type=jnp.float32)
    integral = integral.astype(jnp.bfloat16)
    partial_sum = jnp.einsum(
        "abdc,cdp->abp", integral, amplitudes, preferred_element_type=jnp.float32
    )
    reduced = lax.psum_scatter(partial_sum, "col", scatter_dimension=0, tiled=True)
    result = lax.psum_scatter(reduced, "dev", scatter_dimension=1, tiled=True)
    return result


def solution(mesh):
    placed = (
        P(("frag", "dev"), None, "col"),
        P(("frag", "col"), None, "dev"),
        P(("frag", "col"), "dev", None),
    )
    return jax.shard_map(
        local,
        mesh=mesh,
        in_specs=placed,
        out_specs=P(("frag", "col"), "dev", None),
        check_vma=False,
    )
```

profile of v0, /device:TPU:0, one launch (start us, length us, event | category | flops | bytes accessed | tf_op | source)
XLA Modules:
  0.0 486.7 jit_solution(12520333404982088385)
XLA Ops:
  6.5 0.0 all-gather.5.cloned.1.call-start
  6.5 0.7 all-gather.5.cloned.1.call-update
  7.3 0.0 all-gather.3.cloned.1.call-start
  7.3 0.7 all-gather.3.cloned.1.call-update
  8.0 0.0 reduce-scatter.3.cloned.1.call-start
  8.1 221.8 %all-gather.5.cloned.1.call-done = bf16[1536,32,128]{2,1,0:T(8,128)(2,1)} async-done(((bf16[384,32,128]{2,1,0:T(8,128)(2,1)}), bf16[1536,32,128]{2,1,0:T(8,128)(2,1)}) %all-gather.5.cloned.1.call-update) | async-done | bytes 12582928 | tf_op jit(solution)/shard_map/all_gather | solution.py:9
  229.8 81.9 %all-gather.3.cloned.1.call-done = bf16[1536,32,128]{2,1,0:T(8,128)(2,1)} async-done(((bf16[384,32,128]{2,1,0:T(8,128)(2,1)}), bf16[1536,32,128]{2,1,0:T(8,128)(2,1)}) %all-gather.3.cloned.1.call-update) | async-done | bytes 12582928 | tf_op jit(solution)/shard_map/all_gather | solution.py:8
  311.7 61.4 %fusion.3 = bf16[32,128,32,128]{3,1,2,0:T(8,128)(2,1)} fusion(bf16[1536,32,128,1]{2,1,0,3:T(8,128)(2,1)} %bitcast.15, bf16[1536,32,128,1]{2,1,0,3:T(8,128)(2,1)} %bitcast.16), kind=kOutput, calls=%fused_computation.3 | convolution fusion | flops 51539607552 | bytes 58720256 | tf_op jit(solution)/shard_map/qac,qbd->abdc/dot_general | solution.py:10
  373.0 42.6 %copy.6 = bf16[32,128,32,128]{1,0,3,2:T(8,128)(2,1)} copy(bf16[32,128,32,128]{3,1,2,0:T(8,128)(2,1)} %fusion.3) | data formatting | bytes 67108864 | tf_op jit(solution)/shard_map/qac,qbd->abdc/dot_general | solution.py:10
  415.6 17.4 %fusion.7 = f32[32,32,256]{2,1,0:T(8,128)} fusion(bf16[128,128,256]{2,1,0:T(8,128)(2,1)} %param.5, bf16[32,128,32,128]{1,0,3,2:T(8,128)(2,1)} %copy.6), kind=kOutput, calls=%fused_computation.7 | convolution fusion | flops 8589934592 | bytes 42991616 | tf_op jit(solution)/shard_map/abdc,cdp->abp/dot_general | solution.py:12
  433.0 0.0 reduce-scatter.3.cloned.1.call-update
  433.1 0.0 reduce-scatter.5.cloned.1.call-start
  433.1 24.9 %reduce-scatter.3.cloned.1.call-done = f32[8,32,256]{2,1,0:T(8,128)} async-done(((f32[32,32,256]{2,1,0:T(8,128)}), f32[8,32,256]{2,1,0:T(8,128)}) %reduce-scatter.3.cloned.1.call-update) | async-done | bytes 262160 | tf_op jit(solution)/shard_map/reduce_scatter | solution.py:15
  458.0 0.0 reduce-scatter.5.cloned.1.call-update
  458.1 22.1 %reduce-scatter.5.cloned.1.call-done = f32[8,8,256]{2,1,0:T(8,128)} async-done(((f32[8,32,256]{2,1,0:T(8,128)}), f32[8,8,256]{2,1,0:T(8,128)}) %reduce-scatter.5.cloned.1.call-update) | async-done | bytes 65552 | tf_op jit(solution)/shard_map/reduce_scatter | solution.py:16
Async XLA Ops:
  6.5 223.3 %all-gather.5.cloned.1.call-start = ((), (), s32[]{:S(2)}) async-start(), calls=%async_computation.3 | async-start | bytes 15728640 | tf_op jit(solution)/shard_map/all_gather | solution.py:9
  7.3 304.4 %all-gather.3.cloned.1.call-start = ((), (), s32[]{:S(2)}) async-start(), calls=%async_computation.2 | async-start | bytes 15728640 | tf_op jit(solution)/shard_map/all_gather | solution.py:8
  8.0 450.0 %reduce-scatter.3.cloned.1.call-start = ((), (), s32[]{:S(2)}) async-start(), calls=%async_computation.4 | async-start | bytes 1310720 | tf_op jit(solution)/shard_map/reduce_scatter | solution.py:15
  433.1 47.1 %reduce-scatter.5.cloned.1.call-start = ((), (), s32[]{:S(2)}) async-start(), calls=%async_computation.5 | async-start | bytes 327680 | tf_op jit(solution)/shard_map/reduce_scatter | solution.py:16
Sparse Core Ops, SparseCore 0:
  8.9 220.8 all-gather.4
  231.4 80.2 all-gather.2
  433.2 24.8 reduce-scatter.2
  460.1 19.9 reduce-scatter.4
where the time goes:
time: 488 us; the launch traced here: 487 us
  waiting for transfers between devices  352 us (72%)
  matrix products  78.7 us (16%)
  local copies, waits for them, and re-layouts  42.6 us (9%)
  between operations  13.1 us (3%)
    all_gather x1, waiting for transfers between devices, local(): whole_ac = lax.all_gather(factor_ac, 'dev', axis=0, tiled=True)  222 us
    all_gather x1, waiting for transfers between devices, local(): whole_bd = lax.all_gather(factor_bd, 'col', axis=0, tiled=True)  81.9 us
    dot_general x1, matrix products, local(): jnp.einsum('qac,qbd->abdc', whole_ac, whole_bd, preferred_element_type=jn...  61.4 us
    dot_general x1, local copies, waits for them, and re-layouts, local(): jnp.einsum('qac,qbd->abdc', whole_ac, whole_bd, preferred_element_type=jn...  42.6 us
    reduce_scatter x1, waiting for transfers between devices, local(): lax.psum_scatter(partial_sum, 'col', scatter_dimension=0, tiled=True)  24.9 us
    reduce_scatter x1, waiting for transfers between devices, local(): result = lax.psum_scatter(reduced, 'dev', scatter_dimension=1, tiled=True)  22.1 us
    dot_general x1, matrix products, local(): jnp.einsum('abdc,cdp->abp', integral, amplitudes, preferred_element_type=...  17.4 us
  transfers between devices with their start and end apart: 4, of which 4 were waited for; matrix products, arithmetic and copies ran while one was open for 0% of the time, Pallas kernels for 0%

commit v1 on v0

v1 whole, which is shorter than its diff:
```python
import functools

import jax
import jax.numpy as jnp
from jax import lax
from jax.experimental import pallas as pl
from jax.experimental.pallas import tpu as pltpu
from jax.sharding import PartitionSpec as P


F32 = jnp.float32
ROWS = 8
WIDE = 4


def plain(factor_ac, factor_bd, amplitudes):
    whole_bd = lax.all_gather(factor_bd, "col", axis=0, tiled=True)
    whole_ac = lax.all_gather(factor_ac, "dev", axis=0, tiled=True)
    integral = jnp.einsum("qac,qbd->abdc", whole_ac, whole_bd, preferred_element_type=F32)
    integral = integral.astype(jnp.bfloat16)
    partial_sum = jnp.einsum("abdc,cdp->abp", integral, amplitudes, preferred_element_type=F32)
    reduced = lax.psum_scatter(partial_sum, "col", scatter_dimension=0, tiled=True)
    return lax.psum_scatter(reduced, "dev", scatter_dimension=1, tiled=True)


def block_kernel(first, starts, rows, c_start, where, own, near, far0, far1, end0, end1,
                 b0, b1, b2, b3, t_ref, r_ref, out_ref, a_v, b_v, t_v, i_v, a_sem, b_sem, t_sem):
    depth = own.shape[1]
    count = rows // ROWS
    b_count, _, width = b0.shape
    steps = b_count // WIDE
    sources = (own, near, far0, far1, end0, end1)

    def a_copy(index, slot):
        source = sources[index].at[pl.ds(starts[index], rows), :]
        column = pl.ds(pl.multiple_of(where[slot] * depth, 128), depth)
        return pltpu.make_async_copy(source, a_v.at[:, column], a_sem.at[slot])

    def b_copy(step, slot):
        span = pl.ds(step * WIDE, WIDE)
        deep = pl.ds(pl.multiple_of(where[4 + slot] * depth, 128), depth)
        return pltpu.make_async_copy((b0, b1, b2, b3)[slot].at[span], b_v.at[span, deep, :], b_sem.at[step, slot])

    t_copy = pltpu.make_async_copy(t_ref.at[pl.ds(c_start, count)], t_v, t_sem)
    a_copy(0, 0).start()
    a_copy(1, 1).start()

    @pl.when(where[8] == 1)
    def _():
        a_copy(4, 2).start()
        a_copy(5, 3).start()

    @pl.when(where[8] == 0)
    def _():
        a_copy(2, 2).start()
        a_copy(3, 3).start()

    for slot in range(4):
        b_copy(0, slot).start()

    def begin(step, carry):
        for slot in range(4):
            b_copy(step, slot).start()
        return carry

    lax.fori_loop(1, steps, begin, 0)
    t_copy.start()
    for slot in range(4):
        a_copy(slot, slot).wait()

    def contract(step, carry):
        for slot in range(4):
            b_copy(step, slot).wait()
        right = jnp.concatenate([b_v[step * WIDE + m] for m in range(WIDE)], axis=1)
        part = jnp.dot(a_v[...], right, preferred_element_type=F32).reshape(count, ROWS, WIDE * width)
        tall = jnp.concatenate([part[:, :, m * width:(m + 1) * width] for m in range(WIDE)], axis=1)
        i_v[:, pl.ds(pl.multiple_of(WIDE * ROWS * step, WIDE * ROWS), WIDE * ROWS), :] = tall.astype(jnp.bfloat16)
        return carry

    lax.fori_loop(0, steps, contract, 0)
    t_copy.wait()
    group = 4
    out_ref[...] = jnp.zeros(out_ref.shape, F32) if first else r_ref[...]

    def absorb(g, carry):
        c = g * group
        left = jnp.concatenate([i_v[c + m] for m in range(group)], axis=1)
        amp = t_v[pl.ds(c, group)].reshape(group * width, t_v.shape[2])
        out_ref[...] += jnp.dot(left, amp, preferred_element_type=F32)
        return carry

    lax.fori_loop(0, count // group, absorb, 0, unroll=2)


def block(first, where, pieces, starts, rows, quarters, amplitudes, c_start, total):
    depth = pieces[0].shape[1]
    count = rows // ROWS
    b_count, _, width = quarters[0].shape
    pairs = amplitudes.shape[2]
    q_count = depth * 4
    shape = (b_count * ROWS, pairs)
    flops = 2 * rows * q_count * b_count * width + 2 * count * width * b_count * ROWS * pairs
    anywhere = pl.BlockSpec(memory_space=pl.ANY)
    inside = pl.BlockSpec(memory_space=pltpu.VMEM)
    return pl.pallas_call(
        functools.partial(block_kernel, first, starts, rows, c_start),
        in_specs=[pl.BlockSpec(memory_space=pltpu.SMEM)] + [anywhere] * 11 + [inside],
        out_specs=inside,
        scratch_shapes=[
            pltpu.VMEM((rows, q_count), jnp.bfloat16),
            pltpu.VMEM((b_count, q_count, width), jnp.bfloat16),
            pltpu.VMEM((count, width, pairs), jnp.bfloat16),
            pltpu.VMEM((count, b_count * ROWS, width), jnp.bfloat16),
            pltpu.SemaphoreType.DMA((4,)),
            pltpu.SemaphoreType.DMA((b_count // WIDE, 4)),
            pltpu.SemaphoreType.DMA,
        ],
        out_shape=jax.ShapeDtypeStruct(shape, F32),
        compiler_params=pltpu.CompilerParams(vmem_limit_bytes=66977792),
        cost_estimate=pl.CostEstimate(
            flops=flops,
            transcendentals=0,
            bytes_accessed=2 * (b_count * q_count * width + count * width * pairs + rows * q_count),
        ),
    )(where, *pieces, *quarters, amplitudes, total)


INNER = [(1, 2), (2, 1)]
TO_END = [(1, 0), (2, 3)]


def shuffled(n, mask):
    return [(i, i ^ mask) for i in range(n)]


def laddered(n_dev, n_col, factor_ac, factor_bd, amplitudes):
    depth, a_count, c_count = factor_ac.shape
    _, b_count, _ = factor_bd.shape
    pairs = amplitudes.shape[2]
    dev, col = lax.axis_index("dev").astype(jnp.int32), lax.axis_index("col").astype(jnp.int32)
    low = dev < 2
    outer = (dev == 0) | (dev == 3)
    where = [dev, dev ^ 1, jnp.where(low, 2, 1), jnp.where(low, 3, 0), col, col ^ 1, col ^ 2, col ^ 3, outer]
    where = jnp.stack([x.astype(jnp.int32) for x in where])
    groups = a_count // ROWS
    halves = 2
    each = groups // halves
    tall = c_count * ROWS
    mid = c_count // 2

    def turned(h):
        x = factor_ac[:, h * each * ROWS:(h + 1) * each * ROWS].reshape(depth, each, ROWS, c_count)
        return x.transpose(1, 3, 2, 0).reshape(each * tall, depth)

    own = [turned(h) for h in range(halves)]
    turned_bd = factor_bd.transpose(1, 0, 2)
    near = [lax.ppermute(x, "dev", shuffled(n_dev, 1)) for x in own]
    far0 = [lax.ppermute(x, "dev", INNER) for x in own]
    far1 = [lax.ppermute(x, "dev", INNER) for x in near]
    end0 = [lax.ppermute(x, "dev", TO_END) for x in far0]
    across = lax.ppermute(turned_bd, "col", shuffled(n_col, 2))
    beside = lax.ppermute(turned_bd, "col", shuffled(n_col, 1))
    diagonal = lax.ppermute(across, "col", shuffled(n_col, 1))
    quarters = (turned_bd, beside, across, diagonal)

    def reduced(group, total):
        with_core = [(i, i ^ 1) for i in range(n_col) if i % 2 != group % 2]
        total = total + lax.ppermute(total, "col", with_core)
        total = total + lax.ppermute(total, "col", [(group ^ 2, group)])
        x = total.reshape(n_dev, b_count // n_dev * ROWS, pairs)
        out = lax.dynamic_index_in_dim(x, dev, 0, keepdims=False)
        for mask in range(1, n_dev):
            give = lax.dynamic_index_in_dim(x, dev ^ mask, 0, keepdims=False)
            pattern = [(i * n_col + group, (i ^ mask) * n_col + group) for i in range(n_dev)]
            out = out + lax.ppermute(give, ("dev", "col"), pattern)
        return out

    plan = [[(g, [(0, c_count)]) for g in range(each)] for _ in range(halves)]
    plan[-1][-1] = (each - 1, [(0, mid), (mid, c_count)])
    totals = []
    for h in range(halves):
        for g, spans in plan[h]:
            total = jnp.zeros((b_count * ROWS, pairs), F32)
            for c0, c1 in spans:
                start, rows = g * tall + c0 * ROWS, (c1 - c0) * ROWS
                end1 = lax.ppermute(far1[h][start:start + rows], "dev", TO_END)
                pieces = (own[h], near[h], far0[h], far1[h], end0[h], end1)
                starts = (start,) * 5 + (0,)
                total = block(c0 == 0, where, pieces, starts, rows, quarters, amplitudes, c0, total)
            totals.append(total)
    out = jnp.zeros((b_count // n_dev * ROWS, pairs), F32)
    previous = None
    for group, total in enumerate(totals):
        if previous is not None:
            total, previous = lax.optimization_barrier((total, previous))
        previous = reduced(group, total)
        out = jnp.where(col == group, previous, out)
    return out.reshape(b_count // n_dev, ROWS, pairs).transpose(1, 0, 2)


def solution(mesh):
    n_dev, n_col = mesh.shape["dev"], mesh.shape["col"]
    placed = (
        P(("frag", "dev"), None, "col"),
        P(("frag", "col"), None, "dev"),
        P(("frag", "col"), "dev", None),
    )

    def local(factor_ac, factor_bd, amplitudes):
        depth, a_count, c_count = factor_ac.shape
        _, b_count, width = factor_bd.shape
        fits = n_dev == 4 and n_col == 4 and width == 128 and depth % 128 == 0
        fits = fits and a_count == ROWS * n_col and b_count % 8 == 0 and c_count % 8 == 0
        if fits:
            return laddered(n_dev, n_col, factor_ac, factor_bd, amplitudes)
        return plain(factor_ac, factor_bd, amplitudes)

    return jax.shard_map(
        local,
        mesh=mesh,
        in_specs=placed,
        out_specs=P(("frag", "col"), "dev", None),
        check_vma=False,
    )
```

time: 488 us -> 371 us (0.76)
  the two profiles are of different devices: /device:TPU:0 before, /device:TPU:3 now
where the time goes in v1:
time: 371 us; the launch traced here: 370 us
  waiting for transfers between devices  157 us (42%)
  Pallas kernels  98.9 us (27%)
  starting transfers between devices  78.6 us (21%)
  local copies, waits for them, and re-layouts  26.1 us (7%)
  other arithmetic  9.32 us (3%)
    pallas_call x5, Pallas kernels, block(): pl.pallas_call(functools.partial(block_kernel, first, starts, rows, c_sta...  98.9 us
    ppermute x1, waiting for transfers between devices, laddered(): across = lax.ppermute(turned_bd, 'col', shuffled(n_col, 2))  58.9 us
    ppermute x2, waiting for transfers between devices, laddered(): end0 = [lax.ppermute(x, 'dev', TO_END) for x in far0]  30.1 us
    ppermute x2, waiting for transfers between devices, laddered(): near = [lax.ppermute(x, 'dev', shuffled(n_dev, 1)) for x in own]  28.9 us
    ppermute x4, starting transfers between devices, reduced(): total = total + lax.ppermute(total, 'col', [(group ^ 2, group)])  28.3 us
    ppermute x12, starting transfers between devices, reduced(): out = out + lax.ppermute(give, ('dev', 'col'), pattern)  20.1 us
    ppermute x5, waiting for transfers between devices, laddered(): end1 = lax.ppermute(far1[h][start:start + rows], 'dev', TO_END)  15.6 us
    ppermute x4, waiting for transfers between devices, reduced(): total = total + lax.ppermute(total, 'col', with_core)  13.7 us
  transfers between devices with their start and end apart: 36, of which 10 were waited for; matrix products, arithmetic and copies ran while one was open for 7% of the time, Pallas kernels for 27%

profile of v1, /device:TPU:3, one launch (start us, length us, event | category | flops | bytes accessed | tf_op | source)
XLA Modules:
  0.0 370.1 jit_solution(8456148335874906017)
XLA Ops:
  0.0 3.3 copy.12
  3.4 2.5 slice_bitcast_fusion
  5.9 3.4 copy.9
  13.6 58.9 %collective-permute-done.6.b2 = bf16[32,384,128]{2,1,0:T(8,128)(2,1)} collective-permute-done((bf16[32,384,128]{2,1,0:T(8,128)(2,1)S(1)}, bf16[32,384,128]{2,1,0:T(8,128)(2,1)}, u32[]{:S(2)}, u32[]{:S(2)}) %collective-permute-start.6) | collective-permute-done | bytes 3145760 | tf_op jit(solution)/shard_map/ppermute | solution.py:161
  75.8 3.3 copy.7
  79.1 2.7 collective-permute-start
  83.1 2.7 fusion.10
  87.7 28.9 %collective-permute-done.near = bf16[2048,384]{1,0:T(8,128)(2,1)} collective-permute-done((bf16[2048,384]{1,0:T(8,128)(2,1)}, bf16[2048,384]{1,0:T(8,128)(2,1)}, u32[]{:S(2)}, u32[]{:S(2)}) %collective-permute-start) | collective-permute-done | bytes 1572896 | tf_op jit(solution)/shard_map/ppermute | solution.py:157
  120.2 30.1 %collective-permute-done.13.end0 = bf16[2048,384]{1,0:T(8,128)(2,1)} collective-permute-done((bf16[2048,384]{1,0:T(8,128)(2,1)}, bf16[2048,384]{1,0:T(8,128)(2,1)}, u32[]{:S(2)}, u32[]{:S(2)}) %collective-permute-start.13) | collective-permute-done | bytes 1572896 | tf_op jit(solution)/shard_map/ppermute | solution.py:160
  151.6 15.6 %collective-permute-done.15.end1 = bf16[1024,384]{1,0:T(8,128)(2,1)} collective-permute-done((bf16[1024,384]{1,0:T(8,128)(2,1)}, bf16[1024,384]{1,0:T(8,128)(2,1)}, u32[]{:S(2)}, u32[]{:S(2)}) %collective-permute-start.15) | collective-permute-done | bytes 786464 | tf_op jit(solution)/shard_map/ppermute | solution.py:186
  167.9 23.5 %shard_map.41 = f32[256,256]{1,0:T(8,128)} custom-call(s32[9]{0:T(128)} %stack.43.where, bf16[2048,384]{1,0:T(8,128)(2,1)} %bitcast.96, bf16[2048,384]{1,0:T(8,128)(2,1)} %collective-permute-done.10.near, bf16[2048,384]{1,0:T(8,128)(2,1)} %collective-permute-done.11.far0, bf16[2048,384]{1,0:T(8,128)(2,1)} %collective-permute-done.12.far1, ...), custom_call_target="tpu_custom_call" | custom-call | flops 15032385536 | bytes 24117248 | tf_op jit(solution)/shard_map/pallas_call | solution.py:105
  191.4 3.2 collective-permute-start.16
  207.0 23.5 %shard_map.40 = f32[256,256]{1,0:T(8,128)} custom-call(s32[9]{0:T(128)} %stack.43.where, bf16[2048,384]{1,0:T(8,128)(2,1)} %bitcast.97, bf16[2048,384]{1,0:T(8,128)(2,1)} %collective-permute-done.10.near, bf16[2048,384]{1,0:T(8,128)(2,1)} %collective-permute-done.11.far0, bf16[2048,384]{1,0:T(8,128)(2,1)} %collective-permute-done.12.far1, ...), custom_call_target="tpu_custom_call" | custom-call | flops 15032385536 | bytes 24117248 | tf_op jit(solution)/shard_map/pallas_call | solution.py:105
  233.5 3.4 collective-permute-done.21
  237.8 25.0 %collective-permute-start.22 = (f32[256,256]{1,0:T(8,128)S(1)}, f32[256,256]{1,0:T(8,128)S(1)}, u32[]{:S(2)}, u32[]{:S(2)}) collective-permute-start(f32[256,256]{1,0:T(8,128)S(1)} %add.94), channel_id=1, source_target_pairs={{3,1},{7,5},{11,9},{15,13},{19,17},{23,21},{27,25},{31,29}} | collective-permute-start | bytes 786440 | tf_op jit(solution)/shard_map/ppermute | solution.py:169
  271.4 23.5 %shard_map.39 = f32[256,256]{1,0:T(8,128)} custom-call(s32[9]{0:T(128)} %stack.43.where, bf16[2048,384]{1,0:T(8,128)(2,1)} %bitcast.91, bf16[2048,384]{1,0:T(8,128)(2,1)} %collective-permute-done.near, bf16[2048,384]{1,0:T(8,128)(2,1)} %collective-permute-done.1.far0, bf16[2048,384]{1,0:T(8,128)(2,1)} %collective-permute-done.2.far1, ...), custom_call_target="tpu_custom_call" | custom-call | flops 15032385536 | bytes 24117248 | tf_op jit(solution)/shard_map/pallas_call | solution.py:105
  302.3 14.2 %shard_map.37.r_ref = f32[256,256]{1,0:T(8,128)} custom-call(s32[9]{0:T(128)} %stack.43.where, bf16[2048,384]{1,0:T(8,128)(2,1)} %bitcast.92, bf16[2048,384]{1,0:T(8,128)(2,1)} %collective-permute-done.near, bf16[2048,384]{1,0:T(8,128)(2,1)} %collective-permute-done.1.far0, bf16[2048,384]{1,0:T(8,128)(2,1)} %collective-permute-done.2.far1, ...), custom_call_target="tpu_custom_call" | custom-call | flops 7516192768 | bytes 18350080 | tf_op jit(solution)/shard_map/pallas_call | solution.py:105
  322.7 14.2 %shard_map.38 = f32[256,256]{1,0:T(8,128)} custom-call(s32[9]{0:T(128)} %stack.43.where, bf16[2048,384]{1,0:T(8,128)(2,1)} %bitcast.93, bf16[2048,384]{1,0:T(8,128)(2,1)} %collective-permute-done.near, bf16[2048,384]{1,0:T(8,128)(2,1)} %collective-permute-done.1.far0, bf16[2048,384]{1,0:T(8,128)(2,1)} %collective-permute-done.2.far1, ...), custom_call_target="tpu_custom_call" | custom-call | flops 7516192768 | bytes 18350080 | tf_op jit(solution)/shard_map/pallas_call | solution.py:105
  339.2 8.9 %collective-permute-done.31 = f32[256,256]{1,0:T(8,128)S(1)} collective-permute-done((f32[256,256]{1,0:T(8,128)}, f32[256,256]{1,0:T(8,128)S(1)}, u32[]{:S(2)}, u32[]{:S(2)}) %collective-permute-start.31) | collective-permute-done | bytes 262176 | tf_op jit(solution)/shard_map/ppermute | solution.py:168
  350.4 5.8 %collective-permute-done.32 = f32[256,256]{1,0:T(8,128)S(1)} collective-permute-done((f32[256,256]{1,0:T(8,128)S(1)}, f32[256,256]{1,0:T(8,128)S(1)}, u32[]{:S(2)}, u32[]{:S(2)}) %collective-permute-start.32) | collective-permute-done | bytes 262176 | tf_op jit(solution)/shard_map/ppermute | solution.py:169
  356.3 3.3 collective-permute-start.33
  359.7 2.8 collective-permute-start.34
  362.5 3.1 collective-permute-start.35
  366.0 3.4 collective-permute-done.35
  (93 shorter events, 60.5 us)
Async XLA Ops:
  3.3 69.2 %collective-permute-start.6 = (bf16[32,384,128]{2,1,0:T(8,128)(2,1)S(1)}, bf16[32,384,128]{2,1,0:T(8,128)(2,1)}, u32[]{:S(2)}, u32[]{:S(2)}) collective-permute-start(bf16[32,384,128]{2,1,0:T(8,128)(2,1)S(1)} %bitcast.82), channel_id=1, source_target_pairs={{0,2},{1,3},{2,0},{3,1},{4,6},{5,7},{6,4},{7,5},{8,10},{9,11},{10,... | collective-permute-start | bytes 9437192 | tf_op jit(solution)/shard_map/ppermute | solution.py:161
  9.3 64.7 %collective-permute-start.10 = (bf16[2048,384]{1,0:T(8,128)(2,1)}, bf16[2048,384]{1,0:T(8,128)(2,1)}, u32[]{:S(2)}, u32[]{:S(2)}) collective-permute-start(bf16[2048,384]{1,0:T(8,128)(2,1)} %bitcast.94), channel_id=1, source_target_pairs={{0,4},{4,0},{8,12},{12,8},{1,5},{5,1},{9,13},{13,9},{2,6},{6,2},{1... | collective-permute-start | bytes 4718600 | tf_op jit(solution)/shard_map/ppermute | solution.py:157
  10.6 107.8 %collective-permute-start.5 = (bf16[32,384,128]{2,1,0:T(8,128)(2,1)S(1)}, bf16[32,384,128]{2,1,0:T(8,128)(2,1)}, u32[]{:S(2)}, u32[]{:S(2)}) collective-permute-start(bf16[32,384,128]{2,1,0:T(8,128)(2,1)S(1)} %bitcast.83), channel_id=1, source_target_pairs={{0,1},{1,0},{2,3},{3,2},{4,5},{5,4},{6,7},{7,6},{8,9},{9,8},{10,11... | collective-permute-start | bytes 9437192 | tf_op jit(solution)/shard_map/ppermute | solution.py:162
  11.7 70.1 %collective-permute-start.11 = (bf16[2048,384]{1,0:T(8,128)(2,1)}, bf16[2048,384]{1,0:T(8,128)(2,1)}, u32[]{:S(2)}, u32[]{:S(2)}) collective-permute-start(bf16[2048,384]{1,0:T(8,128)(2,1)} %bitcast.95), channel_id=1, source_target_pairs={{4,8},{8,4},{5,9},{9,5},{6,10},{10,6},{7,11},{11,7},{20,24},{24,20... | collective-permute-start | bytes 4718600 | tf_op jit(solution)/shard_map/ppermute | solution.py:158
  72.4 94.7 %collective-permute-start.7 = (bf16[32,384,128]{2,1,0:T(8,128)(2,1)}, bf16[32,384,128]{2,1,0:T(8,128)(2,1)}, u32[]{:S(2)}, u32[]{:S(2)}) collective-permute-start(bf16[32,384,128]{2,1,0:T(8,128)(2,1)} %collective-permute-done.6.b2), channel_id=1, source_target_pairs={{0,1},{1,0},{2,3},{3,2},{4,5},{5,4},{6,7},{7,6},{8,9},{9,8},{10,11... | collective-permute-start | bytes 9437192 | tf_op jit(solution)/shard_map/ppermute | solution.py:163
  79.1 37.5 %collective-permute-start = (bf16[2048,384]{1,0:T(8,128)(2,1)}, bf16[2048,384]{1,0:T(8,128)(2,1)}, u32[]{:S(2)}, u32[]{:S(2)}) collective-permute-start(bf16[2048,384]{1,0:T(8,128)(2,1)} %bitcast.89), channel_id=1, source_target_pairs={{0,4},{4,0},{8,12},{12,8},{1,5},{5,1},{9,13},{13,9},{2,6},{6,2},{1... | collective-permute-start | bytes 4718600 | tf_op jit(solution)/shard_map/ppermute | solution.py:157
  81.8 68.5 %collective-permute-start.13 = (bf16[2048,384]{1,0:T(8,128)(2,1)}, bf16[2048,384]{1,0:T(8,128)(2,1)}, u32[]{:S(2)}, u32[]{:S(2)}) collective-permute-start(bf16[2048,384]{1,0:T(8,128)(2,1)} %collective-permute-done.11.far0), channel_id=1, source_target_pairs={{4,0},{8,12},{5,1},{9,13},{6,2},{10,14},{7,3},{11,15},{20,16},{24,... | collective-permute-start | bytes 4718600 | tf_op jit(solution)/shard_map/ppermute | solution.py:160
  85.8 81.4 %collective-permute-start.15 = (bf16[1024,384]{1,0:T(8,128)(2,1)}, bf16[1024,384]{1,0:T(8,128)(2,1)}, u32[]{:S(2)}, u32[]{:S(2)}) collective-permute-start(bf16[1024,384]{1,0:T(8,128)(2,1)} %get-tuple-element.13), channel_id=1, source_target_pairs={{4,0},{8,12},{5,1},{9,13},{6,2},{10,14},{7,3},{11,15},{20,16},{24,... | collective-permute-start | bytes 2359304 | tf_op jit(solution)/shard_map/ppermute | solution.py:186
  116.6 81.1 %collective-permute-start.1 = (bf16[2048,384]{1,0:T(8,128)(2,1)}, bf16[2048,384]{1,0:T(8,128)(2,1)}, u32[]{:S(2)}, u32[]{:S(2)}) collective-permute-start(bf16[2048,384]{1,0:T(8,128)(2,1)} %bitcast.90), channel_id=1, source_target_pairs={{4,8},{8,4},{5,9},{9,5},{6,10},{10,6},{7,11},{11,7},{20,24},{24,20... | collective-permute-start | bytes 4718600 | tf_op jit(solution)/shard_map/ppermute | solution.py:158
  118.4 80.6 %collective-permute-start.2 = (bf16[2048,384]{1,0:T(8,128)(2,1)}, bf16[2048,384]{1,0:T(8,128)(2,1)}, u32[]{:S(2)}, u32[]{:S(2)}) collective-permute-start(bf16[2048,384]{1,0:T(8,128)(2,1)} %collective-permute-done.near), channel_id=1, source_target_pairs={{4,8},{8,4},{5,9},{9,5},{6,10},{10,6},{7,11},{11,7},{20,24},{24,20... | collective-permute-start | bytes 4718600 | tf_op jit(solution)/shard_map/ppermute | solution.py:159
  150.3 55.5 %collective-permute-start.14 = (bf16[1024,384]{1,0:T(8,128)(2,1)}, bf16[1024,384]{1,0:T(8,128)(2,1)}, u32[]{:S(2)}, u32[]{:S(2)}) collective-permute-start(bf16[1024,384]{1,0:T(8,128)(2,1)} %get-tuple-element.14), channel_id=1, source_target_pairs={{4,0},{8,12},{5,1},{9,13},{6,2},{10,14},{7,3},{11,15},{20,16},{24,... | collective-permute-start | bytes 2359304 | tf_op jit(solution)/shard_map/ppermute | solution.py:186
  197.7 72.5 %collective-permute-start.3 = (bf16[2048,384]{1,0:T(8,128)(2,1)}, bf16[2048,384]{1,0:T(8,128)(2,1)}, u32[]{:S(2)}, u32[]{:S(2)}) collective-permute-start(bf16[2048,384]{1,0:T(8,128)(2,1)} %collective-permute-done.1.far0), channel_id=1, source_target_pairs={{4,0},{8,12},{5,1},{9,13},{6,2},{10,14},{7,3},{11,15},{20,16},{24,... | collective-permute-start | bytes 4718600 | tf_op jit(solution)/shard_map/ppermute | solution.py:160
  201.1 70.4 %collective-permute-start.9 = (bf16[1024,384]{1,0:T(8,128)(2,1)}, bf16[1024,384]{1,0:T(8,128)(2,1)}, u32[]{:S(2)}, u32[]{:S(2)}) collective-permute-start(bf16[1024,384]{1,0:T(8,128)(2,1)} %slice.30), channel_id=1, source_target_pairs={{4,0},{8,12},{5,1},{9,13},{6,2},{10,14},{7,3},{11,15},{20,16},{24,... | collective-permute-start | bytes 2359304 | tf_op jit(solution)/shard_map/ppermute | solution.py:186
  203.8 26.8 %collective-permute-start.18 = (f32[64,256]{1,0:T(8,128)}, f32[64,256]{1,0:T(8,128)S(1)}, u32[]{:S(2)}, u32[]{:S(2)}) collective-permute-start(f32[64,256]{1,0:T(8,128)} %get-tuple-element.26), channel_id=1, source_target_pairs={{0,4},{4,0},{8,12},{12,8},{16,20},{20,16},{24,28},{28,24}} | collective-permute-start | bytes 196616 | tf_op jit(solution)/shard_map/ppermute | solution.py:175
  204.5 26.1 %collective-permute-start.19 = (f32[64,256]{1,0:T(8,128)}, f32[64,256]{1,0:T(8,128)}, u32[]{:S(2)}, u32[]{:S(2)}) collective-permute-start(f32[64,256]{1,0:T(8,128)} %get-tuple-element.28), channel_id=1, source_target_pairs={{0,8},{4,12},{8,0},{12,4},{16,24},{20,28},{24,16},{28,20}} | collective-permute-start | bytes 196616 | tf_op jit(solution)/shard_map/ppermute | solution.py:175
  205.7 25.5 %collective-permute-start.20 = (f32[64,256]{1,0:T(8,128)}, f32[64,256]{1,0:T(8,128)}, u32[]{:S(2)}, u32[]{:S(2)}) collective-permute-start(f32[64,256]{1,0:T(8,128)} %get-tuple-element.27), channel_id=1, source_target_pairs={{0,12},{4,8},{8,4},{12,0},{16,28},{20,24},{24,20},{28,16}} | collective-permute-start | bytes 196616 | tf_op jit(solution)/shard_map/ppermute | solution.py:175
  237.8 28.4 %collective-permute-start.22 = (f32[256,256]{1,0:T(8,128)S(1)}, f32[256,256]{1,0:T(8,128)S(1)}, u32[]{:S(2)}, u32[]{:S(2)}) collective-permute-start(f32[256,256]{1,0:T(8,128)S(1)} %add.94), channel_id=1, source_target_pairs={{3,1},{7,5},{11,9},{15,13},{19,17},{23,21},{27,25},{31,29}} | collective-permute-start | bytes 786440 | tf_op jit(solution)/shard_map/ppermute | solution.py:169
  264.9 37.3 %collective-permute-start.8 = (bf16[512,384]{1,0:T(8,128)(2,1)}, bf16[512,384]{1,0:T(8,128)(2,1)}, u32[]{:S(2)}, u32[]{:S(2)}) collective-permute-start(bf16[512,384]{1,0:T(8,128)(2,1)} %get-tuple-element.15), channel_id=1, source_target_pairs={{4,0},{8,12},{5,1},{9,13},{6,2},{10,14},{7,3},{11,15},{20,16},{24,... | collective-permute-start | bytes 1179656 | tf_op jit(solution)/shard_map/ppermute | solution.py:186
  267.6 27.3 %collective-permute-start.23 = (f32[64,256]{1,0:T(8,128)}, f32[64,256]{1,0:T(8,128)}, u32[]{:S(2)}, u32[]{:S(2)}) collective-permute-start(f32[64,256]{1,0:T(8,128)} %get-tuple-element.23), channel_id=1, source_target_pairs={{1,5},{5,1},{9,13},{13,9},{17,21},{21,17},{25,29},{29,25}} | collective-permute-start | bytes 196616 | tf_op jit(solution)/shard_map/ppermute | solution.py:175
  268.9 26.1 %collective-permute-start.24 = (f32[64,256]{1,0:T(8,128)}, f32[64,256]{1,0:T(8,128)}, u32[]{:S(2)}, u32[]{:S(2)}) collective-permute-start(f32[64,256]{1,0:T(8,128)} %get-tuple-element.25), channel_id=1, source_target_pairs={{1,9},{5,13},{9,1},{13,5},{17,25},{21,29},{25,17},{29,21}} | collective-permute-start | bytes 196616 | tf_op jit(solution)/shard_map/ppermute | solution.py:175
  270.2 24.8 %collective-permute-start.25 = (f32[64,256]{1,0:T(8,128)}, f32[64,256]{1,0:T(8,128)}, u32[]{:S(2)}, u32[]{:S(2)}) collective-permute-start(f32[64,256]{1,0:T(8,128)} %get-tuple-element.24), channel_id=1, source_target_pairs={{1,13},{5,9},{9,5},{13,1},{17,29},{21,25},{25,21},{29,17}} | collective-permute-start | bytes 196616 | tf_op jit(solution)/shard_map/ppermute | solution.py:175
  297.9 24.8 %collective-permute-start.4 = (bf16[512,384]{1,0:T(8,128)(2,1)}, bf16[512,384]{1,0:T(8,128)(2,1)}, u32[]{:S(2)}, u32[]{:S(2)}) collective-permute-start(bf16[512,384]{1,0:T(8,128)(2,1)} %get-tuple-element.16), channel_id=1, source_target_pairs={{4,0},{8,12},{5,1},{9,13},{6,2},{10,14},{7,3},{11,15},{20,16},{24,... | collective-permute-start | bytes 1179656 | tf_op jit(solution)/shard_map/ppermute | solution.py:186
  318.9 18.0 %collective-permute-start.28 = (f32[64,256]{1,0:T(8,128)}, f32[64,256]{1,0:T(8,128)}, u32[]{:S(2)}, u32[]{:S(2)}) collective-permute-start(f32[64,256]{1,0:T(8,128)} %get-tuple-element.20), channel_id=1, source_target_pairs={{2,6},{6,2},{10,14},{14,10},{18,22},{22,18},{26,30},{30,26}} | collective-permute-start | bytes 196616 | tf_op jit(solution)/shard_map/ppermute | solution.py:175
  320.1 16.8 %collective-permute-start.29 = (f32[64,256]{1,0:T(8,128)}, f32[64,256]{1,0:T(8,128)}, u32[]{:S(2)}, u32[]{:S(2)}) collective-permute-start(f32[64,256]{1,0:T(8,128)} %get-tuple-element.22), channel_id=1, source_target_pairs={{2,10},{6,14},{10,2},{14,6},{18,26},{22,30},{26,18},{30,22}} | collective-permute-start | bytes 196616 | tf_op jit(solution)/shard_map/ppermute | solution.py:175
  (19 other events, 143.2 us)

commit v2 on v1

--- a/solution.py
+++ b/solution.py
@@ -143,58 +143,64 @@
     where = [dev, dev ^ 1, jnp.where(low, 2, 1), jnp.where(low, 3, 0), col, col ^ 1, col ^ 2, col ^ 3, outer]
     where = jnp.stack([x.astype(jnp.int32) for x in where])
     groups = a_count // ROWS
-    halves = 2
-    each = groups // halves
-    tall = c_count * ROWS
     mid = c_count // 2
-
-    def turned(h):
-        x = factor_ac[:, h * each * ROWS:(h + 1) * each * ROWS].reshape(depth, each, ROWS, c_count)
-        return x.transpose(1, 3, 2, 0).reshape(each * tall, depth)
-
-    own = [turned(h) for h in range(halves)]
+    spans = [[(0, c_count)]] * (groups - 1) + [[(0, mid), (mid, c_count)]]
+
+    def turned(g):
+        return factor_ac[:, g * ROWS:(g + 1) * ROWS].transpose(2, 1, 0).reshape(c_count * ROWS, depth)
+
+    def ends(g, x):
+        parts = [x[c0 * ROWS:c1 * ROWS] for c0, c1 in spans[g]] if len(spans[g]) > 1 else [x]
+        return [lax.ppermute(part, "dev", TO_END) for part in parts]
+
+    own = [turned(g) for g in range(groups)]
     turned_bd = factor_bd.transpose(1, 0, 2)
     near = [lax.ppermute(x, "dev", shuffled(n_dev, 1)) for x in own]
     far0 = [lax.ppermute(x, "dev", INNER) for x in own]
     far1 = [lax.ppermute(x, "dev", INNER) for x in near]
-    end0 = [lax.ppermute(x, "dev", TO_END) for x in far0]
+    end0 = [ends(g, x) for g, x in enumerate(far0)]
+    end1 = [ends(g, x) for g, x in enumerate(far1)]
     across = lax.ppermute(turned_bd, "col", shuffled(n_col, 2))
     beside = lax.ppermute(turned_bd, "col", shuffled(n_col, 1))
     diagonal = lax.ppermute(across, "col", shuffled(n_col, 1))
     quarters = (turned_bd, beside, across, diagonal)
 
-    def reduced(group, total):
-        with_core = [(i, i ^ 1) for i in range(n_col) if i % 2 != group % 2]
-        total = total + lax.ppermute(total, "col", with_core)
-        total = total + lax.ppermute(total, "col", [(group ^ 2, group)])
+    def scattered(total, columns):
         x = total.reshape(n_dev, b_count // n_dev * ROWS, pairs)
         out = lax.dynamic_index_in_dim(x, dev, 0, keepdims=False)
         for mask in range(1, n_dev):
             give = lax.dynamic_index_in_dim(x, dev ^ mask, 0, keepdims=False)
-            pattern = [(i * n_col + group, (i ^ mask) * n_col + group) for i in range(n_dev)]
+            pattern = [(i * n_col + j, (i ^ mask) * n_col + j) for i in range(n_dev) for j in columns]
             out = out + lax.ppermute(give, ("dev", "col"), pattern)
         return out
 
-    plan = [[(g, [(0, c_count)]) for g in range(each)] for _ in range(halves)]
-    plan[-1][-1] = (each - 1, [(0, mid), (mid, c_count)])
+    def reduced(group, total):
+        with_core = [(i, i ^ 1) for i in range(n_col) if i % 2 != group % 2]
+        early = total + lax.ppermute(total, "col", with_core)
+        total = early + lax.ppermute(early, "col", [(group ^ 2, group)])
+        return scattered(total, (group,)), early
+
+    def reduced_pair(even, odd):
+        core = col % 2
+        keep, give = jnp.where(core == 0, even, odd), jnp.where(core == 0, odd, even)
+        total = keep + lax.ppermute(give, "col", shuffled(n_col, 1))
+        total = total + lax.ppermute(total, "col", [(2, 0), (3, 1)])
+        return scattered(total, (0, 1))
+
     totals = []
-    for h in range(halves):
-        for g, spans in plan[h]:
-            total = jnp.zeros((b_count * ROWS, pairs), F32)
-            for c0, c1 in spans:
-                start, rows = g * tall + c0 * ROWS, (c1 - c0) * ROWS
-                end1 = lax.ppermute(far1[h][start:start + rows], "dev", TO_END)
-                pieces = (own[h], near[h], far0[h], far1[h], end0[h], end1)
-                starts = (start,) * 5 + (0,)
-                total = block(c0 == 0, where, pieces, starts, rows, quarters, amplitudes, c0, total)
-            totals.append(total)
-    out = jnp.zeros((b_count // n_dev * ROWS, pairs), F32)
-    previous = None
-    for group, total in enumerate(totals):
-        if previous is not None:
-            total, previous = lax.optimization_barrier((total, previous))
-        previous = reduced(group, total)
-        out = jnp.where(col == group, previous, out)
+    for g in range(groups):
+        total = jnp.zeros((b_count * ROWS, pairs), F32)
+        for i, (c0, c1) in enumerate(spans[g]):
+            pieces = (own[g], near[g], far0[g], far1[g], end0[g][i], end1[g][i])
+            starts = (c0 * ROWS,) * 4 + (0, 0)
+            total = block(i == 0, where, pieces, starts, (c1 - c0) * ROWS, quarters, amplitudes, c0, total)
+        totals.append(total)
+    out = reduced_pair(totals[0], totals[1])
+    total, out = lax.optimization_barrier((totals[2], out))
+    third, early = reduced(2, total)
+    total, _ = lax.optimization_barrier((totals[3], early))
+    fourth, _ = reduced(3, total)
+    out = jnp.where(col == 2, third, jnp.where(col == 3, fourth, out))
     return out.reshape(b_count // n_dev, ROWS, pairs).transpose(1, 0, 2)
 
 

time: 371 us -> 360 us (0.970)
  local copies, waits for them, and re-layouts: 26.1 us -> 19.2 us
    ppermute x27 -> x25, waiting for transfers between devices: 68.9 us -> 45.3 us  [the longest x10 29.5 us: ends(): return [lax.ppermute(part, 'dev', TO_END) for part in parts]]
    ppermute x27 -> x25, starting transfers between devices: 64.6 us -> 42.8 us  [the longest x9 14.7 us: scattered(): out = out + lax.ppermute(give, ('dev', 'col'), pattern)]
    ppermute x2 -> x4, waiting for transfers between devices: 28.9 us -> 44.8 us  [laddered(): near = [lax.ppermute(x, 'dev', shuffled(n_dev, 1)) for x in own]]
    ppermute x2 -> x4, starting transfers between devices: 3.99 us -> 18.9 us  [laddered(): near = [lax.ppermute(x, 'dev', shuffled(n_dev, 1)) for x in own]]
    ppermute x1, waiting for transfers between devices: 58.9 us -> 68.6 us  [laddered(): across = lax.ppermute(turned_bd, 'col', shuffled(n_col, 2))]
    reshape x3 -> x0, local copies, waits for them, and re-layouts: 9.21 us -> none  [turned(): factor_ac[:, h * each * ROWS:(h + 1) * each * ROWS]]
    transpose x0 -> x5, local copies, waits for them, and re-layouts: none -> 5.17 us  [turned(): factor_ac[:, g * ROWS:(g + 1) * ROWS].transpose(2, 1, 0)]
    add x11 -> x7, other arithmetic: 9.29 us -> 4.89 us  [the longest x2 2.05 us: reduced(): early = total + lax.ppermute(total, 'col', with_core)]
  transfers between devices with their start and end apart: 36 -> 40, of which waited for: 10 -> 11; matrix products, arithmetic and copies ran while one was open for 7% -> 5% of each run, Pallas kernels for 27% -> 28%
where the time goes in v2:
time: 360 us; the launch traced here: 359 us
  waiting for transfers between devices  159 us (44%)
  Pallas kernels  98.9 us (27%)
  starting transfers between devices  75.4 us (21%)
  local copies, waits for them, and re-layouts  19.2 us (5%)
  other arithmetic  5.98 us (2%)
    pallas_call x5, Pallas kernels, block(): pl.pallas_call(functools.partial(block_kernel, first, starts, rows, c_sta...  98.9 us
    ppermute x1, waiting for transfers between devices, laddered(): across = lax.ppermute(turned_bd, 'col', shuffled(n_col, 2))  68.6 us
    ppermute x4, waiting for transfers between devices, laddered(): near = [lax.ppermute(x, 'dev', shuffled(n_dev, 1)) for x in own]  44.8 us
    ppermute x10, waiting for transfers between devices, ends(): return [lax.ppermute(part, 'dev', TO_END) for part in parts]  29.5 us
    ppermute x4, starting transfers between devices, laddered(): near = [lax.ppermute(x, 'dev', shuffled(n_dev, 1)) for x in own]  18.9 us
    ppermute x9, starting transfers between devices, scattered(): out = out + lax.ppermute(give, ('dev', 'col'), pattern)  14.7 us
    ppermute x10, starting transfers between devices, ends(): return [lax.ppermute(part, 'dev', TO_END) for part in parts]  12.8 us
    ppermute x2, waiting for transfers between devices, reduced(): total = early + lax.ppermute(early, 'col', [(group ^ 2, group)])  10.5 us
  transfers between devices with their start and end apart: 40, of which 11 were waited for; matrix products, arithmetic and copies ran while one was open for 5% of the time, Pallas kernels for 28%

profile of v2, /device:TPU:3, one launch (start us, length us, event | category | flops | bytes accessed | tf_op | source)
XLA Modules:
  0.0 358.9 jit_solution(1198887410124489605)
XLA Ops:
  0.0 4.9 %copy.16 = bf16[384,32,128]{2,0,1:T(8,128)(2,1)} copy(bf16[384,32,128]{2,1,0:T(8,128)(2,1)} %param.4) | data formatting | bytes 6291456 | tf_op args[1]
  5.6 68.6 %collective-permute-done.6.b2 = bf16[32,384,128]{2,1,0:T(8,128)(2,1)} collective-permute-done((bf16[32,384,128]{2,1,0:T(8,128)(2,1)}, bf16[32,384,128]{2,1,0:T(8,128)(2,1)}, u32[]{:S(2)}, u32[]{:S(2)}) %collective-permute-start.6) | collective-permute-done | bytes 3145760 | tf_op jit(solution)/shard_map/ppermute | solution.py:163
  82.5 14.8 %collective-permute-done.near = bf16[1024,384]{1,0:T(8,128)(2,1)} collective-permute-done((bf16[1024,384]{1,0:T(8,128)(2,1)}, bf16[1024,384]{1,0:T(8,128)(2,1)}, u32[]{:S(2)}, u32[]{:S(2)}) %collective-permute-start) | collective-permute-done | bytes 786464 | tf_op jit(solution)/shard_map/ppermute | solution.py:158
  98.6 15.6 %collective-permute-done.13.near = bf16[1024,384]{1,0:T(8,128)(2,1)} collective-permute-done((bf16[1024,384]{1,0:T(8,128)(2,1)S(1)}, bf16[1024,384]{1,0:T(8,128)(2,1)}, u32[]{:S(2)}, u32[]{:S(2)}) %collective-permute-start.13) | collective-permute-done | bytes 786464 | tf_op jit(solution)/shard_map/ppermute | solution.py:158
  116.4 14.5 %collective-permute-done.8.near = bf16[1024,384]{1,0:T(8,128)(2,1)S(1)} collective-permute-done((bf16[1024,384]{1,0:T(8,128)(2,1)S(1)}, bf16[1024,384]{1,0:T(8,128)(2,1)S(1)}, u32[]{:S(2)}, u32[]{:S(2)}) %collective-permute-start.8) | collective-permute-done | bytes 786464 | tf_op jit(solution)/shard_map/ppermute | solution.py:158
  138.2 13.1 %collective-permute-done.16.end0 = bf16[1024,384]{1,0:T(8,128)(2,1)} collective-permute-done((bf16[1024,384]{1,0:T(8,128)(2,1)}, bf16[1024,384]{1,0:T(8,128)(2,1)}, u32[]{:S(2)}, u32[]{:S(2)}) %collective-permute-start.16) | collective-permute-done | bytes 786464 | tf_op jit(solution)/shard_map/ppermute | solution.py:154
  152.9 16.0 %collective-permute-start.28 = (bf16[1024,384]{1,0:T(8,128)(2,1)}, bf16[1024,384]{1,0:T(8,128)(2,1)}, u32[]{:S(2)}, u32[]{:S(2)}) collective-permute-start(bf16[1024,384]{1,0:T(8,128)(2,1)} %bitcast.27.own), channel_id=1, source_target_pairs={{0,4},{4,0},{8,12},{12,8},{1,5},{5,1},{9,13},{13,9},{2,6},{6,2},{1... | collective-permute-start | bytes 2359304 | tf_op jit(solution)/shard_map/ppermute | solution.py:158
  173.8 23.5 %shard_map.39 = f32[256,256]{1,0:T(8,128)} custom-call(s32[9]{0:T(128)} %stack.43.where, bf16[1024,384]{1,0:T(8,128)(2,1)} %bitcast.86, bf16[1024,384]{1,0:T(8,128)(2,1)} %collective-permute-done.13.near, bf16[1024,384]{1,0:T(8,128)(2,1)} %collective-permute-done.14.far0, bf16[1024,384]{1,0:T(8,128)(2,1)} %collective-permute-done.15.far1, ...), custom_call_target="tpu_custom_call" | custom-call | flops 15032385536 | bytes 24117248 | tf_op jit(solution)/shard_map/pallas_call | solution.py:105
  203.9 15.6 %collective-permute-done.12.end1 = bf16[1024,384]{1,0:T(8,128)(2,1)} collective-permute-done((bf16[1024,384]{1,0:T(8,128)(2,1)}, bf16[1024,384]{1,0:T(8,128)(2,1)}, u32[]{:S(2)}, u32[]{:S(2)}) %collective-permute-start.12) | collective-permute-done | bytes 786464 | tf_op jit(solution)/shard_map/ppermute | solution.py:154
  219.4 23.5 %shard_map.38 = f32[256,256]{1,0:T(8,128)} custom-call(s32[9]{0:T(128)} %stack.43.where, bf16[1024,384]{1,0:T(8,128)(2,1)} %bitcast.83, bf16[1024,384]{1,0:T(8,128)(2,1)} %copy-done.7, bf16[1024,384]{1,0:T(8,128)(2,1)} %copy-done.8, bf16[1024,384]{1,0:T(8,128)(2,1)} %collective-permute-done.10.far1, bf16[1024,384]{1,0:T(8,128)(2,1)} %collective-permute-done.11.end0, ...), custom_call_target="tpu_custom_call" | custom-call | flops 15032385536 | bytes 24117248 | tf_op jit(solution)/shard_map/pallas_call | solution.py:105
  244.0 6.2 %collective-permute-start.18 = (f32[256,256]{1,0:T(8,128)S(1)}, f32[256,256]{1,0:T(8,128)S(1)}, u32[]{:S(2)}, u32[]{:S(2)}) collective-permute-start(f32[256,256]{1,0:T(8,128)S(1)} %broadcast_select_fusion), channel_id=1, source_target_pairs={{0,1},{1,0},{2,3},{3,2},{4,5},{5,4},{6,7},{7,6},{8,9},{9,8},{10,11... | collective-permute-start | bytes 786440 | tf_op jit(solution)/shard_map/ppermute | solution.py:186
  250.2 2.1 fusion.10
  254.9 2.1 fusion.9
  260.3 2.9 collective-permute-start.19
  263.3 23.5 %shard_map.37 = f32[256,256]{1,0:T(8,128)} custom-call(s32[9]{0:T(128)} %stack.43.where, bf16[1024,384]{1,0:T(8,128)(2,1)} %bitcast.10.own, bf16[1024,384]{1,0:T(8,128)(2,1)} %collective-permute-done.near, bf16[1024,384]{1,0:T(8,128)(2,1)} %collective-permute-done.1.far0, bf16[1024,384]{1,0:T(8,128)(2,1)} %collective-permute-done.2.far1, ...), custom_call_target="tpu_custom_call" | custom-call | flops 15032385536 | bytes 24117248 | tf_op jit(solution)/shard_map/pallas_call | solution.py:105
  292.6 14.2 %shard_map.40.r_ref = f32[256,256]{1,0:T(8,128)} custom-call(s32[9]{0:T(128)} %stack.43.where, bf16[1024,384]{1,0:T(8,128)(2,1)} %bitcast.27.own, bf16[1024,384]{1,0:T(8,128)(2,1)} %collective-permute-done.28.near, bf16[1024,384]{1,0:T(8,128)(2,1)} %collective-permute-done.29.far0, bf16[1024,384]{1,0:T(8,128)(2,1)} %collective-permute-done.30.far1, ...), custom_call_target="tpu_custom_call" | custom-call | flops 7516192768 | bytes 18350080 | tf_op jit(solution)/shard_map/pallas_call | solution.py:105
  308.4 2.9 collective-permute-start.23
  311.3 14.2 %shard_map.41 = f32[256,256]{1,0:T(8,128)} custom-call(s32[9]{0:T(128)} %stack.43.where, bf16[1024,384]{1,0:T(8,128)(2,1)} %bitcast.27.own, bf16[1024,384]{1,0:T(8,128)(2,1)} %collective-permute-done.28.near, bf16[1024,384]{1,0:T(8,128)(2,1)} %collective-permute-done.29.far0, bf16[1024,384]{1,0:T(8,128)(2,1)} %collective-permute-done.30.far1, ...), custom_call_target="tpu_custom_call" | custom-call | flops 7516192768 | bytes 18350080 | tf_op jit(solution)/shard_map/pallas_call | solution.py:105
  328.6 1.7 collective-permute-done.35
  334.6 10.5 %collective-permute-done.36 = f32[256,256]{1,0:T(8,128)S(1)} collective-permute-done((f32[256,256]{1,0:T(8,128)S(1)}, f32[256,256]{1,0:T(8,128)S(1)}, u32[]{:S(2)}, u32[]{:S(2)}) %collective-permute-start.36) | collective-permute-done | bytes 262176 | tf_op jit(solution)/shard_map/ppermute | solution.py:180
  345.2 4.0 %collective-permute-start.39 = (f32[64,256]{1,0:T(8,128)S(1)}, f32[64,256]{1,0:T(8,128)S(1)}, u32[]{:S(2)}, u32[]{:S(2)}) collective-permute-start(f32[64,256]{1,0:T(8,128)S(1)} %get-tuple-element.23), channel_id=1, source_target_pairs={{3,15},{7,11},{11,7},{15,3},{19,31},{23,27},{27,23},{31,19}} | collective-permute-start | bytes 196616 | tf_op jit(solution)/shard_map/ppermute | solution.py:174
  349.2 2.6 collective-permute-start.38
  351.9 2.7 collective-permute-start.37
  354.6 2.2 collective-permute-done.38
  (102 shorter events, 56.5 us)
Async XLA Ops:
  4.9 69.3 %collective-permute-start.6 = (bf16[32,384,128]{2,1,0:T(8,128)(2,1)}, bf16[32,384,128]{2,1,0:T(8,128)(2,1)}, u32[]{:S(2)}, u32[]{:S(2)}) collective-permute-start(bf16[32,384,128]{2,1,0:T(8,128)(2,1)} %bitcast.74.b0), channel_id=1, source_target_pairs={{0,2},{1,3},{2,0},{3,1},{4,6},{5,7},{6,4},{7,5},{8,10},{9,11},{10,... | collective-permute-start | bytes 9437192 | tf_op jit(solution)/shard_map/ppermute | solution.py:163
  4.9 165.6 %collective-permute-start.5 = (bf16[32,384,128]{2,1,0:T(8,128)(2,1)}, bf16[32,384,128]{2,1,0:T(8,128)(2,1)}, u32[]{:S(2)}, u32[]{:S(2)}) collective-permute-start(bf16[32,384,128]{2,1,0:T(8,128)(2,1)} %bitcast.74.b0), channel_id=1, source_target_pairs={{0,1},{1,0},{2,3},{3,2},{4,5},{5,4},{6,7},{7,6},{8,9},{9,8},{10,11... | collective-permute-start | bytes 9437192 | tf_op jit(solution)/shard_map/ppermute | solution.py:164
  74.2 97.6 %collective-permute-start.7 = (bf16[32,384,128]{2,1,0:T(8,128)(2,1)}, bf16[32,384,128]{2,1,0:T(8,128)(2,1)}, u32[]{:S(2)}, u32[]{:S(2)}) collective-permute-start(bf16[32,384,128]{2,1,0:T(8,128)(2,1)} %collective-permute-done.6.b2), channel_id=1, source_target_pairs={{0,1},{1,0},{2,3},{3,2},{4,5},{5,4},{6,7},{7,6},{8,9},{9,8},{10,11... | collective-permute-start | bytes 9437192 | tf_op jit(solution)/shard_map/ppermute | solution.py:165
  79.9 34.2 %collective-permute-start.13 = (bf16[1024,384]{1,0:T(8,128)(2,1)S(1)}, bf16[1024,384]{1,0:T(8,128)(2,1)}, u32[]{:S(2)}, u32[]{:S(2)}) collective-permute-start(bf16[1024,384]{1,0:T(8,128)(2,1)S(1)} %bitcast.84), channel_id=1, source_target_pairs={{0,4},{4,0},{8,12},{12,8},{1,5},{5,1},{9,13},{13,9},{2,6},{6,2},{1... | collective-permute-start | bytes 2359304 | tf_op jit(solution)/shard_map/ppermute | solution.py:158
  80.2 34.7 %collective-permute-start.14 = (bf16[1024,384]{1,0:T(8,128)(2,1)S(1)}, bf16[1024,384]{1,0:T(8,128)(2,1)}, u32[]{:S(2)}, u32[]{:S(2)}) collective-permute-start(bf16[1024,384]{1,0:T(8,128)(2,1)S(1)} %bitcast.85), channel_id=1, source_target_pairs={{4,8},{8,4},{5,9},{9,5},{6,10},{10,6},{7,11},{11,7},{20,24},{24,20... | collective-permute-start | bytes 2359304 | tf_op jit(solution)/shard_map/ppermute | solution.py:159
  97.3 33.6 %collective-permute-start.8 = (bf16[1024,384]{1,0:T(8,128)(2,1)S(1)}, bf16[1024,384]{1,0:T(8,128)(2,1)S(1)}, u32[]{:S(2)}, u32[]{:S(2)}) collective-permute-start(bf16[1024,384]{1,0:T(8,128)(2,1)S(1)} %bitcast.81), channel_id=1, source_target_pairs={{0,4},{4,0},{8,12},{12,8},{1,5},{5,1},{9,13},{13,9},{2,6},{6,2},{1... | collective-permute-start | bytes 2359304 | tf_op jit(solution)/shard_map/ppermute | solution.py:158
  130.9 20.4 %collective-permute-start.16 = (bf16[1024,384]{1,0:T(8,128)(2,1)}, bf16[1024,384]{1,0:T(8,128)(2,1)}, u32[]{:S(2)}, u32[]{:S(2)}) collective-permute-start(bf16[1024,384]{1,0:T(8,128)(2,1)} %collective-permute-done.14.far0), channel_id=1, source_target_pairs={{4,0},{8,12},{5,1},{9,13},{6,2},{10,14},{7,3},{11,15},{20,16},{24,... | collective-permute-start | bytes 2359304 | tf_op jit(solution)/shard_map/ppermute | solution.py:154
  134.6 34.3 %collective-permute-start.17 = (bf16[1024,384]{1,0:T(8,128)(2,1)}, bf16[1024,384]{1,0:T(8,128)(2,1)}, u32[]{:S(2)}, u32[]{:S(2)}) collective-permute-start(bf16[1024,384]{1,0:T(8,128)(2,1)} %collective-permute-done.15.far1), channel_id=1, source_target_pairs={{4,0},{8,12},{5,1},{9,13},{6,2},{10,14},{7,3},{11,15},{20,16},{24,... | collective-permute-start | bytes 2359304 | tf_op jit(solution)/shard_map/ppermute | solution.py:154
  151.3 46.0 %collective-permute-start.1 = (bf16[1024,384]{1,0:T(8,128)(2,1)}, bf16[1024,384]{1,0:T(8,128)(2,1)}, u32[]{:S(2)}, u32[]{:S(2)}) collective-permute-start(bf16[1024,384]{1,0:T(8,128)(2,1)} %bitcast.10.own), channel_id=1, source_target_pairs={{4,8},{8,4},{5,9},{9,5},{6,10},{10,6},{7,11},{11,7},{20,24},{24,20... | collective-permute-start | bytes 2359304 | tf_op jit(solution)/shard_map/ppermute | solution.py:159
  152.9 46.0 %collective-permute-start.28 = (bf16[1024,384]{1,0:T(8,128)(2,1)}, bf16[1024,384]{1,0:T(8,128)(2,1)}, u32[]{:S(2)}, u32[]{:S(2)}) collective-permute-start(bf16[1024,384]{1,0:T(8,128)(2,1)} %bitcast.27.own), channel_id=1, source_target_pairs={{0,4},{4,0},{8,12},{12,8},{1,5},{5,1},{9,13},{13,9},{2,6},{6,2},{1... | collective-permute-start | bytes 2359304 | tf_op jit(solution)/shard_map/ppermute | solution.py:158
  168.9 31.3 %collective-permute-start.2 = (bf16[1024,384]{1,0:T(8,128)(2,1)}, bf16[1024,384]{1,0:T(8,128)(2,1)}, u32[]{:S(2)}, u32[]{:S(2)}) collective-permute-start(bf16[1024,384]{1,0:T(8,128)(2,1)} %collective-permute-done.near), channel_id=1, source_target_pairs={{4,8},{8,4},{5,9},{9,5},{6,10},{10,6},{7,11},{11,7},{20,24},{24,20... | collective-permute-start | bytes 2359304 | tf_op jit(solution)/shard_map/ppermute | solution.py:160
  170.5 32.1 %collective-permute-start.11 = (bf16[1024,384]{1,0:T(8,128)(2,1)}, bf16[1024,384]{1,0:T(8,128)(2,1)}, u32[]{:S(2)}, u32[]{:S(2)}) collective-permute-start(bf16[1024,384]{1,0:T(8,128)(2,1)} %copy-done.8), channel_id=1, source_target_pairs={{4,0},{8,12},{5,1},{9,13},{6,2},{10,14},{7,3},{11,15},{20,16},{24,... | collective-permute-start | bytes 2359304 | tf_op jit(solution)/shard_map/ppermute | solution.py:154
  171.8 47.6 %collective-permute-start.12 = (bf16[1024,384]{1,0:T(8,128)(2,1)}, bf16[1024,384]{1,0:T(8,128)(2,1)}, u32[]{:S(2)}, u32[]{:S(2)}) collective-permute-start(bf16[1024,384]{1,0:T(8,128)(2,1)} %collective-permute-done.10.far1), channel_id=1, source_target_pairs={{4,0},{8,12},{5,1},{9,13},{6,2},{10,14},{7,3},{11,15},{20,16},{24,... | collective-permute-start | bytes 2359304 | tf_op jit(solution)/shard_map/ppermute | solution.py:154
  197.4 52.8 %collective-permute-start.29 = (bf16[1024,384]{1,0:T(8,128)(2,1)}, bf16[1024,384]{1,0:T(8,128)(2,1)}, u32[]{:S(2)}, u32[]{:S(2)}) collective-permute-start(bf16[1024,384]{1,0:T(8,128)(2,1)} %bitcast.27.own), channel_id=1, source_target_pairs={{4,8},{8,4},{5,9},{9,5},{6,10},{10,6},{7,11},{11,7},{20,24},{24,20... | collective-permute-start | bytes 2359304 | tf_op jit(solution)/shard_map/ppermute | solution.py:159
  198.9 60.1 %collective-permute-start.3 = (bf16[1024,384]{1,0:T(8,128)(2,1)}, bf16[1024,384]{1,0:T(8,128)(2,1)}, u32[]{:S(2)}, u32[]{:S(2)}) collective-permute-start(bf16[1024,384]{1,0:T(8,128)(2,1)} %collective-permute-done.1.far0), channel_id=1, source_target_pairs={{4,0},{8,12},{5,1},{9,13},{6,2},{10,14},{7,3},{11,15},{20,16},{24,... | collective-permute-start | bytes 2359304 | tf_op jit(solution)/shard_map/ppermute | solution.py:154
  200.2 53.4 %collective-permute-start.30 = (bf16[1024,384]{1,0:T(8,128)(2,1)}, bf16[1024,384]{1,0:T(8,128)(2,1)}, u32[]{:S(2)}, u32[]{:S(2)}) collective-permute-start(bf16[1024,384]{1,0:T(8,128)(2,1)} %collective-permute-done.28.near), channel_id=1, source_target_pairs={{4,8},{8,4},{5,9},{9,5},{6,10},{10,6},{7,11},{11,7},{20,24},{24,20... | collective-permute-start | bytes 2359304 | tf_op jit(solution)/shard_map/ppermute | solution.py:160
  202.6 57.8 %collective-permute-start.4 = (bf16[1024,384]{1,0:T(8,128)(2,1)}, bf16[1024,384]{1,0:T(8,128)(2,1)}, u32[]{:S(2)}, u32[]{:S(2)}) collective-permute-start(bf16[1024,384]{1,0:T(8,128)(2,1)} %collective-permute-done.2.far1), channel_id=1, source_target_pairs={{4,0},{8,12},{5,1},{9,13},{6,2},{10,14},{7,3},{11,15},{20,16},{24,... | collective-permute-start | bytes 2359304 | tf_op jit(solution)/shard_map/ppermute | solution.py:154
  252.3 59.0 %collective-permute-start.31 = (bf16[512,384]{1,0:T(8,128)(2,1)}, bf16[512,384]{1,0:T(8,128)(2,1)}, u32[]{:S(2)}, u32[]{:S(2)}) collective-permute-start(bf16[512,384]{1,0:T(8,128)(2,1)} %get-tuple-element.18), channel_id=1, source_target_pairs={{4,0},{8,12},{5,1},{9,13},{6,2},{10,14},{7,3},{11,15},{20,16},{24,... | collective-permute-start | bytes 1179656 | tf_op jit(solution)/shard_map/ppermute | solution.py:154
  253.6 36.3 %collective-permute-start.33 = (bf16[512,384]{1,0:T(8,128)(2,1)}, bf16[512,384]{1,0:T(8,128)(2,1)}, u32[]{:S(2)}, u32[]{:S(2)}) collective-permute-start(bf16[512,384]{1,0:T(8,128)(2,1)} %get-tuple-element.17), channel_id=1, source_target_pairs={{4,0},{8,12},{5,1},{9,13},{6,2},{10,14},{7,3},{11,15},{20,16},{24,... | collective-permute-start | bytes 1179656 | tf_op jit(solution)/shard_map/ppermute | solution.py:154
  257.0 54.4 %collective-permute-start.32 = (bf16[512,384]{1,0:T(8,128)(2,1)}, bf16[512,384]{1,0:T(8,128)(2,1)}, u32[]{:S(2)}, u32[]{:S(2)}) collective-permute-start(bf16[512,384]{1,0:T(8,128)(2,1)} %get-tuple-element.16), channel_id=1, source_target_pairs={{4,0},{8,12},{5,1},{9,13},{6,2},{10,14},{7,3},{11,15},{20,16},{24,... | collective-permute-start | bytes 1179656 | tf_op jit(solution)/shard_map/ppermute | solution.py:154
  259.0 32.1 %collective-permute-start.34 = (bf16[512,384]{1,0:T(8,128)(2,1)}, bf16[512,384]{1,0:T(8,128)(2,1)}, u32[]{:S(2)}, u32[]{:S(2)}) collective-permute-start(bf16[512,384]{1,0:T(8,128)(2,1)} %get-tuple-element.15), channel_id=1, source_target_pairs={{4,0},{8,12},{5,1},{9,13},{6,2},{10,14},{7,3},{11,15},{20,16},{24,... | collective-permute-start | bytes 1179656 | tf_op jit(solution)/shard_map/ppermute | solution.py:154
  260.3 26.4 %collective-permute-start.19 = (f32[256,256]{1,0:T(8,128)}, f32[256,256]{1,0:T(8,128)}, u32[]{:S(2)}, u32[]{:S(2)}) collective-permute-start(f32[256,256]{1,0:T(8,128)} %select_add_fusion), channel_id=1, source_target_pairs={{2,0},{3,1},{6,4},{7,5},{10,8},{11,9},{14,12},{15,13},{18,16},{19,... | collective-permute-start | bytes 786440 | tf_op jit(solution)/shard_map/ppermute | solution.py:187
  333.3 21.3 %collective-permute-start.26 = (f32[64,256]{1,0:T(8,128)S(1)}, f32[64,256]{1,0:T(8,128)S(1)}, u32[]{:S(2)}, u32[]{:S(2)}) collective-permute-start(f32[64,256]{1,0:T(8,128)S(1)} %get-tuple-element.21), channel_id=1, source_target_pairs={{2,10},{6,14},{10,2},{14,6},{18,26},{22,30},{26,18},{30,22}} | collective-permute-start | bytes 196616 | tf_op jit(solution)/shard_map/ppermute | solution.py:174
  333.9 20.6 %collective-permute-start.25 = (f32[64,256]{1,0:T(8,128)S(1)}, f32[64,256]{1,0:T(8,128)S(1)}, u32[]{:S(2)}, u32[]{:S(2)}) collective-permute-start(f32[64,256]{1,0:T(8,128)S(1)} %get-tuple-element.19), channel_id=1, source_target_pairs={{2,6},{6,2},{10,14},{14,10},{18,22},{22,18},{26,30},{30,26}} | collective-permute-start | bytes 196616 | tf_op jit(solution)/shard_map/ppermute | solution.py:174
  (25 other events, 450.4 us)

commit v3 on v2

--- a/solution.py
+++ b/solution.py
@@ -79,17 +79,13 @@
 
     lax.fori_loop(0, steps, contract, 0)
     t_copy.wait()
-    group = 4
-    out_ref[...] = jnp.zeros(out_ref.shape, F32) if first else r_ref[...]
-
-    def absorb(g, carry):
-        c = g * group
+    group = 8
+    total = jnp.zeros(out_ref.shape, F32) if first else r_ref[...]
+    for c in range(0, count, group):
         left = jnp.concatenate([i_v[c + m] for m in range(group)], axis=1)
-        amp = t_v[pl.ds(c, group)].reshape(group * width, t_v.shape[2])
-        out_ref[...] += jnp.dot(left, amp, preferred_element_type=F32)
-        return carry
-
-    lax.fori_loop(0, count // group, absorb, 0, unroll=2)
+        amp = t_v[c:c + group].reshape(group * width, t_v.shape[2])
+        total += jnp.dot(left, amp, preferred_element_type=F32)
+    out_ref[...] = total
 
 
 def block(first, where, pieces, starts, rows, quarters, amplitudes, c_start, total):
@@ -158,49 +154,45 @@
     near = [lax.ppermute(x, "dev", shuffled(n_dev, 1)) for x in own]
     far0 = [lax.ppermute(x, "dev", INNER) for x in own]
     far1 = [lax.ppermute(x, "dev", INNER) for x in near]
-    end0 = [ends(g, x) for g, x in enumerate(far0)]
-    end1 = [ends(g, x) for g, x in enumerate(far1)]
     across = lax.ppermute(turned_bd, "col", shuffled(n_col, 2))
     beside = lax.ppermute(turned_bd, "col", shuffled(n_col, 1))
     diagonal = lax.ppermute(across, "col", shuffled(n_col, 1))
     quarters = (turned_bd, beside, across, diagonal)
 
-    def scattered(total, columns):
-        x = total.reshape(n_dev, b_count // n_dev * ROWS, pairs)
-        out = lax.dynamic_index_in_dim(x, dev, 0, keepdims=False)
-        for mask in range(1, n_dev):
-            give = lax.dynamic_index_in_dim(x, dev ^ mask, 0, keepdims=False)
-            pattern = [(i * n_col + j, (i ^ mask) * n_col + j) for i in range(n_dev) for j in columns]
-            out = out + lax.ppermute(give, ("dev", "col"), pattern)
-        return out
-
-    def reduced(group, total):
+    def to_owner(group, total):
         with_core = [(i, i ^ 1) for i in range(n_col) if i % 2 != group % 2]
         early = total + lax.ppermute(total, "col", with_core)
-        total = early + lax.ppermute(early, "col", [(group ^ 2, group)])
-        return scattered(total, (group,)), early
-
-    def reduced_pair(even, odd):
+        return early + lax.ppermute(early, "col", [(group ^ 2, group)]), early
+
+    def to_owners(even, odd):
         core = col % 2
         keep, give = jnp.where(core == 0, even, odd), jnp.where(core == 0, odd, even)
-        total = keep + lax.ppermute(give, "col", shuffled(n_col, 1))
-        total = total + lax.ppermute(total, "col", [(2, 0), (3, 1)])
-        return scattered(total, (0, 1))
+        early = keep + lax.ppermute(give, "col", shuffled(n_col, 1))
+        return early + lax.ppermute(early, "col", [(2, 0), (3, 1)]), early
 
     totals = []
     for g in range(groups):
         total = jnp.zeros((b_count * ROWS, pairs), F32)
+        third, fourth = far0[g], far1[g]
+        if len(spans[g]) > 1:
+            third, fourth, totals[1] = lax.optimization_barrier((third, fourth, totals[1]))
+        end0, end1 = ends(g, third), ends(g, fourth)
         for i, (c0, c1) in enumerate(spans[g]):
-            pieces = (own[g], near[g], far0[g], far1[g], end0[g][i], end1[g][i])
+            pieces = (own[g], near[g], third, fourth, end0[i], end1[i])
             starts = (c0 * ROWS,) * 4 + (0, 0)
             total = block(i == 0, where, pieces, starts, (c1 - c0) * ROWS, quarters, amplitudes, c0, total)
         totals.append(total)
-    out = reduced_pair(totals[0], totals[1])
-    total, out = lax.optimization_barrier((totals[2], out))
-    third, early = reduced(2, total)
+    both, early = to_owners(totals[0], totals[1])
+    total, _ = lax.optimization_barrier((totals[2], early))
+    third, early = to_owner(2, total)
     total, _ = lax.optimization_barrier((totals[3], early))
-    fourth, _ = reduced(3, total)
-    out = jnp.where(col == 2, third, jnp.where(col == 3, fourth, out))
+    fourth, _ = to_owner(3, total)
+    mine = jnp.where(col == 3, fourth, jnp.where(col == 2, third, both))
+    mine = mine.reshape(n_dev, b_count // n_dev * ROWS, pairs)
+    out = lax.dynamic_index_in_dim(mine, dev, 0, keepdims=False)
+    for mask in range(1, n_dev):
+        give = lax.dynamic_index_in_dim(mine, dev ^ mask, 0, keepdims=False)
+        out = out + lax.ppermute(give, "dev", shuffled(n_dev, mask))
     return out.reshape(b_count // n_dev, ROWS, pairs).transpose(1, 0, 2)
 
 

time: 360 us -> 325 us (0.903)
  the two profiles are of different devices: /device:TPU:3 before, /device:TPU:0 now
where the time goes in v3:
time: 325 us; the launch traced here: 324 us
  waiting for transfers between devices  157 us (48%)
  Pallas kernels  88.8 us (27%)
  starting transfers between devices  53.7 us (17%)
  local copies, waits for them, and re-layouts  17.2 us (5%)
  other arithmetic  6.6 us (2%)
    pallas_call x5, Pallas kernels, block(): pl.pallas_call(functools.partial(block_kernel, first, starts, rows, c_sta...  88.8 us
    ppermute x1, waiting for transfers between devices, laddered(): across = lax.ppermute(turned_bd, 'col', shuffled(n_col, 2))  63.2 us
    ppermute x10, waiting for transfers between devices, ends(): return [lax.ppermute(part, 'dev', TO_END) for part in parts]  44.3 us
    ppermute x4, waiting for transfers between devices, laddered(): near = [lax.ppermute(x, 'dev', shuffled(n_dev, 1)) for x in own]  39.5 us
    ppermute x10, starting transfers between devices, ends(): return [lax.ppermute(part, 'dev', TO_END) for part in parts]  13 us
    ppermute x4, starting transfers between devices, laddered(): near = [lax.ppermute(x, 'dev', shuffled(n_dev, 1)) for x in own]  9.71 us
  transfers between devices with their start and end apart: 34, of which 11 were waited for; matrix products, arithmetic and copies ran while one was open for 5% of the time, Pallas kernels for 27%

profile of v3, /device:TPU:0, one launch (start us, length us, event | category | flops | bytes accessed | tf_op | source)
XLA Modules:
  0.0 324.1 jit_solution(14773287840981292894)
XLA Ops:
  0.0 4.9 %copy.16 = bf16[384,32,128]{2,0,1:T(8,128)(2,1)} copy(bf16[384,32,128]{2,1,0:T(8,128)(2,1)} %param.4) | data formatting | bytes 6291456 | tf_op args[1]
  4.9 3.0 collective-permute-start.9
  13.1 63.2 %collective-permute-done.9.b2 = bf16[32,384,128]{2,1,0:T(8,128)(2,1)} collective-permute-done((bf16[32,384,128]{2,1,0:T(8,128)(2,1)}, bf16[32,384,128]{2,1,0:T(8,128)(2,1)}, u32[]{:S(2)}, u32[]{:S(2)}) %collective-permute-start.9) | collective-permute-done | bytes 3145760 | tf_op jit(solution)/shard_map/ppermute | solution.py:157
  81.2 4.4 %collective-permute-start.15 = (bf16[1024,384]{1,0:T(8,128)(2,1)}, bf16[1024,384]{1,0:T(8,128)(2,1)}, u32[]{:S(2)}, u32[]{:S(2)}) collective-permute-start(bf16[1024,384]{1,0:T(8,128)(2,1)} %bitcast.15.own), channel_id=1, source_target_pairs={{0,4},{4,0},{8,12},{12,8},{1,5},{5,1},{9,13},{13,9},{2,6},{6,2},{1... | collective-permute-start | bytes 2359304 | tf_op jit(solution)/shard_map/ppermute | solution.py:154
  86.4 11.2 %collective-permute-done.near = bf16[1024,384]{1,0:T(8,128)(2,1)} collective-permute-done((bf16[1024,384]{1,0:T(8,128)(2,1)S(1)}, bf16[1024,384]{1,0:T(8,128)(2,1)}, u32[]{:S(2)}, u32[]{:S(2)}) %collective-permute-start) | collective-permute-done | bytes 786464 | tf_op jit(solution)/shard_map/ppermute | solution.py:154
  101.9 12.6 %collective-permute-done.15.near = bf16[1024,384]{1,0:T(8,128)(2,1)} collective-permute-done((bf16[1024,384]{1,0:T(8,128)(2,1)}, bf16[1024,384]{1,0:T(8,128)(2,1)}, u32[]{:S(2)}, u32[]{:S(2)}) %collective-permute-start.15) | collective-permute-done | bytes 786464 | tf_op jit(solution)/shard_map/ppermute | solution.py:154
  115.2 15.7 %collective-permute-done.20.near = bf16[1024,384]{1,0:T(8,128)(2,1)S(1)} collective-permute-done((bf16[1024,384]{1,0:T(8,128)(2,1)S(1)}, bf16[1024,384]{1,0:T(8,128)(2,1)S(1)}, u32[]{:S(2)}, u32[]{:S(2)}) %collective-permute-start.20) | collective-permute-done | bytes 786464 | tf_op jit(solution)/shard_map/ppermute | solution.py:154
  135.7 17.7 %collective-permute-done.6.end0 = bf16[1024,384]{1,0:T(8,128)(2,1)S(1)} collective-permute-done((bf16[1024,384]{1,0:T(8,128)(2,1)}, bf16[1024,384]{1,0:T(8,128)(2,1)S(1)}, u32[]{:S(2)}, u32[]{:S(2)}) %collective-permute-start.6) | collective-permute-done | bytes 786464 | tf_op jit(solution)/shard_map/ppermute | solution.py:150
  156.5 12.5 %collective-permute-done.7.end1 = bf16[1024,384]{1,0:T(8,128)(2,1)S(1)} collective-permute-done((bf16[1024,384]{1,0:T(8,128)(2,1)S(1)}, bf16[1024,384]{1,0:T(8,128)(2,1)S(1)}, u32[]{:S(2)}, u32[]{:S(2)}) %collective-permute-start.7) | collective-permute-done | bytes 786464 | tf_op jit(solution)/shard_map/ppermute | solution.py:150
  173.9 20.9 %shard_map.37 = f32[256,256]{1,0:T(8,128)} custom-call(s32[9]{0:T(128)} %stack.43.where, bf16[1024,384]{1,0:T(8,128)(2,1)} %bitcast.54, bf16[1024,384]{1,0:T(8,128)(2,1)} %collective-permute-done.3.near, bf16[1024,384]{1,0:T(8,128)(2,1)} %collective-permute-done.4.far0, bf16[1024,384]{1,0:T(8,128)(2,1)} %copy-done.5, bf16[1024,384]{1,0:T(8,128)(2,1)} %copy-done.6, ...), custom_call_target="tpu_custom_call" | custom-call | flops 15032385536 | bytes 24117248 | tf_op jit(solution)/shard_map/pallas_call | solution.py:101
  197.5 2.1 fusion.4
  200.9 2.1 fusion.3
  204.2 5.9 %collective-permute-done.24.end1 = bf16[1024,384]{1,0:T(8,128)(2,1)} collective-permute-done((bf16[1024,384]{1,0:T(8,128)(2,1)}, bf16[1024,384]{1,0:T(8,128)(2,1)}, u32[]{:S(2)}, u32[]{:S(2)}) %collective-permute-start.24) | collective-permute-done | bytes 786464 | tf_op jit(solution)/shard_map/ppermute | solution.py:150
  211.6 21.0 %shard_map.41 = f32[256,256]{1,0:T(8,128)} custom-call(s32[9]{0:T(128)} %stack.43.where, bf16[1024,384]{1,0:T(8,128)(2,1)} %bitcast.51, bf16[1024,384]{1,0:T(8,128)(2,1)} %copy-done.4, bf16[1024,384]{1,0:T(8,128)(2,1)} %collective-permute-done.21.far0, bf16[1024,384]{1,0:T(8,128)(2,1)} %collective-permute-done.22.far1, ...), custom_call_target="tpu_custom_call" | custom-call | flops 15032385536 | bytes 24117248 | tf_op jit(solution)/shard_map/pallas_call | solution.py:101
  235.5 8.3 %collective-permute-done.19.end1 = bf16[1024,384]{1,0:T(8,128)(2,1)} collective-permute-done((bf16[1024,384]{1,0:T(8,128)(2,1)}, bf16[1024,384]{1,0:T(8,128)(2,1)}, u32[]{:S(2)}, u32[]{:S(2)}) %collective-permute-start.19) | collective-permute-done | bytes 786464 | tf_op jit(solution)/shard_map/ppermute | solution.py:150
  243.8 21.0 %shard_map.40 = f32[256,256]{1,0:T(8,128)} custom-call(s32[9]{0:T(128)} %stack.43.where, bf16[1024,384]{1,0:T(8,128)(2,1)} %bitcast.15.own, bf16[1024,384]{1,0:T(8,128)(2,1)} %collective-permute-done.15.near, bf16[1024,384]{1,0:T(8,128)(2,1)} %collective-permute-done.16.far0, bf16[1024,384]{1,0:T(8,128)(2,1)} %collective-permute-done.17.far1, ...), custom_call_target="tpu_custom_call" | custom-call | flops 15032385536 | bytes 24117248 | tf_op jit(solution)/shard_map/pallas_call | solution.py:101
  267.9 13.0 %shard_map.38.r_ref = f32[256,256]{1,0:T(8,128)} custom-call(s32[9]{0:T(128)} %stack.43.where, bf16[1024,384]{1,0:T(8,128)(2,1)} %bitcast.47, bf16[1024,384]{1,0:T(8,128)(2,1)} %collective-permute-done.near, bf16[1024,384]{1,0:T(8,128)(2,1)} %copy-done.2, bf16[1024,384]{1,0:T(8,128)(2,1)} %collective-permute-done.2.far1, ...), custom_call_target="tpu_custom_call" | custom-call | flops 7516192768 | bytes 18350080 | tf_op jit(solution)/shard_map/pallas_call | solution.py:101
  280.9 13.0 %shard_map.39 = f32[256,256]{1,0:T(8,128)} custom-call(s32[9]{0:T(128)} %stack.43.where, bf16[1024,384]{1,0:T(8,128)(2,1)} %bitcast.48, bf16[1024,384]{1,0:T(8,128)(2,1)} %collective-permute-done.near, bf16[1024,384]{1,0:T(8,128)(2,1)} %copy-done.2, bf16[1024,384]{1,0:T(8,128)(2,1)} %collective-permute-done.2.far1, ...), custom_call_target="tpu_custom_call" | custom-call | flops 7516192768 | bytes 18350080 | tf_op jit(solution)/shard_map/pallas_call | solution.py:101
  294.9 3.7 %collective-permute-start.27 = (f32[256,256]{1,0:T(8,128)}, f32[256,256]{1,0:T(8,128)S(1)}, u32[]{:S(2)}, u32[]{:S(2)}) collective-permute-start(f32[256,256]{1,0:T(8,128)} %shard_map.39), channel_id=1, source_target_pairs={{0,1},{2,3},{4,5},{6,7},{8,9},{10,11},{12,13},{14,15},{16,17},{18,... | collective-permute-start | bytes 786440 | tf_op jit(solution)/shard_map/ppermute | solution.py:164
  300.0 4.6 %collective-permute-start.29 = (f32[256,256]{1,0:T(8,128)S(1)}, f32[256,256]{1,0:T(8,128)S(1)}, u32[]{:S(2)}, u32[]{:S(2)}) collective-permute-start(f32[256,256]{1,0:T(8,128)S(1)} %add.46), channel_id=1, source_target_pairs={{0,2},{4,6},{8,10},{12,14},{16,18},{20,22},{24,26},{28,30}} | collective-permute-start | bytes 786440 | tf_op jit(solution)/shard_map/ppermute | solution.py:165
  306.3 2.1 collective-permute-done.30
  308.4 2.7 collective-permute-done.29
  312.1 3.3 %collective-permute-start.31 = (f32[64,256]{1,0:T(8,128)S(1)}, f32[64,256]{1,0:T(8,128)S(1)}, u32[]{:S(2)}, u32[]{:S(2)}) collective-permute-start(f32[64,256]{1,0:T(8,128)S(1)} %get-tuple-element.23), channel_id=1, source_target_pairs={{0,4},{4,0},{8,12},{12,8},{1,5},{5,1},{9,13},{13,9},{2,6},{6,2},{1... | collective-permute-start | bytes 196616 | tf_op jit(solution)/shard_map/ppermute | solution.py:195
  317.9 5.6 %collective-permute-done.32 = f32[64,256]{1,0:T(8,128)S(1)} collective-permute-done((f32[64,256]{1,0:T(8,128)S(1)}, f32[64,256]{1,0:T(8,128)S(1)}, u32[]{:S(2)}, u32[]{:S(2)}) %collective-permute-start.32) | collective-permute-done | bytes 65568 | tf_op jit(solution)/shard_map/ppermute | solution.py:195
  (83 shorter events, 49.5 us)
Async XLA Ops:
  4.9 71.4 %collective-permute-start.9 = (bf16[32,384,128]{2,1,0:T(8,128)(2,1)}, bf16[32,384,128]{2,1,0:T(8,128)(2,1)}, u32[]{:S(2)}, u32[]{:S(2)}) collective-permute-start(bf16[32,384,128]{2,1,0:T(8,128)(2,1)} %bitcast.42.b0), channel_id=1, source_target_pairs={{0,2},{1,3},{2,0},{3,1},{4,6},{5,7},{6,4},{7,5},{8,10},{9,11},{10,... | collective-permute-start | bytes 9437192 | tf_op jit(solution)/shard_map/ppermute | solution.py:157
  10.0 70.5 %collective-permute-start.3 = (bf16[1024,384]{1,0:T(8,128)(2,1)}, bf16[1024,384]{1,0:T(8,128)(2,1)}, u32[]{:S(2)}, u32[]{:S(2)}) collective-permute-start(bf16[1024,384]{1,0:T(8,128)(2,1)} %bitcast.52), channel_id=1, source_target_pairs={{0,4},{4,0},{8,12},{12,8},{1,5},{5,1},{9,13},{13,9},{2,6},{6,2},{1... | collective-permute-start | bytes 2359304 | tf_op jit(solution)/shard_map/ppermute | solution.py:154
  11.6 69.7 %collective-permute-start.4 = (bf16[1024,384]{1,0:T(8,128)(2,1)}, bf16[1024,384]{1,0:T(8,128)(2,1)}, u32[]{:S(2)}, u32[]{:S(2)}) collective-permute-start(bf16[1024,384]{1,0:T(8,128)(2,1)} %bitcast.53), channel_id=1, source_target_pairs={{4,8},{8,4},{5,9},{9,5},{6,10},{10,6},{7,11},{11,7},{20,24},{24,20... | collective-permute-start | bytes 2359304 | tf_op jit(solution)/shard_map/ppermute | solution.py:155
  13.1 157.4 %collective-permute-start.8 = (bf16[32,384,128]{2,1,0:T(8,128)(2,1)}, bf16[32,384,128]{2,1,0:T(8,128)(2,1)}, u32[]{:S(2)}, u32[]{:S(2)}) collective-permute-start(bf16[32,384,128]{2,1,0:T(8,128)(2,1)} %bitcast.42.b0), channel_id=1, source_target_pairs={{0,1},{1,0},{2,3},{3,2},{4,5},{5,4},{6,7},{7,6},{8,9},{9,8},{10,11... | collective-permute-start | bytes 9437192 | tf_op jit(solution)/shard_map/ppermute | solution.py:158
  76.3 95.6 %collective-permute-start.10 = (bf16[32,384,128]{2,1,0:T(8,128)(2,1)}, bf16[32,384,128]{2,1,0:T(8,128)(2,1)}, u32[]{:S(2)}, u32[]{:S(2)}) collective-permute-start(bf16[32,384,128]{2,1,0:T(8,128)(2,1)} %collective-permute-done.9.b2), channel_id=1, source_target_pairs={{0,1},{1,0},{2,3},{3,2},{4,5},{5,4},{6,7},{7,6},{8,9},{9,8},{10,11... | collective-permute-start | bytes 9437192 | tf_op jit(solution)/shard_map/ppermute | solution.py:159
  81.2 33.2 %collective-permute-start.15 = (bf16[1024,384]{1,0:T(8,128)(2,1)}, bf16[1024,384]{1,0:T(8,128)(2,1)}, u32[]{:S(2)}, u32[]{:S(2)}) collective-permute-start(bf16[1024,384]{1,0:T(8,128)(2,1)} %bitcast.15.own), channel_id=1, source_target_pairs={{0,4},{4,0},{8,12},{12,8},{1,5},{5,1},{9,13},{13,9},{2,6},{6,2},{1... | collective-permute-start | bytes 2359304 | tf_op jit(solution)/shard_map/ppermute | solution.py:154
  97.6 33.2 %collective-permute-start.20 = (bf16[1024,384]{1,0:T(8,128)(2,1)S(1)}, bf16[1024,384]{1,0:T(8,128)(2,1)S(1)}, u32[]{:S(2)}, u32[]{:S(2)}) collective-permute-start(bf16[1024,384]{1,0:T(8,128)(2,1)S(1)} %bitcast.49), channel_id=1, source_target_pairs={{0,4},{4,0},{8,12},{12,8},{1,5},{5,1},{9,13},{13,9},{2,6},{6,2},{1... | collective-permute-start | bytes 2359304 | tf_op jit(solution)/shard_map/ppermute | solution.py:154
  100.4 31.8 %collective-permute-start.21 = (bf16[1024,384]{1,0:T(8,128)(2,1)S(1)}, bf16[1024,384]{1,0:T(8,128)(2,1)}, u32[]{:S(2)}, u32[]{:S(2)}) collective-permute-start(bf16[1024,384]{1,0:T(8,128)(2,1)S(1)} %bitcast.50), channel_id=1, source_target_pairs={{4,8},{8,4},{5,9},{9,5},{6,10},{10,6},{7,11},{11,7},{20,24},{24,20... | collective-permute-start | bytes 2359304 | tf_op jit(solution)/shard_map/ppermute | solution.py:155
  130.9 22.5 %collective-permute-start.6 = (bf16[1024,384]{1,0:T(8,128)(2,1)}, bf16[1024,384]{1,0:T(8,128)(2,1)S(1)}, u32[]{:S(2)}, u32[]{:S(2)}) collective-permute-start(bf16[1024,384]{1,0:T(8,128)(2,1)} %collective-permute-done.4.far0), channel_id=1, source_target_pairs={{4,0},{8,12},{5,1},{9,13},{6,2},{10,14},{7,3},{11,15},{20,16},{24,... | collective-permute-start | bytes 2359304 | tf_op jit(solution)/shard_map/ppermute | solution.py:150
  132.2 22.7 %collective-permute-start.22 = (bf16[1024,384]{1,0:T(8,128)(2,1)S(1)}, bf16[1024,384]{1,0:T(8,128)(2,1)}, u32[]{:S(2)}, u32[]{:S(2)}) collective-permute-start(bf16[1024,384]{1,0:T(8,128)(2,1)S(1)} %collective-permute-done.20.near), channel_id=1, source_target_pairs={{4,8},{8,4},{5,9},{9,5},{6,10},{10,6},{7,11},{11,7},{20,24},{24,20... | collective-permute-start | bytes 2359304 | tf_op jit(solution)/shard_map/ppermute | solution.py:156
  133.7 35.2 %collective-permute-start.7 = (bf16[1024,384]{1,0:T(8,128)(2,1)S(1)}, bf16[1024,384]{1,0:T(8,128)(2,1)S(1)}, u32[]{:S(2)}, u32[]{:S(2)}) collective-permute-start(bf16[1024,384]{1,0:T(8,128)(2,1)S(1)} %collective-permute-done.5.far1), channel_id=1, source_target_pairs={{4,0},{8,12},{5,1},{9,13},{6,2},{10,14},{7,3},{11,15},{20,16},{24,... | collective-permute-start | bytes 2359304 | tf_op jit(solution)/shard_map/ppermute | solution.py:150
  153.4 41.5 %collective-permute-start.16 = (bf16[1024,384]{1,0:T(8,128)(2,1)}, bf16[1024,384]{1,0:T(8,128)(2,1)}, u32[]{:S(2)}, u32[]{:S(2)}) collective-permute-start(bf16[1024,384]{1,0:T(8,128)(2,1)} %bitcast.15.own), channel_id=1, source_target_pairs={{4,8},{8,4},{5,9},{9,5},{6,10},{10,6},{7,11},{11,7},{20,24},{24,20... | collective-permute-start | bytes 2359304 | tf_op jit(solution)/shard_map/ppermute | solution.py:155
  154.9 42.5 %collective-permute-start.2 = (bf16[1024,384]{1,0:T(8,128)(2,1)}, bf16[1024,384]{1,0:T(8,128)(2,1)}, u32[]{:S(2)}, u32[]{:S(2)}) collective-permute-start(bf16[1024,384]{1,0:T(8,128)(2,1)} %collective-permute-done.near), channel_id=1, source_target_pairs={{4,8},{8,4},{5,9},{9,5},{6,10},{10,6},{7,11},{11,7},{20,24},{24,20... | collective-permute-start | bytes 2359304 | tf_op jit(solution)/shard_map/ppermute | solution.py:156
  169.0 27.2 %collective-permute-start.17 = (bf16[1024,384]{1,0:T(8,128)(2,1)}, bf16[1024,384]{1,0:T(8,128)(2,1)}, u32[]{:S(2)}, u32[]{:S(2)}) collective-permute-start(bf16[1024,384]{1,0:T(8,128)(2,1)} %collective-permute-done.15.near), channel_id=1, source_target_pairs={{4,8},{8,4},{5,9},{9,5},{6,10},{10,6},{7,11},{11,7},{20,24},{24,20... | collective-permute-start | bytes 2359304 | tf_op jit(solution)/shard_map/ppermute | solution.py:156
  170.6 32.4 %collective-permute-start.23 = (bf16[1024,384]{1,0:T(8,128)(2,1)}, bf16[1024,384]{1,0:T(8,128)(2,1)}, u32[]{:S(2)}, u32[]{:S(2)}) collective-permute-start(bf16[1024,384]{1,0:T(8,128)(2,1)} %collective-permute-done.21.far0), channel_id=1, source_target_pairs={{4,0},{8,12},{5,1},{9,13},{6,2},{10,14},{7,3},{11,15},{20,16},{24,... | collective-permute-start | bytes 2359304 | tf_op jit(solution)/shard_map/ppermute | solution.py:150
  171.8 38.2 %collective-permute-start.24 = (bf16[1024,384]{1,0:T(8,128)(2,1)}, bf16[1024,384]{1,0:T(8,128)(2,1)}, u32[]{:S(2)}, u32[]{:S(2)}) collective-permute-start(bf16[1024,384]{1,0:T(8,128)(2,1)} %collective-permute-done.22.far1), channel_id=1, source_target_pairs={{4,0},{8,12},{5,1},{9,13},{6,2},{10,14},{7,3},{11,15},{20,16},{24,... | collective-permute-start | bytes 2359304 | tf_op jit(solution)/shard_map/ppermute | solution.py:150
  194.8 39.4 %collective-permute-start.18 = (bf16[1024,384]{1,0:T(8,128)(2,1)}, bf16[1024,384]{1,0:T(8,128)(2,1)}, u32[]{:S(2)}, u32[]{:S(2)}) collective-permute-start(bf16[1024,384]{1,0:T(8,128)(2,1)} %collective-permute-done.16.far0), channel_id=1, source_target_pairs={{4,0},{8,12},{5,1},{9,13},{6,2},{10,14},{7,3},{11,15},{20,16},{24,... | collective-permute-start | bytes 2359304 | tf_op jit(solution)/shard_map/ppermute | solution.py:150
  196.2 47.6 %collective-permute-start.19 = (bf16[1024,384]{1,0:T(8,128)(2,1)}, bf16[1024,384]{1,0:T(8,128)(2,1)}, u32[]{:S(2)}, u32[]{:S(2)}) collective-permute-start(bf16[1024,384]{1,0:T(8,128)(2,1)} %collective-permute-done.17.far1), channel_id=1, source_target_pairs={{4,0},{8,12},{5,1},{9,13},{6,2},{10,14},{7,3},{11,15},{20,16},{24,... | collective-permute-start | bytes 2359304 | tf_op jit(solution)/shard_map/ppermute | solution.py:150
  199.6 68.3 %collective-permute-start.13 = (bf16[512,384]{1,0:T(8,128)(2,1)}, bf16[512,384]{1,0:T(8,128)(2,1)}, u32[]{:S(2)}, u32[]{:S(2)}) collective-permute-start(bf16[512,384]{1,0:T(8,128)(2,1)} %get-tuple-element.21), channel_id=1, source_target_pairs={{4,0},{8,12},{5,1},{9,13},{6,2},{10,14},{7,3},{11,15},{20,16},{24,... | collective-permute-start | bytes 1179656 | tf_op jit(solution)/shard_map/ppermute | solution.py:150
  202.9 64.9 %collective-permute-start.14 = (bf16[512,384]{1,0:T(8,128)(2,1)}, bf16[512,384]{1,0:T(8,128)(2,1)}, u32[]{:S(2)}, u32[]{:S(2)}) collective-permute-start(bf16[512,384]{1,0:T(8,128)(2,1)} %get-tuple-element.19), channel_id=1, source_target_pairs={{4,0},{8,12},{5,1},{9,13},{6,2},{10,14},{7,3},{11,15},{20,16},{24,... | collective-permute-start | bytes 1179656 | tf_op jit(solution)/shard_map/ppermute | solution.py:150
  210.1 70.8 %collective-permute-start.11 = (bf16[512,384]{1,0:T(8,128)(2,1)}, bf16[512,384]{1,0:T(8,128)(2,1)}, u32[]{:S(2)}, u32[]{:S(2)}) collective-permute-start(bf16[512,384]{1,0:T(8,128)(2,1)} %get-tuple-element.22), channel_id=1, source_target_pairs={{4,0},{8,12},{5,1},{9,13},{6,2},{10,14},{7,3},{11,15},{20,16},{24,... | collective-permute-start | bytes 1179656 | tf_op jit(solution)/shard_map/ppermute | solution.py:150
  234.2 46.6 %collective-permute-start.12 = (bf16[512,384]{1,0:T(8,128)(2,1)}, bf16[512,384]{1,0:T(8,128)(2,1)}, u32[]{:S(2)}, u32[]{:S(2)}) collective-permute-start(bf16[512,384]{1,0:T(8,128)(2,1)} %get-tuple-element.20), channel_id=1, source_target_pairs={{4,0},{8,12},{5,1},{9,13},{6,2},{10,14},{7,3},{11,15},{20,16},{24,... | collective-permute-start | bytes 1179656 | tf_op jit(solution)/shard_map/ppermute | solution.py:150
  243.8 21.0 %collective-permute-start.25 = (f32[256,256]{1,0:T(8,128)}, f32[256,256]{1,0:T(8,128)}, u32[]{:S(2)}, u32[]{:S(2)}) collective-permute-start(f32[256,256]{1,0:T(8,128)} %broadcast_select_fusion), channel_id=1, source_target_pairs={{0,1},{1,0},{2,3},{3,2},{4,5},{5,4},{6,7},{7,6},{8,9},{9,8},{10,11... | collective-permute-start | bytes 786440 | tf_op jit(solution)/shard_map/ppermute | solution.py:170
  266.6 27.3 %collective-permute-start.26 = (f32[256,256]{1,0:T(8,128)}, f32[256,256]{1,0:T(8,128)}, u32[]{:S(2)}, u32[]{:S(2)}) collective-permute-start(f32[256,256]{1,0:T(8,128)} %shard_map.40), channel_id=1, source_target_pairs={{1,0},{3,2},{5,4},{7,6},{9,8},{11,10},{13,12},{15,14},{17,16},{19,... | collective-permute-start | bytes 786440 | tf_op jit(solution)/shard_map/ppermute | solution.py:164
  (18 other events, 188.8 us)

commit v4 on v3

--- a/solution.py
+++ b/solution.py
@@ -11,6 +11,7 @@
 F32 = jnp.float32
 ROWS = 8
 WIDE = 4
+LIMIT = 24 * 2**20
 
 
 def plain(factor_ac, factor_bd, amplitudes):
@@ -24,11 +25,10 @@
 
 
 def block_kernel(first, starts, rows, c_start, where, own, near, far0, far1, end0, end1,
-                 b0, b1, b2, b3, t_ref, r_ref, out_ref, a_v, b_v, t_v, i_v, a_sem, b_sem, t_sem):
+                 b_ref, t_ref, r_ref, out_ref, a_v, t_v, i_v, a_sem, t_sem):
     depth = own.shape[1]
     count = rows // ROWS
-    b_count, _, width = b0.shape
-    steps = b_count // WIDE
+    b_count, _, width = b_ref.shape
     sources = (own, near, far0, far1, end0, end1)
 
     def a_copy(index, slot):
@@ -36,48 +36,34 @@
         column = pl.ds(pl.multiple_of(where[slot] * depth, 128), depth)
         return pltpu.make_async_copy(source, a_v.at[:, column], a_sem.at[slot])
 
-    def b_copy(step, slot):
-        span = pl.ds(step * WIDE, WIDE)
-        deep = pl.ds(pl.multiple_of(where[4 + slot] * depth, 128), depth)
-        return pltpu.make_async_copy((b0, b1, b2, b3)[slot].at[span], b_v.at[span, deep, :], b_sem.at[step, slot])
-
     t_copy = pltpu.make_async_copy(t_ref.at[pl.ds(c_start, count)], t_v, t_sem)
     a_copy(0, 0).start()
     a_copy(1, 1).start()
 
-    @pl.when(where[8] == 1)
+    @pl.when(where[4] == 1)
     def _():
         a_copy(4, 2).start()
         a_copy(5, 3).start()
 
-    @pl.when(where[8] == 0)
+    @pl.when(where[4] == 0)
     def _():
         a_copy(2, 2).start()
         a_copy(3, 3).start()
 
-    for slot in range(4):
-        b_copy(0, slot).start()
-
-    def begin(step, carry):
-        for slot in range(4):
-            b_copy(step, slot).start()
-        return carry
-
-    lax.fori_loop(1, steps, begin, 0)
     t_copy.start()
     for slot in range(4):
         a_copy(slot, slot).wait()
 
     def contract(step, carry):
-        for slot in range(4):
-            b_copy(step, slot).wait()
-        right = jnp.concatenate([b_v[step * WIDE + m] for m in range(WIDE)], axis=1)
-        part = jnp.dot(a_v[...], right, preferred_element_type=F32).reshape(count, ROWS, WIDE * width)
+        start = step * WIDE
+        right = jnp.concatenate([b_ref[start + m] for m in range(WIDE)], axis=1)
+        part = jnp.dot(a_v[...], right, preferred_element_type=F32)
+        part = part.reshape(count, ROWS, WIDE * width)
         tall = jnp.concatenate([part[:, :, m * width:(m + 1) * width] for m in range(WIDE)], axis=1)
-        i_v[:, pl.ds(pl.multiple_of(WIDE * ROWS * step, WIDE * ROWS), WIDE * ROWS), :] = tall.astype(jnp.bfloat16)
+        i_v[:, pl.ds(pl.multiple_of(ROWS * start, WIDE * ROWS), WIDE * ROWS), :] = tall.astype(jnp.bfloat16)
         return carry
 
-    lax.fori_loop(0, steps, contract, 0)
+    lax.fori_loop(0, b_count // WIDE, contract, 0)
     t_copy.wait()
     group = 8
     total = jnp.zeros(out_ref.shape, F32) if first else r_ref[...]
@@ -88,10 +74,35 @@
     out_ref[...] = total
 
 
-def block(first, where, pieces, starts, rows, quarters, amplitudes, c_start, total):
+def gather_kernel(b0, b1, b2, b3, out_ref, sem):
+    depth = b0.shape[1]
+    copies = [
+        pltpu.make_async_copy(b, out_ref.at[:, pl.ds(m * depth, depth), :], sem.at[m])
+        for m, b in enumerate((b0, b1, b2, b3))
+    ]
+    for copy in copies:
+        copy.start()
+    for copy in copies:
+        copy.wait()
+
+
+def gathered(quarters):
+    b_count, depth, width = quarters[0].shape
+    anywhere = pl.BlockSpec(memory_space=pl.ANY)
+    return pl.pallas_call(
+        gather_kernel,
+        in_specs=[anywhere] * 4,
+        out_specs=pl.BlockSpec(memory_space=pltpu.VMEM),
+        out_shape=pltpu.VMEM((b_count, 4 * depth, width), quarters[0].dtype),
+        scratch_shapes=[pltpu.SemaphoreType.DMA((4,))],
+        compiler_params=pltpu.CompilerParams(vmem_limit_bytes=2**20),
+    )(*quarters)
+
+
+def block(first, where, pieces, starts, rows, whole_bd, amplitudes, c_start, total):
     depth = pieces[0].shape[1]
     count = rows // ROWS
-    b_count, _, width = quarters[0].shape
+    b_count, _, width = whole_bd.shape
     pairs = amplitudes.shape[2]
     q_count = depth * 4
     shape = (b_count * ROWS, pairs)
@@ -100,25 +111,23 @@
     inside = pl.BlockSpec(memory_space=pltpu.VMEM)
     return pl.pallas_call(
         functools.partial(block_kernel, first, starts, rows, c_start),
-        in_specs=[pl.BlockSpec(memory_space=pltpu.SMEM)] + [anywhere] * 11 + [inside],
+        in_specs=[pl.BlockSpec(memory_space=pltpu.SMEM)] + [anywhere] * 6 + [inside, anywhere, inside],
         out_specs=inside,
         scratch_shapes=[
             pltpu.VMEM((rows, q_count), jnp.bfloat16),
-            pltpu.VMEM((b_count, q_count, width), jnp.bfloat16),
             pltpu.VMEM((count, width, pairs), jnp.bfloat16),
             pltpu.VMEM((count, b_count * ROWS, width), jnp.bfloat16),
             pltpu.SemaphoreType.DMA((4,)),
-            pltpu.SemaphoreType.DMA((b_count // WIDE, 4)),
             pltpu.SemaphoreType.DMA,
         ],
         out_shape=jax.ShapeDtypeStruct(shape, F32),
-        compiler_params=pltpu.CompilerParams(vmem_limit_bytes=66977792),
+        compiler_params=pltpu.CompilerParams(vmem_limit_bytes=LIMIT),
         cost_estimate=pl.CostEstimate(
             flops=flops,
             transcendentals=0,
             bytes_accessed=2 * (b_count * q_count * width + count * width * pairs + rows * q_count),
         ),
-    )(where, *pieces, *quarters, amplitudes, total)
+    )(where, *pieces, pltpu.with_memory_space_constraint(whole_bd, pltpu.VMEM), amplitudes, total)
 
 
 INNER = [(1, 2), (2, 1)]
@@ -136,8 +145,8 @@
     dev, col = lax.axis_index("dev").astype(jnp.int32), lax.axis_index("col").astype(jnp.int32)
     low = dev < 2
     outer = (dev == 0) | (dev == 3)
-    where = [dev, dev ^ 1, jnp.where(low, 2, 1), jnp.where(low, 3, 0), col, col ^ 1, col ^ 2, col ^ 3, outer]
-    where = jnp.stack([x.astype(jnp.int32) for x in where])
+    order = [dev, dev ^ 1, jnp.where(low, 2, 1), jnp.where(low, 3, 0)]
+    where = jnp.stack([x ^ col for x in order] + [outer.astype(jnp.int32)])
     groups = a_count // ROWS
     mid = c_count // 2
     spans = [[(0, c_count)]] * (groups - 1) + [[(0, mid), (mid, c_count)]]
@@ -157,37 +166,31 @@
     across = lax.ppermute(turned_bd, "col", shuffled(n_col, 2))
     beside = lax.ppermute(turned_bd, "col", shuffled(n_col, 1))
     diagonal = lax.ppermute(across, "col", shuffled(n_col, 1))
-    quarters = (turned_bd, beside, across, diagonal)
+    whole_bd = gathered((turned_bd, beside, across, diagonal))
 
     def to_owner(group, total):
         with_core = [(i, i ^ 1) for i in range(n_col) if i % 2 != group % 2]
         early = total + lax.ppermute(total, "col", with_core)
         return early + lax.ppermute(early, "col", [(group ^ 2, group)]), early
-
-    def to_owners(even, odd):
-        core = col % 2
-        keep, give = jnp.where(core == 0, even, odd), jnp.where(core == 0, odd, even)
-        early = keep + lax.ppermute(give, "col", shuffled(n_col, 1))
-        return early + lax.ppermute(early, "col", [(2, 0), (3, 1)]), early
 
     totals = []
     for g in range(groups):
         total = jnp.zeros((b_count * ROWS, pairs), F32)
         third, fourth = far0[g], far1[g]
         if len(spans[g]) > 1:
-            third, fourth, totals[1] = lax.optimization_barrier((third, fourth, totals[1]))
+            third, totals[0] = lax.optimization_barrier((third, totals[0]))
+            fourth, totals[1] = lax.optimization_barrier((fourth, totals[1]))
         end0, end1 = ends(g, third), ends(g, fourth)
         for i, (c0, c1) in enumerate(spans[g]):
             pieces = (own[g], near[g], third, fourth, end0[i], end1[i])
             starts = (c0 * ROWS,) * 4 + (0, 0)
-            total = block(i == 0, where, pieces, starts, (c1 - c0) * ROWS, quarters, amplitudes, c0, total)
+            total = block(i == 0, where, pieces, starts, (c1 - c0) * ROWS, whole_bd, amplitudes, c0, total)
         totals.append(total)
-    both, early = to_owners(totals[0], totals[1])
-    total, _ = lax.optimization_barrier((totals[2], early))
-    third, early = to_owner(2, total)
-    total, _ = lax.optimization_barrier((totals[3], early))
-    fourth, _ = to_owner(3, total)
-    mine = jnp.where(col == 3, fourth, jnp.where(col == 2, third, both))
+    mine, early = to_owner(0, totals[0])
+    for group in range(1, groups):
+        total, _ = lax.optimization_barrier((totals[group], early))
+        whole, early = to_owner(group, total)
+        mine = jnp.where(col == group, whole, mine)
     mine = mine.reshape(n_dev, b_count // n_dev * ROWS, pairs)
     out = lax.dynamic_index_in_dim(mine, dev, 0, keepdims=False)
     for mask in range(1, n_dev):

time: 325 us -> 328 us (level)
  waiting for transfers between devices: 157 us -> 169 us
  Pallas kernels: 88.8 us -> 81.6 us
  other arithmetic: 6.6 us -> 0.3 us
  local copies, waits for them, and re-layouts: 17.2 us -> 21.1 us
    pallas_call x5, Pallas kernels: 88.8 us -> 77.5 us  [block(): pl.pallas_call(functools.partial(block_kernel, first, starts, rows, c_sta...]
    transpose x5, local copies, waits for them, and re-layouts: 5.17 us -> 12.6 us  [turned(): factor_ac[:, g * ROWS:(g + 1) * ROWS].transpose(2, 1, 0)]
    ppermute x1, waiting for transfers between devices: 63.2 us -> 68.2 us  [laddered(): across = lax.ppermute(turned_bd, 'col', shuffled(n_col, 2))]
    ppermute x4, waiting for transfers between devices: 39.5 us -> 44.1 us  [laddered(): near = [lax.ppermute(x, 'dev', shuffled(n_dev, 1)) for x in own]]
    pallas_call x0 -> x1, Pallas kernels: none -> 4.09 us  [gathered(): pl.pallas_call(gather_kernel, in_specs=[anywhere] * 4, out_specs=pl.Block...]
    ppermute x2 -> x4, starting transfers between devices: 5.02 us -> 8.7 us  [to_owner(): early = total + lax.ppermute(total, 'col', with_core)]
    ppermute x2 -> x4, starting transfers between devices: 5.25 us -> 7.22 us  [to_owner(): return (early + lax.ppermute(early, 'col', [(group ^ 2, group)]), early)]
  transfers between devices with their start and end apart: 34 -> 36, of which waited for: 11 -> 13; matrix products, arithmetic and copies ran while one was open for 5% -> 4% of each run, Pallas kernels for 27% -> 25%
where the time goes in v4:
time: 328 us; the launch traced here: 327 us
  waiting for transfers between devices  169 us (52%)
  Pallas kernels  81.6 us (25%)
  starting transfers between devices  54.5 us (17%)
  local copies, waits for them, and re-layouts  21.1 us (6%)
    pallas_call x5, Pallas kernels, block(): pl.pallas_call(functools.partial(block_kernel, first, starts, rows, c_sta...  77.5 us
    ppermute x1, waiting for transfers between devices, laddered(): across = lax.ppermute(turned_bd, 'col', shuffled(n_col, 2))  68.2 us
    ppermute x10, waiting for transfers between devices, ends(): return [lax.ppermute(part, 'dev', TO_END) for part in parts]  47.2 us
    ppermute x4, waiting for transfers between devices, laddered(): near = [lax.ppermute(x, 'dev', shuffled(n_dev, 1)) for x in own]  44.1 us
    ppermute x10, starting transfers between devices, ends(): return [lax.ppermute(part, 'dev', TO_END) for part in parts]  13.1 us
    transpose x5, local copies, waits for them, and re-layouts, turned(): factor_ac[:, g * ROWS:(g + 1) * ROWS].transpose(2, 1, 0)  12.6 us
    ppermute x4, starting transfers between devices, laddered(): near = [lax.ppermute(x, 'dev', shuffled(n_dev, 1)) for x in own]  8.88 us
    ppermute x4, starting transfers between devices, to_owner(): early = total + lax.ppermute(total, 'col', with_core)  8.7 us
  transfers between devices with their start and end apart: 36, of which 13 were waited for; matrix products, arithmetic and copies ran while one was open for 4% of the time, Pallas kernels for 25%

profile of v4, /device:TPU:0, one launch (start us, length us, event | category | flops | bytes accessed | tf_op | source)
XLA Modules:
  0.0 327.2 jit_solution(10414502684199853995)
XLA Ops:
  0.0 3.3 copy.16
  3.3 3.0 collective-permute-start.8
  6.3 68.2 %collective-permute-done.8.b2 = bf16[32,384,128]{2,1,0:T(8,128)(2,1)} collective-permute-done((bf16[32,384,128]{2,1,0:T(8,128)(2,1)S(1)}, bf16[32,384,128]{2,1,0:T(8,128)(2,1)}, u32[]{:S(2)}, u32[]{:S(2)}) %collective-permute-start.8) | collective-permute-done | bytes 3145760 | tf_op jit(solution)/shard_map/ppermute | solution.py:166
  85.2 3.5 %collective-permute-start = (bf16[1024,384]{1,0:T(8,128)(2,1)}, bf16[1024,384]{1,0:T(8,128)(2,1)}, u32[]{:S(2)}, u32[]{:S(2)}) collective-permute-start(bf16[1024,384]{1,0:T(8,128)(2,1)} %bitcast.42), channel_id=1, source_target_pairs={{0,4},{4,0},{8,12},{12,8},{1,5},{5,1},{9,13},{13,9},{2,6},{6,2},{1... | collective-permute-start | bytes 2359304 | tf_op jit(solution)/shard_map/ppermute | solution.py:163
  91.3 8.5 %collective-permute-done.11.near = bf16[1024,384]{1,0:T(8,128)(2,1)} collective-permute-done((bf16[1024,384]{1,0:T(8,128)(2,1)}, bf16[1024,384]{1,0:T(8,128)(2,1)}, u32[]{:S(2)}, u32[]{:S(2)}) %collective-permute-start.11) | collective-permute-done | bytes 786464 | tf_op jit(solution)/shard_map/ppermute | solution.py:163
  105.9 10.8 %collective-permute-done.near = bf16[1024,384]{1,0:T(8,128)(2,1)} collective-permute-done((bf16[1024,384]{1,0:T(8,128)(2,1)}, bf16[1024,384]{1,0:T(8,128)(2,1)}, u32[]{:S(2)}, u32[]{:S(2)}) %collective-permute-start) | collective-permute-done | bytes 786464 | tf_op jit(solution)/shard_map/ppermute | solution.py:163
  118.2 14.9 %collective-permute-done.2.near = bf16[1024,384]{1,0:T(8,128)(2,1)} collective-permute-done((bf16[1024,384]{1,0:T(8,128)(2,1)}, bf16[1024,384]{1,0:T(8,128)(2,1)}, u32[]{:S(2)}, u32[]{:S(2)}) %collective-permute-start.2) | collective-permute-done | bytes 786464 | tf_op jit(solution)/shard_map/ppermute | solution.py:163
  139.2 4.1 %shard_map.37.b_ref = bf16[32,1536,128]{2,1,0:T(8,128)(2,1)S(1)} custom-call(bf16[32,384,128]{2,1,0:T(8,128)(2,1)S(1)} %bitcast.41, bf16[32,384,128]{2,1,0:T(8,128)(2,1)} %collective-permute-done.7.b1, bf16[32,384,128]{2,1,0:T(8,128)(2,1)} %collective-permute-done.8.b2, bf16[32,384,128]{2,1,0:T(8,128)(2,1)} %collective-permute-done.9.b3), custom_call_target="tpu_custom_call" | custom-call | tf_op jit(solution)/shard_map/pallas_call | solution.py:92
  144.0 9.9 %collective-permute-done.20.near = bf16[1024,384]{1,0:T(8,128)(2,1)} collective-permute-done((bf16[1024,384]{1,0:T(8,128)(2,1)}, bf16[1024,384]{1,0:T(8,128)(2,1)}, u32[]{:S(2)}, u32[]{:S(2)}) %collective-permute-start.20) | collective-permute-done | bytes 786464 | tf_op jit(solution)/shard_map/ppermute | solution.py:163
  154.6 16.1 %collective-permute-done.14.end0 = bf16[1024,384]{1,0:T(8,128)(2,1)} collective-permute-done((bf16[1024,384]{1,0:T(8,128)(2,1)}, bf16[1024,384]{1,0:T(8,128)(2,1)}, u32[]{:S(2)}, u32[]{:S(2)}) %collective-permute-start.14) | collective-permute-done | bytes 786464 | tf_op jit(solution)/shard_map/ppermute | solution.py:159
  172.8 14.8 %collective-permute-done.15.end1 = bf16[1024,384]{1,0:T(8,128)(2,1)} collective-permute-done((bf16[1024,384]{1,0:T(8,128)(2,1)}, bf16[1024,384]{1,0:T(8,128)(2,1)}, u32[]{:S(2)}, u32[]{:S(2)}) %collective-permute-start.15) | collective-permute-done | bytes 786464 | tf_op jit(solution)/shard_map/ppermute | solution.py:159
  188.9 3.4 %copy-done.4 = bf16[128,128,256]{2,1,0:T(8,128)(2,1)S(1)} copy-done((bf16[128,128,256]{2,1,0:T(8,128)(2,1)S(1)}, bf16[128,128,256]{2,1,0:T(8,128)(2,1)}, u32[]{:S(2)}) %copy-start.4) | copy-done | bytes 8388632
  192.3 18.9 %shard_map.39 = f32[256,256]{1,0:T(8,128)S(1)} custom-call(s32[5]{0:T(128)S(1)} %stack.27.where, bf16[1024,384]{1,0:T(8,128)(2,1)S(1)} %bitcast.54, bf16[1024,384]{1,0:T(8,128)(2,1)} %collective-permute-done.11.near, bf16[1024,384]{1,0:T(8,128)(2,1)} %collective-permute-done.12.far0, bf16[1024,384]{1,0:T(8,128)(2,1)} %collective-permute-done.13.far1, ...), custom_call_target="tpu_custom_call" | custom-call | flops 15032385536 | bytes 24117248 | tf_op jit(solution)/shard_map/pallas_call | solution.py:112
  217.1 4.2 %collective-permute-done.6.end1 = bf16[1024,384]{1,0:T(8,128)(2,1)} collective-permute-done((bf16[1024,384]{1,0:T(8,128)(2,1)}, bf16[1024,384]{1,0:T(8,128)(2,1)}, u32[]{:S(2)}, u32[]{:S(2)}) %collective-permute-start.6) | collective-permute-done | bytes 786464 | tf_op jit(solution)/shard_map/ppermute | solution.py:159
  221.3 18.7 %shard_map.38 = f32[256,256]{1,0:T(8,128)S(1)} custom-call(s32[5]{0:T(128)S(1)} %stack.27.where, bf16[1024,384]{1,0:T(8,128)(2,1)S(1)} %bitcast.51, bf16[1024,384]{1,0:T(8,128)(2,1)} %collective-permute-done.2.near, bf16[1024,384]{1,0:T(8,128)(2,1)} %collective-permute-done.3.far0, bf16[1024,384]{1,0:T(8,128)(2,1)} %collective-permute-done.4.far1, ...), custom_call_target="tpu_custom_call" | custom-call | flops 15032385536 | bytes 24117248 | tf_op jit(solution)/shard_map/pallas_call | solution.py:112
  244.0 12.1 %collective-permute-done.24.end1 = bf16[1024,384]{1,0:T(8,128)(2,1)S(1)} collective-permute-done((bf16[1024,384]{1,0:T(8,128)(2,1)S(1)}, bf16[1024,384]{1,0:T(8,128)(2,1)S(1)}, u32[]{:S(2)}, u32[]{:S(2)}) %collective-permute-start.24) | collective-permute-done | bytes 786464 | tf_op jit(solution)/shard_map/ppermute | solution.py:159
  257.4 18.4 %shard_map.42 = f32[256,256]{1,0:T(8,128)S(1)} custom-call(s32[5]{0:T(128)S(1)} %stack.27.where, bf16[1024,384]{1,0:T(8,128)(2,1)S(1)} %bitcast.48, bf16[1024,384]{1,0:T(8,128)(2,1)} %collective-permute-done.20.near, bf16[1024,384]{1,0:T(8,128)(2,1)S(1)} %collective-permute-done.21.far0, bf16[1024,384]{1,0:T(8,128)(2,1)S(1)} %collective-permute-done.22.far1, ...), custom_call_target="tpu_custom_call" | custom-call | flops 15032385536 | bytes 24117248 | tf_op jit(solution)/shard_map/pallas_call | solution.py:112
  275.9 3.1 collective-permute-start.26
  279.0 10.7 %shard_map.40.r_ref = f32[256,256]{1,0:T(8,128)S(1)} custom-call(s32[5]{0:T(128)S(1)} %stack.27.where, bf16[1024,384]{1,0:T(8,128)(2,1)S(1)} %bitcast.44, bf16[1024,384]{1,0:T(8,128)(2,1)} %collective-permute-done.near, bf16[1024,384]{1,0:T(8,128)(2,1)S(1)} %collective-permute-done.1.far0, bf16[1024,384]{1,0:T(8,128)(2,1)S(1)} %collective-permute-done.10.far1, ...), custom_call_target="tpu_custom_call" | custom-call | flops 7516192768 | bytes 18350080 | tf_op jit(solution)/shard_map/pallas_call | solution.py:112
  291.1 10.7 %shard_map.41 = f32[256,256]{1,0:T(8,128)S(1)} custom-call(s32[5]{0:T(128)S(1)} %stack.27.where, bf16[1024,384]{1,0:T(8,128)(2,1)S(1)} %bitcast.45, bf16[1024,384]{1,0:T(8,128)(2,1)} %collective-permute-done.near, bf16[1024,384]{1,0:T(8,128)(2,1)S(1)} %collective-permute-done.1.far0, bf16[1024,384]{1,0:T(8,128)(2,1)S(1)} %collective-permute-done.10.far1, ...), custom_call_target="tpu_custom_call" | custom-call | flops 7516192768 | bytes 18350080 | tf_op jit(solution)/shard_map/pallas_call | solution.py:112
  301.9 3.1 collective-permute-start.28
  307.0 4.6 %collective-permute-start.30 = (f32[256,256]{1,0:T(8,128)S(1)}, f32[256,256]{1,0:T(8,128)S(1)}, u32[]{:S(2)}, u32[]{:S(2)}) collective-permute-start(f32[256,256]{1,0:T(8,128)S(1)} %add.48), channel_id=1, source_target_pairs={{0,2},{4,6},{8,10},{12,14},{16,18},{20,22},{24,26},{28,30}} | collective-permute-start | bytes 786440 | tf_op jit(solution)/shard_map/ppermute | solution.py:174
  317.3 3.1 collective-permute-start.34
  323.1 3.4 %collective-permute-done.35 = f32[64,256]{1,0:T(8,128)S(1)} collective-permute-done((f32[64,256]{1,0:T(8,128)S(1)}, f32[64,256]{1,0:T(8,128)S(1)}, u32[]{:S(2)}, u32[]{:S(2)}) %collective-permute-start.35) | collective-permute-done | bytes 65568 | tf_op jit(solution)/shard_map/ppermute | solution.py:198
  (89 shorter events, 55.2 us)
Async XLA Ops:
  3.3 71.2 %collective-permute-start.8 = (bf16[32,384,128]{2,1,0:T(8,128)(2,1)S(1)}, bf16[32,384,128]{2,1,0:T(8,128)(2,1)}, u32[]{:S(2)}, u32[]{:S(2)}) collective-permute-start(bf16[32,384,128]{2,1,0:T(8,128)(2,1)S(1)} %bitcast.39), channel_id=1, source_target_pairs={{0,2},{1,3},{2,0},{3,1},{4,6},{5,7},{6,4},{7,5},{8,10},{9,11},{10,... | collective-permute-start | bytes 9437192 | tf_op jit(solution)/shard_map/ppermute | solution.py:166
  6.3 129.9 %collective-permute-start.7 = (bf16[32,384,128]{2,1,0:T(8,128)(2,1)S(1)}, bf16[32,384,128]{2,1,0:T(8,128)(2,1)}, u32[]{:S(2)}, u32[]{:S(2)}) collective-permute-start(bf16[32,384,128]{2,1,0:T(8,128)(2,1)S(1)} %bitcast.40), channel_id=1, source_target_pairs={{0,1},{1,0},{2,3},{3,2},{4,5},{5,4},{6,7},{7,6},{8,9},{9,8},{10,11... | collective-permute-start | bytes 9437192 | tf_op jit(solution)/shard_map/ppermute | solution.py:167
  74.5 63.3 %collective-permute-start.9 = (bf16[32,384,128]{2,1,0:T(8,128)(2,1)}, bf16[32,384,128]{2,1,0:T(8,128)(2,1)}, u32[]{:S(2)}, u32[]{:S(2)}) collective-permute-start(bf16[32,384,128]{2,1,0:T(8,128)(2,1)} %collective-permute-done.8.b2), channel_id=1, source_target_pairs={{0,1},{1,0},{2,3},{3,2},{4,5},{5,4},{6,7},{7,6},{8,9},{9,8},{10,11... | collective-permute-start | bytes 9437192 | tf_op jit(solution)/shard_map/ppermute | solution.py:168
  79.1 20.7 %collective-permute-start.11 = (bf16[1024,384]{1,0:T(8,128)(2,1)}, bf16[1024,384]{1,0:T(8,128)(2,1)}, u32[]{:S(2)}, u32[]{:S(2)}) collective-permute-start(bf16[1024,384]{1,0:T(8,128)(2,1)} %bitcast.52), channel_id=1, source_target_pairs={{0,4},{4,0},{8,12},{12,8},{1,5},{5,1},{9,13},{13,9},{2,6},{6,2},{1... | collective-permute-start | bytes 2359304 | tf_op jit(solution)/shard_map/ppermute | solution.py:163
  80.9 20.7 %collective-permute-start.12 = (bf16[1024,384]{1,0:T(8,128)(2,1)}, bf16[1024,384]{1,0:T(8,128)(2,1)}, u32[]{:S(2)}, u32[]{:S(2)}) collective-permute-start(bf16[1024,384]{1,0:T(8,128)(2,1)} %bitcast.53), channel_id=1, source_target_pairs={{4,8},{8,4},{5,9},{9,5},{6,10},{10,6},{7,11},{11,7},{20,24},{24,20... | collective-permute-start | bytes 2359304 | tf_op jit(solution)/shard_map/ppermute | solution.py:164
  85.2 31.5 %collective-permute-start = (bf16[1024,384]{1,0:T(8,128)(2,1)}, bf16[1024,384]{1,0:T(8,128)(2,1)}, u32[]{:S(2)}, u32[]{:S(2)}) collective-permute-start(bf16[1024,384]{1,0:T(8,128)(2,1)} %bitcast.42), channel_id=1, source_target_pairs={{0,4},{4,0},{8,12},{12,8},{1,5},{5,1},{9,13},{13,9},{2,6},{6,2},{1... | collective-permute-start | bytes 2359304 | tf_op jit(solution)/shard_map/ppermute | solution.py:163
  99.8 33.3 %collective-permute-start.2 = (bf16[1024,384]{1,0:T(8,128)(2,1)}, bf16[1024,384]{1,0:T(8,128)(2,1)}, u32[]{:S(2)}, u32[]{:S(2)}) collective-permute-start(bf16[1024,384]{1,0:T(8,128)(2,1)} %bitcast.49), channel_id=1, source_target_pairs={{0,4},{4,0},{8,12},{12,8},{1,5},{5,1},{9,13},{13,9},{2,6},{6,2},{1... | collective-permute-start | bytes 2359304 | tf_op jit(solution)/shard_map/ppermute | solution.py:163
  101.7 33.2 %collective-permute-start.13 = (bf16[1024,384]{1,0:T(8,128)(2,1)}, bf16[1024,384]{1,0:T(8,128)(2,1)}, u32[]{:S(2)}, u32[]{:S(2)}) collective-permute-start(bf16[1024,384]{1,0:T(8,128)(2,1)} %collective-permute-done.11.near), channel_id=1, source_target_pairs={{4,8},{8,4},{5,9},{9,5},{6,10},{10,6},{7,11},{11,7},{20,24},{24,20... | collective-permute-start | bytes 2359304 | tf_op jit(solution)/shard_map/ppermute | solution.py:165
  116.7 26.6 %collective-permute-start.3 = (bf16[1024,384]{1,0:T(8,128)(2,1)}, bf16[1024,384]{1,0:T(8,128)(2,1)}, u32[]{:S(2)}, u32[]{:S(2)}) collective-permute-start(bf16[1024,384]{1,0:T(8,128)(2,1)} %bitcast.50), channel_id=1, source_target_pairs={{4,8},{8,4},{5,9},{9,5},{6,10},{10,6},{7,11},{11,7},{20,24},{24,20... | collective-permute-start | bytes 2359304 | tf_op jit(solution)/shard_map/ppermute | solution.py:164
  134.9 35.8 %collective-permute-start.14 = (bf16[1024,384]{1,0:T(8,128)(2,1)}, bf16[1024,384]{1,0:T(8,128)(2,1)}, u32[]{:S(2)}, u32[]{:S(2)}) collective-permute-start(bf16[1024,384]{1,0:T(8,128)(2,1)} %collective-permute-done.12.far0), channel_id=1, source_target_pairs={{4,0},{8,12},{5,1},{9,13},{6,2},{10,14},{7,3},{11,15},{20,16},{24,... | collective-permute-start | bytes 2359304 | tf_op jit(solution)/shard_map/ppermute | solution.py:159
  136.2 35.8 %collective-permute-start.4 = (bf16[1024,384]{1,0:T(8,128)(2,1)}, bf16[1024,384]{1,0:T(8,128)(2,1)}, u32[]{:S(2)}, u32[]{:S(2)}) collective-permute-start(bf16[1024,384]{1,0:T(8,128)(2,1)} %collective-permute-done.2.near), channel_id=1, source_target_pairs={{4,8},{8,4},{5,9},{9,5},{6,10},{10,6},{7,11},{11,7},{20,24},{24,20... | collective-permute-start | bytes 2359304 | tf_op jit(solution)/shard_map/ppermute | solution.py:165
  137.8 49.8 %collective-permute-start.15 = (bf16[1024,384]{1,0:T(8,128)(2,1)}, bf16[1024,384]{1,0:T(8,128)(2,1)}, u32[]{:S(2)}, u32[]{:S(2)}) collective-permute-start(bf16[1024,384]{1,0:T(8,128)(2,1)} %collective-permute-done.13.far1), channel_id=1, source_target_pairs={{4,0},{8,12},{5,1},{9,13},{6,2},{10,14},{7,3},{11,15},{20,16},{24,... | collective-permute-start | bytes 2359304 | tf_op jit(solution)/shard_map/ppermute | solution.py:159
  143.3 67.9 %collective-permute-start.21 = (bf16[1024,384]{1,0:T(8,128)(2,1)S(1)}, bf16[1024,384]{1,0:T(8,128)(2,1)S(1)}, u32[]{:S(2)}, u32[]{:S(2)}) collective-permute-start(bf16[1024,384]{1,0:T(8,128)(2,1)S(1)} %bitcast.47), channel_id=1, source_target_pairs={{4,8},{8,4},{5,9},{9,5},{6,10},{10,6},{7,11},{11,7},{20,24},{24,20... | collective-permute-start | bytes 2359304 | tf_op jit(solution)/shard_map/ppermute | solution.py:164
  153.9 58.1 %collective-permute-start.10 = (bf16[1024,384]{1,0:T(8,128)(2,1)}, bf16[1024,384]{1,0:T(8,128)(2,1)S(1)}, u32[]{:S(2)}, u32[]{:S(2)}) collective-permute-start(bf16[1024,384]{1,0:T(8,128)(2,1)} %collective-permute-done.near), channel_id=1, source_target_pairs={{4,8},{8,4},{5,9},{9,5},{6,10},{10,6},{7,11},{11,7},{20,24},{24,20... | collective-permute-start | bytes 2359304 | tf_op jit(solution)/shard_map/ppermute | solution.py:165
  170.7 44.8 %collective-permute-start.5 = (bf16[1024,384]{1,0:T(8,128)(2,1)}, bf16[1024,384]{1,0:T(8,128)(2,1)S(1)}, u32[]{:S(2)}, u32[]{:S(2)}) collective-permute-start(bf16[1024,384]{1,0:T(8,128)(2,1)} %collective-permute-done.3.far0), channel_id=1, source_target_pairs={{4,0},{8,12},{5,1},{9,13},{6,2},{10,14},{7,3},{11,15},{20,16},{24,... | collective-permute-start | bytes 2359304 | tf_op jit(solution)/shard_map/ppermute | solution.py:159
  172.0 41.2 %collective-permute-start.22 = (bf16[1024,384]{1,0:T(8,128)(2,1)}, bf16[1024,384]{1,0:T(8,128)(2,1)S(1)}, u32[]{:S(2)}, u32[]{:S(2)}) collective-permute-start(bf16[1024,384]{1,0:T(8,128)(2,1)} %collective-permute-done.20.near), channel_id=1, source_target_pairs={{4,8},{8,4},{5,9},{9,5},{6,10},{10,6},{7,11},{11,7},{20,24},{24,20... | collective-permute-start | bytes 2359304 | tf_op jit(solution)/shard_map/ppermute | solution.py:165
  187.6 33.7 %collective-permute-start.6 = (bf16[1024,384]{1,0:T(8,128)(2,1)}, bf16[1024,384]{1,0:T(8,128)(2,1)}, u32[]{:S(2)}, u32[]{:S(2)}) collective-permute-start(bf16[1024,384]{1,0:T(8,128)(2,1)} %collective-permute-done.4.far1), channel_id=1, source_target_pairs={{4,0},{8,12},{5,1},{9,13},{6,2},{10,14},{7,3},{11,15},{20,16},{24,... | collective-permute-start | bytes 2359304 | tf_op jit(solution)/shard_map/ppermute | solution.py:159
  211.2 28.8 %collective-permute-start.1 = (bf16[1024,384]{1,0:T(8,128)(2,1)S(1)}, bf16[1024,384]{1,0:T(8,128)(2,1)S(1)}, u32[]{:S(2)}, u32[]{:S(2)}) collective-permute-start(bf16[1024,384]{1,0:T(8,128)(2,1)S(1)} %bitcast.43), channel_id=1, source_target_pairs={{4,8},{8,4},{5,9},{9,5},{6,10},{10,6},{7,11},{11,7},{20,24},{24,20... | collective-permute-start | bytes 2359304 | tf_op jit(solution)/shard_map/ppermute | solution.py:164
  212.0 30.7 %collective-permute-start.23 = (bf16[1024,384]{1,0:T(8,128)(2,1)S(1)}, bf16[1024,384]{1,0:T(8,128)(2,1)S(1)}, u32[]{:S(2)}, u32[]{:S(2)}) collective-permute-start(bf16[1024,384]{1,0:T(8,128)(2,1)S(1)} %collective-permute-done.21.far0), channel_id=1, source_target_pairs={{4,0},{8,12},{5,1},{9,13},{6,2},{10,14},{7,3},{11,15},{20,16},{24,... | collective-permute-start | bytes 2359304 | tf_op jit(solution)/shard_map/ppermute | solution.py:159
  213.3 42.8 %collective-permute-start.24 = (bf16[1024,384]{1,0:T(8,128)(2,1)S(1)}, bf16[1024,384]{1,0:T(8,128)(2,1)S(1)}, u32[]{:S(2)}, u32[]{:S(2)}) collective-permute-start(bf16[1024,384]{1,0:T(8,128)(2,1)S(1)} %collective-permute-done.22.far1), channel_id=1, source_target_pairs={{4,0},{8,12},{5,1},{9,13},{6,2},{10,14},{7,3},{11,15},{20,16},{24,... | collective-permute-start | bytes 2359304 | tf_op jit(solution)/shard_map/ppermute | solution.py:159
  215.6 63.4 %collective-permute-start.19 = (bf16[512,384]{1,0:T(8,128)(2,1)}, bf16[512,384]{1,0:T(8,128)(2,1)S(1)}, u32[]{:S(2)}, u32[]{:S(2)}) collective-permute-start(bf16[512,384]{1,0:T(8,128)(2,1)} %get-tuple-element.23), channel_id=1, source_target_pairs={{4,0},{8,12},{5,1},{9,13},{6,2},{10,14},{7,3},{11,15},{20,16},{24,... | collective-permute-start | bytes 1179656 | tf_op jit(solution)/shard_map/ppermute | solution.py:159
  240.1 38.9 %collective-permute-start.18 = (bf16[512,384]{1,0:T(8,128)(2,1)S(1)}, bf16[512,384]{1,0:T(8,128)(2,1)S(1)}, u32[]{:S(2)}, u32[]{:S(2)}) collective-permute-start(bf16[512,384]{1,0:T(8,128)(2,1)S(1)} %get-tuple-element.25), channel_id=1, source_target_pairs={{4,0},{8,12},{5,1},{9,13},{6,2},{10,14},{7,3},{11,15},{20,16},{24,... | collective-permute-start | bytes 1179656 | tf_op jit(solution)/shard_map/ppermute | solution.py:159
  241.4 49.7 %collective-permute-start.17 = (bf16[512,384]{1,0:T(8,128)(2,1)}, bf16[512,384]{1,0:T(8,128)(2,1)S(1)}, u32[]{:S(2)}, u32[]{:S(2)}) collective-permute-start(bf16[512,384]{1,0:T(8,128)(2,1)} %get-tuple-element.24), channel_id=1, source_target_pairs={{4,0},{8,12},{5,1},{9,13},{6,2},{10,14},{7,3},{11,15},{20,16},{24,... | collective-permute-start | bytes 1179656 | tf_op jit(solution)/shard_map/ppermute | solution.py:159
  242.7 48.4 %collective-permute-start.16 = (bf16[512,384]{1,0:T(8,128)(2,1)S(1)}, bf16[512,384]{1,0:T(8,128)(2,1)S(1)}, u32[]{:S(2)}, u32[]{:S(2)}) collective-permute-start(bf16[512,384]{1,0:T(8,128)(2,1)S(1)} %get-tuple-element.26), channel_id=1, source_target_pairs={{4,0},{8,12},{5,1},{9,13},{6,2},{10,14},{7,3},{11,15},{20,16},{24,... | collective-permute-start | bytes 1179656 | tf_op jit(solution)/shard_map/ppermute | solution.py:159
  (20 other events, 390.2 us)

commit v5 on v4

--- a/solution.py
+++ b/solution.py
@@ -24,35 +24,34 @@
     return lax.psum_scatter(reduced, "dev", scatter_dimension=1, tiled=True)
 
 
-def block_kernel(first, starts, rows, c_start, where, own, near, far0, far1, end0, end1,
-                 b_ref, t_ref, r_ref, out_ref, a_v, t_v, i_v, a_sem, t_sem):
-    depth = own.shape[1]
+def block_kernel(first, rows, c_start, where, held, far, end, b_ref, t_ref, r_ref, out_ref,
+                 a_v, t_v, i_v, a_sem, t_sem):
+    depth = held.shape[1]
     count = rows // ROWS
     b_count, _, width = b_ref.shape
-    sources = (own, near, far0, far1, end0, end1)
-
-    def a_copy(index, slot):
-        source = sources[index].at[pl.ds(starts[index], rows), :]
+
+    def a_copy(source, slot):
+        span = pl.ds(slot % 2 * rows, rows)
         column = pl.ds(pl.multiple_of(where[slot] * depth, 128), depth)
-        return pltpu.make_async_copy(source, a_v.at[:, column], a_sem.at[slot])
+        return pltpu.make_async_copy(source.at[span, :], a_v.at[:, column], a_sem.at[slot])
 
     t_copy = pltpu.make_async_copy(t_ref.at[pl.ds(c_start, count)], t_v, t_sem)
-    a_copy(0, 0).start()
-    a_copy(1, 1).start()
+    a_copy(held, 0).start()
+    a_copy(held, 1).start()
 
     @pl.when(where[4] == 1)
     def _():
-        a_copy(4, 2).start()
-        a_copy(5, 3).start()
+        a_copy(end, 2).start()
+        a_copy(end, 3).start()
 
     @pl.when(where[4] == 0)
     def _():
-        a_copy(2, 2).start()
-        a_copy(3, 3).start()
+        a_copy(far, 2).start()
+        a_copy(far, 3).start()
 
     t_copy.start()
     for slot in range(4):
-        a_copy(slot, slot).wait()
+        a_copy(held, slot).wait()
 
     def contract(step, carry):
         start = step * WIDE
@@ -74,8 +73,9 @@
     out_ref[...] = total
 
 
-def gather_kernel(b0, b1, b2, b3, out_ref, sem):
+def gather_kernel(b0, b1, b2, b3, out_ref, token_ref, sem):
     depth = b0.shape[1]
+    token_ref[...] = jnp.zeros(token_ref.shape, F32)
     copies = [
         pltpu.make_async_copy(b, out_ref.at[:, pl.ds(m * depth, depth), :], sem.at[m])
         for m, b in enumerate((b0, b1, b2, b3))
@@ -92,15 +92,18 @@
     return pl.pallas_call(
         gather_kernel,
         in_specs=[anywhere] * 4,
-        out_specs=pl.BlockSpec(memory_space=pltpu.VMEM),
-        out_shape=pltpu.VMEM((b_count, 4 * depth, width), quarters[0].dtype),
+        out_specs=[pl.BlockSpec(memory_space=pltpu.VMEM)] * 2,
+        out_shape=[
+            pltpu.VMEM((b_count, 4 * depth, width), quarters[0].dtype),
+            jax.ShapeDtypeStruct((8, 128), F32),
+        ],
         scratch_shapes=[pltpu.SemaphoreType.DMA((4,))],
         compiler_params=pltpu.CompilerParams(vmem_limit_bytes=2**20),
     )(*quarters)
 
 
-def block(first, where, pieces, starts, rows, whole_bd, amplitudes, c_start, total):
-    depth = pieces[0].shape[1]
+def block(first, where, pieces, whole_bd, amplitudes, c_start, total):
+    rows, depth = pieces[0].shape[0] // 2, pieces[0].shape[1]
     count = rows // ROWS
     b_count, _, width = whole_bd.shape
     pairs = amplitudes.shape[2]
@@ -110,8 +113,8 @@
     anywhere = pl.BlockSpec(memory_space=pl.ANY)
     inside = pl.BlockSpec(memory_space=pltpu.VMEM)
     return pl.pallas_call(
-        functools.partial(block_kernel, first, starts, rows, c_start),
-        in_specs=[pl.BlockSpec(memory_space=pltpu.SMEM)] + [anywhere] * 6 + [inside, anywhere, inside],
+        functools.partial(block_kernel, first, rows, c_start),
+        in_specs=[pl.BlockSpec(memory_space=pltpu.SMEM)] + [anywhere] * 3 + [inside, anywhere, inside],
         out_specs=inside,
         scratch_shapes=[
             pltpu.VMEM((rows, q_count), jnp.bfloat16),
@@ -148,49 +151,59 @@
     order = [dev, dev ^ 1, jnp.where(low, 2, 1), jnp.where(low, 3, 0)]
     where = jnp.stack([x ^ col for x in order] + [outer.astype(jnp.int32)])
     groups = a_count // ROWS
-    mid = c_count // 2
-    spans = [[(0, c_count)]] * (groups - 1) + [[(0, mid), (mid, c_count)]]
-
-    def turned(g):
-        return factor_ac[:, g * ROWS:(g + 1) * ROWS].transpose(2, 1, 0).reshape(c_count * ROWS, depth)
-
-    def ends(g, x):
-        parts = [x[c0 * ROWS:c1 * ROWS] for c0, c1 in spans[g]] if len(spans[g]) > 1 else [x]
-        return [lax.ppermute(part, "dev", TO_END) for part in parts]
-
-    own = [turned(g) for g in range(groups)]
+    eighth = c_count // 8
+    cuts = [(0, 8), (0, 8), (0, 4, 8), (0, 3, 6, 8)]
+    spans = [[(p * eighth, q * eighth) for p, q in zip(cut, cut[1:])] for cut in cuts]
+
+    def raw(g):
+        return factor_ac[:, g * ROWS:(g + 1) * ROWS]
+
+    def turned(x):
+        return lax.optimization_barrier(x.transpose(2, 1, 0).reshape(c_count * ROWS, depth))
+
+    first = lax.optimization_barrier(raw(0))
+    own = [turned(first)] + [turned(raw(g)) for g in range(1, groups)]
     turned_bd = factor_bd.transpose(1, 0, 2)
-    near = [lax.ppermute(x, "dev", shuffled(n_dev, 1)) for x in own]
-    far0 = [lax.ppermute(x, "dev", INNER) for x in own]
-    far1 = [lax.ppermute(x, "dev", INNER) for x in near]
+    near = [turned(lax.ppermute(first, "dev", shuffled(n_dev, 1)))]
+    near += [lax.ppermute(own[g], "dev", shuffled(n_dev, 1)) for g in range(1, groups)]
     across = lax.ppermute(turned_bd, "col", shuffled(n_col, 2))
     beside = lax.ppermute(turned_bd, "col", shuffled(n_col, 1))
     diagonal = lax.ppermute(across, "col", shuffled(n_col, 1))
-    whole_bd = gathered((turned_bd, beside, across, diagonal))
-
-    def to_owner(group, total):
-        with_core = [(i, i ^ 1) for i in range(n_col) if i % 2 != group % 2]
-        early = total + lax.ppermute(total, "col", with_core)
-        return early + lax.ppermute(early, "col", [(group ^ 2, group)]), early
-
-    totals = []
-    for g in range(groups):
-        total = jnp.zeros((b_count * ROWS, pairs), F32)
-        third, fourth = far0[g], far1[g]
-        if len(spans[g]) > 1:
-            third, totals[0] = lax.optimization_barrier((third, totals[0]))
-            fourth, totals[1] = lax.optimization_barrier((fourth, totals[1]))
-        end0, end1 = ends(g, third), ends(g, fourth)
+    whole_bd, token = gathered((turned_bd, beside, across, diagonal))
+
+    core, chip = col % 2, col // 2
+
+    def paired(even, odd):
+        keep, give = jnp.where(core == 0, even, odd), jnp.where(core == 0, odd, even)
+        return keep + lax.ppermute(give, "col", shuffled(n_col, 1))
+
+    totals = [jnp.zeros((b_count * ROWS, pairs), F32)] * groups
+    ready = []
+
+    def send(g, *gates):
+        mine, other, *_ = lax.optimization_barrier((own[g], near[g], *gates))
         for i, (c0, c1) in enumerate(spans[g]):
-            pieces = (own[g], near[g], third, fourth, end0[i], end1[i])
-            starts = (c0 * ROWS,) * 4 + (0, 0)
-            total = block(i == 0, where, pieces, starts, (c1 - c0) * ROWS, whole_bd, amplitudes, c0, total)
-        totals.append(total)
-    mine, early = to_owner(0, totals[0])
-    for group in range(1, groups):
-        total, _ = lax.optimization_barrier((totals[group], early))
-        whole, early = to_owner(group, total)
-        mine = jnp.where(col == group, whole, mine)
+            held = jnp.concatenate([x[c0 * ROWS:c1 * ROWS] for x in (mine, other)], axis=0)
+            far = lax.ppermute(held, "dev", INNER)
+            ready.append((g, i, c0, held, far, lax.ppermute(far, "dev", TO_END)))
+
+    def work(g):
+        for h, i, c0, *parts in ready:
+            if h == g:
+                totals[g] = block(i == 0, where, parts, whole_bd, amplitudes, c0, totals[g])
+        return totals[g]
+
+    send(0)
+    send(1)
+    send(2, token)
+    send(3, work(0))
+    for g in range(1, groups):
+        work(g)
+    lower = paired(totals[0], totals[1])
+    even, odd, _ = lax.optimization_barrier((totals[2], totals[3], lower))
+    upper = paired(even, odd)
+    keep, give = jnp.where(chip == 0, lower, upper), jnp.where(chip == 0, upper, lower)
+    mine = keep + lax.ppermute(give, "col", shuffled(n_col, 2))
     mine = mine.reshape(n_dev, b_count // n_dev * ROWS, pairs)
     out = lax.dynamic_index_in_dim(mine, dev, 0, keepdims=False)
     for mask in range(1, n_dev):
@@ -211,7 +224,7 @@
         depth, a_count, c_count = factor_ac.shape
         _, b_count, width = factor_bd.shape
         fits = n_dev == 4 and n_col == 4 and width == 128 and depth % 128 == 0
-        fits = fits and a_count == ROWS * n_col and b_count % 8 == 0 and c_count % 8 == 0
+        fits = fits and a_count == ROWS * n_col and b_count % 8 == 0 and c_count % 64 == 0
         if fits:
             return laddered(n_dev, n_col, factor_ac, factor_bd, amplitudes)
         return plain(factor_ac, factor_bd, amplitudes)

time: 328 us -> 365 us (1.11)
  starting transfers between devices: 54.5 us -> 85.4 us
  waiting for transfers between devices: 169 us -> 155 us
  local copies, waits for them, and re-layouts: 21.1 us -> 34.4 us
  Pallas kernels: 81.6 us -> 86.9 us
    ppermute x30 -> x21, starting transfers between devices: 47.1 us -> 77.9 us  [the longest x3 57.5 us: laddered(): lax.ppermute(own[g], 'dev', shuffled(n_dev, 1))]
    ppermute x1, waiting for transfers between devices: 68.2 us -> 42 us  [laddered(): across = lax.ppermute(turned_bd, 'col', shuffled(n_col, 2))]
    ppermute x30 -> x21, waiting for transfers between devices: 96.1 us -> 109 us  [the longest x7 55.4 us: send(): ready.append((g, i, c0, held, far, lax.ppermute(far, 'dev', TO_END)))]
    unnamed x17 -> x29, local copies, waits for them, and re-layouts: 6.66 us -> 12.6 us
    pallas_call x6 -> x8, Pallas kernels: 81.6 us -> 86.9 us  [the longest x7 82 us: block(): pl.pallas_call(functools.partial(block_kernel, first, rows, c_start), in_...]
    transpose x5 -> x6, local copies, waits for them, and re-layouts: 12.6 us -> 15.4 us  [turned(): x.transpose(2, 1, 0).reshape(c_count * ROWS, depth)]
  transfers between devices with their start and end apart: 36 -> 27, of which waited for: 13 -> 11; matrix products, arithmetic and copies ran while one was open for 4% -> 7% of each run, Pallas kernels for 25% -> 22%
where the time goes in v5:
time: 365 us; the launch traced here: 364 us
  waiting for transfers between devices  155 us (42%)
  Pallas kernels  86.9 us (24%)
  starting transfers between devices  85.4 us (23%)
  local copies, waits for them, and re-layouts  34.4 us (9%)
    pallas_call x7, Pallas kernels, block(): pl.pallas_call(functools.partial(block_kernel, first, rows, c_start), in_...  82 us
    ppermute x3, starting transfers between devices, laddered(): lax.ppermute(own[g], 'dev', shuffled(n_dev, 1))  57.5 us
    ppermute x7, waiting for transfers between devices, send(): ready.append((g, i, c0, held, far, lax.ppermute(far, 'dev', TO_END)))  55.4 us
    ppermute x1, waiting for transfers between devices, laddered(): across = lax.ppermute(turned_bd, 'col', shuffled(n_col, 2))  42 us
    ppermute x3, waiting for transfers between devices, laddered(): lax.ppermute(own[g], 'dev', shuffled(n_dev, 1))  29.9 us
    transpose x6, local copies, waits for them, and re-layouts, turned(): x.transpose(2, 1, 0).reshape(c_count * ROWS, depth)  15.4 us
    ppermute x1, waiting for transfers between devices, laddered(): near = [turned(lax.ppermute(first, 'dev', shuffled(n_dev, 1)))]  15 us
    unnamed x29, local copies, waits for them, and re-layouts  12.6 us
  transfers between devices with their start and end apart: 27, of which 11 were waited for; matrix products, arithmetic and copies ran while one was open for 7% of the time, Pallas kernels for 22%

profile of v5, /device:TPU:0, one launch (start us, length us, event | category | flops | bytes accessed | tf_op | source)
XLA Modules:
  0.0 364.0 jit_solution(4872520959835550603)
XLA Ops:
  0.0 3.3 copy.18
  3.3 3.0 collective-permute-start.4
  12.6 15.0 %collective-permute-done = bf16[384,8,128]{2,1,0:T(8,128)(2,1)} collective-permute-done((bf16[384,8,128]{2,1,0:T(8,128)(2,1)}, bf16[384,8,128]{2,1,0:T(8,128)(2,1)}, u32[]{:S(2)}, u32[]{:S(2)}) %collective-permute-start) | collective-permute-done | bytes 786464 | tf_op jit(solution)/shard_map/ppermute | solution.py:167
  32.5 42.0 %collective-permute-done.4.b2 = bf16[32,384,128]{2,1,0:T(8,128)(2,1)} collective-permute-done((bf16[32,384,128]{2,1,0:T(8,128)(2,1)S(1)}, bf16[32,384,128]{2,1,0:T(8,128)(2,1)}, u32[]{:S(2)}, u32[]{:S(2)}) %collective-permute-start.4) | collective-permute-done | bytes 3145760 | tf_op jit(solution)/shard_map/ppermute | solution.py:169
  80.0 3.5 collective-permute-start.10
  86.1 16.0 %collective-permute-done.10 = bf16[1024,384]{1,0:T(8,128)(2,1)} collective-permute-done((bf16[1024,384]{1,0:T(8,128)(2,1)}, bf16[1024,384]{1,0:T(8,128)(2,1)}, u32[]{:S(2)}, u32[]{:S(2)}) %collective-permute-start.10) | collective-permute-done | bytes 786464 | tf_op jit(solution)/shard_map/ppermute | solution.py:168
  104.7 13.8 %collective-permute-done.6 = bf16[1024,384]{1,0:T(8,128)(2,1)S(1)} collective-permute-done((bf16[1024,384]{1,0:T(8,128)(2,1)}, bf16[1024,384]{1,0:T(8,128)(2,1)S(1)}, u32[]{:S(2)}, u32[]{:S(2)}) %collective-permute-start.6) | collective-permute-done | bytes 786464 | tf_op jit(solution)/shard_map/ppermute | solution.py:168
  126.9 2.7 copy.15
  129.7 54.0 %collective-permute-start.15 = (bf16[1024,384]{1,0:T(8,128)(2,1)}, bf16[1024,384]{1,0:T(8,128)(2,1)}, u32[]{:S(2)}, u32[]{:S(2)}) collective-permute-start(bf16[1024,384]{1,0:T(8,128)(2,1)} %bitcast.49), channel_id=1, source_target_pairs={{0,4},{4,0},{8,12},{12,8},{1,5},{5,1},{9,13},{13,9},{2,6},{6,2},{1... | collective-permute-start | bytes 2359304 | tf_op jit(solution)/shard_map/ppermute | solution.py:168
  189.6 4.9 %shard_map.37 = (bf16[32,1536,128]{2,1,0:T(8,128)(2,1)S(1)}, f32[8,128]{1,0:T(8,128)}) custom-call(bf16[32,384,128]{2,1,0:T(8,128)(2,1)S(1)} %bitcast.44, bf16[32,384,128]{2,1,0:T(8,128)(2,1)} %collective-permute-done.3.b1, bf16[32,384,128]{2,1,0:T(8,128)(2,1)} %collective-permute-done.4.b2, bf16[32,384,128]{2,1,0:T(8,128)(2,1)} %collective-permute-done.5.b3), custom_call_target="tpu_custom_call" | custom-call | tf_op jit(solution)/shard_map/pallas_call | solution.py:92
  194.5 3.4 copy-done
  197.9 19.2 %shard_map.38 = f32[256,256]{1,0:T(8,128)S(1)} custom-call(s32[5]{0:T(128)S(1)} %stack.27.where, bf16[2048,384]{1,0:T(8,128)(2,1)} %constant_dynamic-update-slice_fusion.held, bf16[2048,384]{1,0:T(8,128)(2,1)} %collective-permute-done.1.far, bf16[2048,384]{1,0:T(8,128)(2,1)} %collective-permute-done.2.end, ...), custom_call_target="tpu_custom_call" | custom-call | flops 15032385536 | bytes 24117248 | tf_op jit(solution)/shard_map/pallas_call | solution.py:115
  220.9 47.8 %collective-permute-done.8.end = bf16[2048,384]{1,0:T(8,128)(2,1)S(1)} collective-permute-done((bf16[2048,384]{1,0:T(8,128)(2,1)}, bf16[2048,384]{1,0:T(8,128)(2,1)S(1)}, u32[]{:S(2)}, u32[]{:S(2)}) %collective-permute-start.8) | collective-permute-done | bytes 1572896 | tf_op jit(solution)/shard_map/ppermute | solution.py:188
  269.4 18.6 %shard_map.39 = f32[256,256]{1,0:T(8,128)S(1)} custom-call(s32[5]{0:T(128)S(1)} %stack.27.where, bf16[2048,384]{1,0:T(8,128)(2,1)} %constant_dynamic-update-slice_fusion.2.held, bf16[2048,384]{1,0:T(8,128)(2,1)} %collective-permute-done.7.far, bf16[2048,384]{1,0:T(8,128)(2,1)S(1)} %collective-permute-done.8.end, ...), custom_call_target="tpu_custom_call" | custom-call | flops 15032385536 | bytes 24117248 | tf_op jit(solution)/shard_map/pallas_call | solution.py:115
  288.2 10.9 %shard_map.40.r_ref = f32[256,256]{1,0:T(8,128)S(1)} custom-call(s32[5]{0:T(128)S(1)} %stack.27.where, bf16[1024,384]{1,0:T(8,128)(2,1)S(1)} %copy-done.4, bf16[1024,384]{1,0:T(8,128)(2,1)S(1)} %copy-done.6, bf16[1024,384]{1,0:T(8,128)(2,1)} %collective-permute-done.14.end, bf16[32,1536,128]{2,1,0:T(8,128)(2,1)S(1)} %get-tuple-element.18.b_ref, ...), custom_call_target="tpu_custom_call" | custom-call | flops 7516192768 | bytes 18350080 | tf_op jit(solution)/shard_map/pallas_call | solution.py:115
  300.4 10.8 %shard_map.41 = f32[256,256]{1,0:T(8,128)S(1)} custom-call(s32[5]{0:T(128)S(1)} %stack.27.where, bf16[1024,384]{1,0:T(8,128)(2,1)} %pad_maximum_fusion.held, bf16[1024,384]{1,0:T(8,128)(2,1)} %collective-permute-done.11.far, bf16[1024,384]{1,0:T(8,128)(2,1)S(1)} %collective-permute-done.12.end, bf16[32,1536,128]{2,1,0:T(8,128)(2,1)S(1)} %get-tuple-element.18.b_ref, ...), custom_call_target="tpu_custom_call" | custom-call | flops 7516192768 | bytes 18350080 | tf_op jit(solution)/shard_map/pallas_call | solution.py:115
  313.9 3.0 collective-permute-done.21.end
  316.9 8.2 %shard_map.42.r_ref = f32[256,256]{1,0:T(8,128)S(1)} custom-call(s32[5]{0:T(128)S(1)} %stack.27.where, bf16[768,384]{1,0:T(8,128)(2,1)S(1)} %pad_maximum_fusion.3.held, bf16[768,384]{1,0:T(8,128)(2,1)S(1)} %collective-permute-done.20.far, bf16[768,384]{1,0:T(8,128)(2,1)S(1)} %collective-permute-done.21.end, ...), custom_call_target="tpu_custom_call" | custom-call | flops 5637144576 | bytes 16908288 | tf_op jit(solution)/shard_map/pallas_call | solution.py:115
  325.1 4.5 %collective-permute-done.19.end = bf16[768,384]{1,0:T(8,128)(2,1)S(1)} collective-permute-done((bf16[768,384]{1,0:T(8,128)(2,1)S(1)}, bf16[768,384]{1,0:T(8,128)(2,1)S(1)}, u32[]{:S(2)}, u32[]{:S(2)}) %collective-permute-start.19) | collective-permute-done | bytes 589856 | tf_op jit(solution)/shard_map/ppermute | solution.py:188
  329.6 8.2 %shard_map.43.r_ref = f32[256,256]{1,0:T(8,128)S(1)} custom-call(s32[5]{0:T(128)S(1)} %stack.27.where, bf16[768,384]{1,0:T(8,128)(2,1)S(1)} %pad_maximum_fusion.2.held, bf16[768,384]{1,0:T(8,128)(2,1)S(1)} %collective-permute-done.18.far, bf16[768,384]{1,0:T(8,128)(2,1)S(1)} %collective-permute-done.19.end, ...), custom_call_target="tpu_custom_call" | custom-call | flops 5637144576 | bytes 16908288 | tf_op jit(solution)/shard_map/pallas_call | solution.py:115
  337.8 6.2 %shard_map.44 = f32[256,256]{1,0:T(8,128)S(1)} custom-call(s32[5]{0:T(128)S(1)} %stack.27.where, bf16[512,384]{1,0:T(8,128)(2,1)S(1)} %pad_maximum_fusion.4.held, bf16[512,384]{1,0:T(8,128)(2,1)S(1)} %collective-permute-done.16.far, bf16[512,384]{1,0:T(8,128)(2,1)S(1)} %collective-permute-done.17.end, bf16[32,1536,128]{2,1,0:T(8,128)(2,1)S(1)} %get-tuple-element.18.b_ref, ...), custom_call_target="tpu_custom_call" | custom-call | flops 3758096384 | bytes 15466496 | tf_op jit(solution)/shard_map/pallas_call | solution.py:115
  347.2 6.8 %collective-permute-done.23 = f32[256,256]{1,0:T(8,128)S(1)} collective-permute-done((f32[256,256]{1,0:T(8,128)S(1)}, f32[256,256]{1,0:T(8,128)S(1)}, u32[]{:S(2)}, u32[]{:S(2)}) %collective-permute-start.23) | collective-permute-done | bytes 262176 | tf_op jit(solution)/shard_map/ppermute | solution.py:206
  354.2 3.0 collective-permute-start.25
  358.6 3.1 collective-permute-done.25
  (95 shorter events, 51.5 us)
Async XLA Ops:
  3.3 71.2 %collective-permute-start.4 = (bf16[32,384,128]{2,1,0:T(8,128)(2,1)S(1)}, bf16[32,384,128]{2,1,0:T(8,128)(2,1)}, u32[]{:S(2)}, u32[]{:S(2)}) collective-permute-start(bf16[32,384,128]{2,1,0:T(8,128)(2,1)S(1)} %bitcast.42), channel_id=1, source_target_pairs={{0,2},{1,3},{2,0},{3,1},{4,6},{5,7},{6,4},{7,5},{8,10},{9,11},{10,... | collective-permute-start | bytes 9437192 | tf_op jit(solution)/shard_map/ppermute | solution.py:169
  8.3 19.3 %collective-permute-start = (bf16[384,8,128]{2,1,0:T(8,128)(2,1)}, bf16[384,8,128]{2,1,0:T(8,128)(2,1)}, u32[]{:S(2)}, u32[]{:S(2)}) collective-permute-start(bf16[384,8,128]{2,1,0:T(8,128)(2,1)} %get-tuple-element.31), channel_id=1, source_target_pairs={{0,4},{4,0},{8,12},{12,8},{1,5},{5,1},{9,13},{13,9},{2,6},{6,2},{1... | collective-permute-start | bytes 2359304 | tf_op jit(solution)/shard_map/ppermute | solution.py:167
  9.9 175.2 %collective-permute-start.3 = (bf16[32,384,128]{2,1,0:T(8,128)(2,1)S(1)}, bf16[32,384,128]{2,1,0:T(8,128)(2,1)}, u32[]{:S(2)}, u32[]{:S(2)}) collective-permute-start(bf16[32,384,128]{2,1,0:T(8,128)(2,1)S(1)} %bitcast.43), channel_id=1, source_target_pairs={{0,1},{1,0},{2,3},{3,2},{4,5},{5,4},{6,7},{7,6},{8,9},{9,8},{10,11... | collective-permute-start | bytes 9437192 | tf_op jit(solution)/shard_map/ppermute | solution.py:170
  74.5 111.8 %collective-permute-start.5 = (bf16[32,384,128]{2,1,0:T(8,128)(2,1)}, bf16[32,384,128]{2,1,0:T(8,128)(2,1)}, u32[]{:S(2)}, u32[]{:S(2)}) collective-permute-start(bf16[32,384,128]{2,1,0:T(8,128)(2,1)} %collective-permute-done.4.b2), channel_id=1, source_target_pairs={{0,1},{1,0},{2,3},{3,2},{4,5},{5,4},{6,7},{7,6},{8,9},{9,8},{10,11... | collective-permute-start | bytes 9437192 | tf_op jit(solution)/shard_map/ppermute | solution.py:171
  75.5 46.7 %collective-permute-start.1 = (bf16[2048,384]{1,0:T(8,128)(2,1)}, bf16[2048,384]{1,0:T(8,128)(2,1)}, u32[]{:S(2)}, u32[]{:S(2)}) collective-permute-start(bf16[2048,384]{1,0:T(8,128)(2,1)} %constant_dynamic-update-slice_fusion.held), channel_id=1, source_target_pairs={{4,8},{8,4},{5,9},{9,5},{6,10},{10,6},{7,11},{11,7},{20,24},{24,20... | collective-permute-start | bytes 4718600 | tf_op jit(solution)/shard_map/ppermute | solution.py:187
  80.0 22.2 %collective-permute-start.10 = (bf16[1024,384]{1,0:T(8,128)(2,1)}, bf16[1024,384]{1,0:T(8,128)(2,1)}, u32[]{:S(2)}, u32[]{:S(2)}) collective-permute-start(bf16[1024,384]{1,0:T(8,128)(2,1)} %bitcast.52), channel_id=1, source_target_pairs={{0,4},{4,0},{8,12},{12,8},{1,5},{5,1},{9,13},{13,9},{2,6},{6,2},{1... | collective-permute-start | bytes 2359304 | tf_op jit(solution)/shard_map/ppermute | solution.py:168
  86.1 32.3 %collective-permute-start.6 = (bf16[1024,384]{1,0:T(8,128)(2,1)}, bf16[1024,384]{1,0:T(8,128)(2,1)S(1)}, u32[]{:S(2)}, u32[]{:S(2)}) collective-permute-start(bf16[1024,384]{1,0:T(8,128)(2,1)} %bitcast.45), channel_id=1, source_target_pairs={{0,4},{4,0},{8,12},{12,8},{1,5},{5,1},{9,13},{13,9},{2,6},{6,2},{1... | collective-permute-start | bytes 2359304 | tf_op jit(solution)/shard_map/ppermute | solution.py:168
  103.8 20.7 %collective-permute-start.13 = (bf16[1024,384]{1,0:T(8,128)(2,1)S(1)}, bf16[1024,384]{1,0:T(8,128)(2,1)S(1)}, u32[]{:S(2)}, u32[]{:S(2)}) collective-permute-start(bf16[1024,384]{1,0:T(8,128)(2,1)S(1)} %pad_maximum_fusion.1.held), channel_id=1, source_target_pairs={{4,8},{8,4},{5,9},{9,5},{6,10},{10,6},{7,11},{11,7},{20,24},{24,20... | collective-permute-start | bytes 2359304 | tf_op jit(solution)/shard_map/ppermute | solution.py:187
  120.4 63.4 %collective-permute-start.7 = (bf16[2048,384]{1,0:T(8,128)(2,1)}, bf16[2048,384]{1,0:T(8,128)(2,1)}, u32[]{:S(2)}, u32[]{:S(2)}) collective-permute-start(bf16[2048,384]{1,0:T(8,128)(2,1)} %constant_dynamic-update-slice_fusion.2.held), channel_id=1, source_target_pairs={{4,8},{8,4},{5,9},{9,5},{6,10},{10,6},{7,11},{11,7},{20,24},{24,20... | collective-permute-start | bytes 4718600 | tf_op jit(solution)/shard_map/ppermute | solution.py:187
  122.2 72.2 %collective-permute-start.2 = (bf16[2048,384]{1,0:T(8,128)(2,1)}, bf16[2048,384]{1,0:T(8,128)(2,1)}, u32[]{:S(2)}, u32[]{:S(2)}) collective-permute-start(bf16[2048,384]{1,0:T(8,128)(2,1)} %collective-permute-done.1.far), channel_id=1, source_target_pairs={{4,0},{8,12},{5,1},{9,13},{6,2},{10,14},{7,3},{11,15},{20,16},{24,... | collective-permute-start | bytes 4718600 | tf_op jit(solution)/shard_map/ppermute | solution.py:188
  129.7 87.3 %collective-permute-start.15 = (bf16[1024,384]{1,0:T(8,128)(2,1)}, bf16[1024,384]{1,0:T(8,128)(2,1)}, u32[]{:S(2)}, u32[]{:S(2)}) collective-permute-start(bf16[1024,384]{1,0:T(8,128)(2,1)} %bitcast.49), channel_id=1, source_target_pairs={{0,4},{4,0},{8,12},{12,8},{1,5},{5,1},{9,13},{13,9},{2,6},{6,2},{1... | collective-permute-start | bytes 2359304 | tf_op jit(solution)/shard_map/ppermute | solution.py:168
  183.8 104.3 %collective-permute-start.14 = (bf16[1024,384]{1,0:T(8,128)(2,1)}, bf16[1024,384]{1,0:T(8,128)(2,1)}, u32[]{:S(2)}, u32[]{:S(2)}) collective-permute-start(bf16[1024,384]{1,0:T(8,128)(2,1)} %copy-done.5), channel_id=1, source_target_pairs={{4,0},{8,12},{5,1},{9,13},{6,2},{10,14},{7,3},{11,15},{20,16},{24,... | collective-permute-start | bytes 2359304 | tf_op jit(solution)/shard_map/ppermute | solution.py:188
  185.1 115.3 %collective-permute-start.12 = (bf16[1024,384]{1,0:T(8,128)(2,1)}, bf16[1024,384]{1,0:T(8,128)(2,1)S(1)}, u32[]{:S(2)}, u32[]{:S(2)}) collective-permute-start(bf16[1024,384]{1,0:T(8,128)(2,1)} %collective-permute-done.11.far), channel_id=1, source_target_pairs={{4,0},{8,12},{5,1},{9,13},{6,2},{10,14},{7,3},{11,15},{20,16},{24,... | collective-permute-start | bytes 2359304 | tf_op jit(solution)/shard_map/ppermute | solution.py:188
  186.4 82.4 %collective-permute-start.8 = (bf16[2048,384]{1,0:T(8,128)(2,1)}, bf16[2048,384]{1,0:T(8,128)(2,1)S(1)}, u32[]{:S(2)}, u32[]{:S(2)}) collective-permute-start(bf16[2048,384]{1,0:T(8,128)(2,1)} %collective-permute-done.7.far), channel_id=1, source_target_pairs={{4,0},{8,12},{5,1},{9,13},{6,2},{10,14},{7,3},{11,15},{20,16},{24,... | collective-permute-start | bytes 4718600 | tf_op jit(solution)/shard_map/ppermute | solution.py:188
  219.3 79.8 %collective-permute-start.20 = (bf16[768,384]{1,0:T(8,128)(2,1)S(1)}, bf16[768,384]{1,0:T(8,128)(2,1)S(1)}, u32[]{:S(2)}, u32[]{:S(2)}) collective-permute-start(bf16[768,384]{1,0:T(8,128)(2,1)S(1)} %pad_maximum_fusion.3.held), channel_id=1, source_target_pairs={{4,8},{8,4},{5,9},{9,5},{6,10},{10,6},{7,11},{11,7},{20,24},{24,20... | collective-permute-start | bytes 1769480 | tf_op jit(solution)/shard_map/ppermute | solution.py:187
  220.1 91.1 %collective-permute-start.18 = (bf16[768,384]{1,0:T(8,128)(2,1)S(1)}, bf16[768,384]{1,0:T(8,128)(2,1)S(1)}, u32[]{:S(2)}, u32[]{:S(2)}) collective-permute-start(bf16[768,384]{1,0:T(8,128)(2,1)S(1)} %pad_maximum_fusion.2.held), channel_id=1, source_target_pairs={{4,8},{8,4},{5,9},{9,5},{6,10},{10,6},{7,11},{11,7},{20,24},{24,20... | collective-permute-start | bytes 1769480 | tf_op jit(solution)/shard_map/ppermute | solution.py:187
  268.7 43.9 %collective-permute-start.16 = (bf16[512,384]{1,0:T(8,128)(2,1)S(1)}, bf16[512,384]{1,0:T(8,128)(2,1)S(1)}, u32[]{:S(2)}, u32[]{:S(2)}) collective-permute-start(bf16[512,384]{1,0:T(8,128)(2,1)S(1)} %pad_maximum_fusion.4.held), channel_id=1, source_target_pairs={{4,8},{8,4},{5,9},{9,5},{6,10},{10,6},{7,11},{11,7},{20,24},{24,20... | collective-permute-start | bytes 1179656 | tf_op jit(solution)/shard_map/ppermute | solution.py:187
  288.1 24.4 %collective-permute-start.9 = (f32[256,256]{1,0:T(8,128)S(1)}, f32[256,256]{1,0:T(8,128)S(1)}, u32[]{:S(2)}, u32[]{:S(2)}) collective-permute-start(f32[256,256]{1,0:T(8,128)S(1)} %broadcast_select_fusion.1), channel_id=1, source_target_pairs={{0,1},{1,0},{2,3},{3,2},{4,5},{5,4},{6,7},{7,6},{8,9},{9,8},{10,11... | collective-permute-start | bytes 786440 | tf_op jit(solution)/shard_map/ppermute | solution.py:178
  299.1 17.8 %collective-permute-start.21 = (bf16[768,384]{1,0:T(8,128)(2,1)S(1)}, bf16[768,384]{1,0:T(8,128)(2,1)S(1)}, u32[]{:S(2)}, u32[]{:S(2)}) collective-permute-start(bf16[768,384]{1,0:T(8,128)(2,1)S(1)} %collective-permute-done.20.far), channel_id=1, source_target_pairs={{4,0},{8,12},{5,1},{9,13},{6,2},{10,14},{7,3},{11,15},{20,16},{24,... | collective-permute-start | bytes 1769480 | tf_op jit(solution)/shard_map/ppermute | solution.py:188
  311.2 18.4 %collective-permute-start.19 = (bf16[768,384]{1,0:T(8,128)(2,1)S(1)}, bf16[768,384]{1,0:T(8,128)(2,1)S(1)}, u32[]{:S(2)}, u32[]{:S(2)}) collective-permute-start(bf16[768,384]{1,0:T(8,128)(2,1)S(1)} %collective-permute-done.18.far), channel_id=1, source_target_pairs={{4,0},{8,12},{5,1},{9,13},{6,2},{10,14},{7,3},{11,15},{20,16},{24,... | collective-permute-start | bytes 1769480 | tf_op jit(solution)/shard_map/ppermute | solution.py:188
  312.6 25.2 %collective-permute-start.17 = (bf16[512,384]{1,0:T(8,128)(2,1)S(1)}, bf16[512,384]{1,0:T(8,128)(2,1)S(1)}, u32[]{:S(2)}, u32[]{:S(2)}) collective-permute-start(bf16[512,384]{1,0:T(8,128)(2,1)S(1)} %collective-permute-done.16.far), channel_id=1, source_target_pairs={{4,0},{8,12},{5,1},{9,13},{6,2},{10,14},{7,3},{11,15},{20,16},{24,... | collective-permute-start | bytes 1179656 | tf_op jit(solution)/shard_map/ppermute | solution.py:188
  345.7 8.4 %collective-permute-start.23 = (f32[256,256]{1,0:T(8,128)S(1)}, f32[256,256]{1,0:T(8,128)S(1)}, u32[]{:S(2)}, u32[]{:S(2)}) collective-permute-start(f32[256,256]{1,0:T(8,128)S(1)} %get-tuple-element.27), channel_id=1, source_target_pairs={{0,2},{1,3},{2,0},{3,1},{4,6},{5,7},{6,4},{7,5},{8,10},{9,11},{10,... | collective-permute-start | bytes 786440 | tf_op jit(solution)/shard_map/ppermute | solution.py:206
  354.2 7.5 %collective-permute-start.25 = (f32[64,256]{1,0:T(8,128)S(1)}, f32[64,256]{1,0:T(8,128)S(1)}, u32[]{:S(2)}, u32[]{:S(2)}) collective-permute-start(f32[64,256]{1,0:T(8,128)S(1)} %get-tuple-element.43), channel_id=1, source_target_pairs={{0,8},{4,12},{8,0},{12,4},{1,9},{5,13},{9,1},{13,5},{2,10},{6,14},... | collective-permute-start | bytes 196616 | tf_op jit(solution)/shard_map/ppermute | solution.py:211
  357.3 6.1 %collective-permute-start.26 = (f32[64,256]{1,0:T(8,128)S(1)}, f32[64,256]{1,0:T(8,128)S(1)}, u32[]{:S(2)}, u32[]{:S(2)}) collective-permute-start(f32[64,256]{1,0:T(8,128)S(1)} %get-tuple-element.42), channel_id=1, source_target_pairs={{0,12},{4,8},{8,4},{12,0},{1,13},{5,9},{9,5},{13,1},{2,14},{6,10},... | collective-permute-start | bytes 196616 | tf_op jit(solution)/shard_map/ppermute | solution.py:211
  (16 other events, 410.4 us)

commit v6 on v5

--- a/solution.py
+++ b/solution.py
@@ -10,7 +10,7 @@
 
 F32 = jnp.float32
 ROWS = 8
-WIDE = 4
+WIDE = 8
 LIMIT = 24 * 2**20
 
 
@@ -155,8 +155,10 @@
     cuts = [(0, 8), (0, 8), (0, 4, 8), (0, 3, 6, 8)]
     spans = [[(p * eighth, q * eighth) for p, q in zip(cut, cut[1:])] for cut in cuts]
 
+    turns = (0, 2, 1, 3)
+
     def raw(g):
-        return factor_ac[:, g * ROWS:(g + 1) * ROWS]
+        return factor_ac[:, turns[g] * ROWS:(turns[g] + 1) * ROWS]
 
     def turned(x):
         return lax.optimization_barrier(x.transpose(2, 1, 0).reshape(c_count * ROWS, depth))
@@ -173,9 +175,14 @@
 
     core, chip = col % 2, col // 2
 
-    def paired(even, odd):
-        keep, give = jnp.where(core == 0, even, odd), jnp.where(core == 0, odd, even)
-        return keep + lax.ppermute(give, "col", shuffled(n_col, 1))
+    def joined(keeper, pair):
+        away = [(i, i ^ 1) for i in range(n_col) if i % 2 != keeper]
+        across_chips = [(i, i ^ 2) for i in range(n_col) if i % 2 == keeper]
+        both = jnp.stack(pair)
+        both = both + lax.ppermute(both, "col", away)
+        give = lax.dynamic_index_in_dim(both, 1 - chip, 0, keepdims=False)
+        keep = lax.dynamic_index_in_dim(both, chip, 0, keepdims=False)
+        return keep + lax.ppermute(give, "col", across_chips)
 
     totals = [jnp.zeros((b_count * ROWS, pairs), F32)] * groups
     ready = []
@@ -199,14 +206,12 @@
     send(3, work(0))
     for g in range(1, groups):
         work(g)
-    lower = paired(totals[0], totals[1])
-    even, odd, _ = lax.optimization_barrier((totals[2], totals[3], lower))
-    upper = paired(even, odd)
-    keep, give = jnp.where(chip == 0, lower, upper), jnp.where(chip == 0, upper, lower)
-    mine = keep + lax.ppermute(give, "col", shuffled(n_col, 2))
+    lower = joined(0, totals[:2])
+    third, fourth, lower = lax.optimization_barrier((totals[2], totals[3], lower))
+    mine = jnp.where(core == 0, lower, joined(1, [third, fourth]))
     mine = mine.reshape(n_dev, b_count // n_dev * ROWS, pairs)
     out = lax.dynamic_index_in_dim(mine, dev, 0, keepdims=False)
-    for mask in range(1, n_dev):
+    for mask in (3, 2, 1):
         give = lax.dynamic_index_in_dim(mine, dev ^ mask, 0, keepdims=False)
         out = out + lax.ppermute(give, "dev", shuffled(n_dev, mask))
     return out.reshape(b_count // n_dev, ROWS, pairs).transpose(1, 0, 2)

time: 365 us -> 372 us (1.019); the launches traced: 364 us -> 366 us
  starting transfers between devices: 85.4 us -> 90.5 us
  Pallas kernels: 86.9 us -> 82.4 us
    ppermute x7, waiting for transfers between devices: 55.4 us -> 64.2 us  [send(): ready.append((g, i, c0, held, far, lax.ppermute(far, 'dev', TO_END)))]
    ppermute x3 -> x4, waiting for transfers between devices: 8.36 us -> 1.49 us  [the longest x2 1.49 us: joined(): both = both + lax.ppermute(both, 'col', away)]
    ppermute x3 -> x4, starting transfers between devices: 1.7 us -> 6.82 us  [the longest x2 4.21 us: joined(): return keep + lax.ppermute(give, 'col', across_chips)]
    pallas_call x7, Pallas kernels: 82 us -> 77.5 us  [block(): pl.pallas_call(functools.partial(block_kernel, first, rows, c_start), in_...]
  transfers between devices with their start and end apart: 27 -> 28, of which waited for: 11 -> 10; matrix products, arithmetic and copies ran while one was open for 7% -> 7% of each run, Pallas kernels for 22% -> 21%
where the time goes in v6:
time: 372 us; the launch traced here: 366 us
  waiting for transfers between devices  157 us (42%)
  starting transfers between devices  90.5 us (24%)
  Pallas kernels  82.4 us (22%)
  local copies, waits for them, and re-layouts  34.5 us (9%)
    pallas_call x7, Pallas kernels, block(): pl.pallas_call(functools.partial(block_kernel, first, rows, c_start), in_...  77.5 us
    ppermute x7, waiting for transfers between devices, send(): ready.append((g, i, c0, held, far, lax.ppermute(far, 'dev', TO_END)))  64.2 us
    ppermute x3, starting transfers between devices, laddered(): lax.ppermute(own[g], 'dev', shuffled(n_dev, 1))  57.5 us
    ppermute x1, waiting for transfers between devices, laddered(): across = lax.ppermute(turned_bd, 'col', shuffled(n_col, 2))  42 us
    ppermute x3, waiting for transfers between devices, laddered(): lax.ppermute(own[g], 'dev', shuffled(n_dev, 1))  29.9 us
    transpose x6, local copies, waits for them, and re-layouts, turned(): x.transpose(2, 1, 0).reshape(c_count * ROWS, depth)  15.4 us
    ppermute x1, waiting for transfers between devices, laddered(): near = [turned(lax.ppermute(first, 'dev', shuffled(n_dev, 1)))]  15 us
    unnamed x29, local copies, waits for them, and re-layouts  12.6 us
  transfers between devices with their start and end apart: 28, of which 10 were waited for; matrix products, arithmetic and copies ran while one was open for 7% of the time, Pallas kernels for 21%

profile of v6, /device:TPU:0, one launch (start us, length us, event | category | flops | bytes accessed | tf_op | source)
XLA Modules:
  0.0 366.1 jit_solution(9848991095236296507)
XLA Ops:
  0.0 3.3 copy.18
  3.3 3.0 collective-permute-start.4
  9.9 2.7 copy.13
  12.6 15.0 %collective-permute-done.9 = bf16[384,8,128]{2,1,0:T(8,128)(2,1)} collective-permute-done((bf16[384,8,128]{2,1,0:T(8,128)(2,1)}, bf16[384,8,128]{2,1,0:T(8,128)(2,1)}, u32[]{:S(2)}, u32[]{:S(2)}) %collective-permute-start.9) | collective-permute-done | bytes 786464 | tf_op jit(solution)/shard_map/ppermute | solution.py:169
  32.5 42.0 %collective-permute-done.4.b2 = bf16[32,384,128]{2,1,0:T(8,128)(2,1)} collective-permute-done((bf16[32,384,128]{2,1,0:T(8,128)(2,1)S(1)}, bf16[32,384,128]{2,1,0:T(8,128)(2,1)}, u32[]{:S(2)}, u32[]{:S(2)}) %collective-permute-start.4) | collective-permute-done | bytes 3145760 | tf_op jit(solution)/shard_map/ppermute | solution.py:171
  80.0 3.5 collective-permute-start
  86.1 16.0 %collective-permute-done = bf16[1024,384]{1,0:T(8,128)(2,1)} collective-permute-done((bf16[1024,384]{1,0:T(8,128)(2,1)}, bf16[1024,384]{1,0:T(8,128)(2,1)}, u32[]{:S(2)}, u32[]{:S(2)}) %collective-permute-start) | collective-permute-done | bytes 786464 | tf_op jit(solution)/shard_map/ppermute | solution.py:170
  104.7 13.8 %collective-permute-done.18 = bf16[1024,384]{1,0:T(8,128)(2,1)S(1)} collective-permute-done((bf16[1024,384]{1,0:T(8,128)(2,1)}, bf16[1024,384]{1,0:T(8,128)(2,1)S(1)}, u32[]{:S(2)}, u32[]{:S(2)}) %collective-permute-start.18) | collective-permute-done | bytes 786464 | tf_op jit(solution)/shard_map/ppermute | solution.py:170
  126.9 2.7 copy.12
  129.7 54.0 %collective-permute-start.8 = (bf16[1024,384]{1,0:T(8,128)(2,1)}, bf16[1024,384]{1,0:T(8,128)(2,1)}, u32[]{:S(2)}, u32[]{:S(2)}) collective-permute-start(bf16[1024,384]{1,0:T(8,128)(2,1)} %bitcast.71), channel_id=1, source_target_pairs={{0,4},{4,0},{8,12},{12,8},{1,5},{5,1},{9,13},{13,9},{2,6},{6,2},{1... | collective-permute-start | bytes 2359304 | tf_op jit(solution)/shard_map/ppermute | solution.py:170
  189.6 4.9 %shard_map.37 = (bf16[32,1536,128]{2,1,0:T(8,128)(2,1)S(1)}, f32[8,128]{1,0:T(8,128)}) custom-call(bf16[32,384,128]{2,1,0:T(8,128)(2,1)S(1)} %bitcast.58, bf16[32,384,128]{2,1,0:T(8,128)(2,1)} %collective-permute-done.3.b1, bf16[32,384,128]{2,1,0:T(8,128)(2,1)} %collective-permute-done.4.b2, bf16[32,384,128]{2,1,0:T(8,128)(2,1)} %collective-permute-done.5.b3), custom_call_target="tpu_custom_call" | custom-call | tf_op jit(solution)/shard_map/pallas_call | solution.py:92
  194.5 3.4 copy-done
  197.9 18.6 %shard_map.40 = f32[256,256]{1,0:T(8,128)S(1)} custom-call(s32[5]{0:T(128)S(1)} %stack.45.where, bf16[2048,384]{1,0:T(8,128)(2,1)} %constant_dynamic-update-slice_fusion.held, bf16[2048,384]{1,0:T(8,128)(2,1)} %collective-permute-done.10.far, bf16[2048,384]{1,0:T(8,128)(2,1)} %collective-permute-done.11.end, ...), custom_call_target="tpu_custom_call" | custom-call | flops 15032385536 | bytes 24117248 | tf_op jit(solution)/shard_map/pallas_call | solution.py:115
  220.2 48.5 %collective-permute-done.20.end = bf16[2048,384]{1,0:T(8,128)(2,1)S(1)} collective-permute-done((bf16[2048,384]{1,0:T(8,128)(2,1)}, bf16[2048,384]{1,0:T(8,128)(2,1)S(1)}, u32[]{:S(2)}, u32[]{:S(2)}) %collective-permute-start.20) | collective-permute-done | bytes 1572896 | tf_op jit(solution)/shard_map/ppermute | solution.py:195
  269.4 18.0 %shard_map.44 = f32[256,256]{1,0:T(8,128)S(1)} custom-call(s32[5]{0:T(128)S(1)} %stack.45.where, bf16[2048,384]{1,0:T(8,128)(2,1)} %constant_dynamic-update-slice_fusion.2.held, bf16[2048,384]{1,0:T(8,128)(2,1)} %collective-permute-done.19.far, bf16[2048,384]{1,0:T(8,128)(2,1)S(1)} %collective-permute-done.20.end, ...), custom_call_target="tpu_custom_call" | custom-call | flops 15032385536 | bytes 24117248 | tf_op jit(solution)/shard_map/pallas_call | solution.py:115
  288.8 10.1 %shard_map.38.r_ref = f32[256,256]{1,0:T(8,128)S(1)} custom-call(s32[5]{0:T(128)S(1)} %stack.45.where, bf16[1024,384]{1,0:T(8,128)(2,1)} %pad_maximum_fusion.1.held, bf16[1024,384]{1,0:T(8,128)(2,1)} %collective-permute-done.6.far, bf16[1024,384]{1,0:T(8,128)(2,1)S(1)} %collective-permute-done.7.end, bf16[32,1536,128]{2,1,0:T(8,128)(2,1)S(1)} %get-tuple-element.19.b_ref, ...), custom_call_target="tpu_custom_call" | custom-call | flops 7516192768 | bytes 18350080 | tf_op jit(solution)/shard_map/pallas_call | solution.py:115
  299.1 3.5 collective-permute-start.22
  303.9 10.2 %shard_map.39 = f32[256,256]{1,0:T(8,128)S(1)} custom-call(s32[5]{0:T(128)S(1)} %stack.45.where, bf16[1024,384]{1,0:T(8,128)(2,1)S(1)} %copy-done.4, bf16[1024,384]{1,0:T(8,128)(2,1)S(1)} %copy-done.6, bf16[1024,384]{1,0:T(8,128)(2,1)} %collective-permute-done.2.end, bf16[32,1536,128]{2,1,0:T(8,128)(2,1)S(1)} %get-tuple-element.19.b_ref, ...), custom_call_target="tpu_custom_call" | custom-call | flops 7516192768 | bytes 18350080 | tf_op jit(solution)/shard_map/pallas_call | solution.py:115
  316.8 3.9 %collective-permute-done.17.end = bf16[768,384]{1,0:T(8,128)(2,1)S(1)} collective-permute-done((bf16[768,384]{1,0:T(8,128)(2,1)S(1)}, bf16[768,384]{1,0:T(8,128)(2,1)S(1)}, u32[]{:S(2)}, u32[]{:S(2)}) %collective-permute-start.17) | collective-permute-done | bytes 589856 | tf_op jit(solution)/shard_map/ppermute | solution.py:195
  320.7 7.5 %shard_map.41.r_ref = f32[256,256]{1,0:T(8,128)S(1)} custom-call(s32[5]{0:T(128)S(1)} %stack.45.where, bf16[768,384]{1,0:T(8,128)(2,1)S(1)} %pad_maximum_fusion.3.held, bf16[768,384]{1,0:T(8,128)(2,1)S(1)} %collective-permute-done.16.far, bf16[768,384]{1,0:T(8,128)(2,1)S(1)} %collective-permute-done.17.end, ...), custom_call_target="tpu_custom_call" | custom-call | flops 5637144576 | bytes 16908288 | tf_op jit(solution)/shard_map/pallas_call | solution.py:115
  328.2 11.8 %collective-permute-done.15.end = bf16[768,384]{1,0:T(8,128)(2,1)S(1)} collective-permute-done((bf16[768,384]{1,0:T(8,128)(2,1)S(1)}, bf16[768,384]{1,0:T(8,128)(2,1)S(1)}, u32[]{:S(2)}, u32[]{:S(2)}) %collective-permute-start.15) | collective-permute-done | bytes 589856 | tf_op jit(solution)/shard_map/ppermute | solution.py:195
  340.0 7.7 %shard_map.42.r_ref = f32[256,256]{1,0:T(8,128)S(1)} custom-call(s32[5]{0:T(128)S(1)} %stack.45.where, bf16[768,384]{1,0:T(8,128)(2,1)S(1)} %pad_maximum_fusion.2.held, bf16[768,384]{1,0:T(8,128)(2,1)S(1)} %collective-permute-done.14.far, bf16[768,384]{1,0:T(8,128)(2,1)S(1)} %collective-permute-done.15.end, ...), custom_call_target="tpu_custom_call" | custom-call | flops 5637144576 | bytes 16908288 | tf_op jit(solution)/shard_map/pallas_call | solution.py:115
  347.7 5.5 %shard_map.43 = f32[256,256]{1,0:T(8,128)S(1)} custom-call(s32[5]{0:T(128)S(1)} %stack.45.where, bf16[512,384]{1,0:T(8,128)(2,1)S(1)} %pad_maximum_fusion.6.held, bf16[512,384]{1,0:T(8,128)(2,1)S(1)} %collective-permute-done.12.far, bf16[512,384]{1,0:T(8,128)(2,1)S(1)} %collective-permute-done.13.end, bf16[32,1536,128]{2,1,0:T(8,128)(2,1)S(1)} %get-tuple-element.19.b_ref, ...), custom_call_target="tpu_custom_call" | custom-call | flops 3758096384 | bytes 15466496 | tf_op jit(solution)/shard_map/pallas_call | solution.py:115
  362.3 3.1 collective-permute-done.25
  (100 shorter events, 52.8 us)
Async XLA Ops:
  3.3 71.2 %collective-permute-start.4 = (bf16[32,384,128]{2,1,0:T(8,128)(2,1)S(1)}, bf16[32,384,128]{2,1,0:T(8,128)(2,1)}, u32[]{:S(2)}, u32[]{:S(2)}) collective-permute-start(bf16[32,384,128]{2,1,0:T(8,128)(2,1)S(1)} %bitcast.56), channel_id=1, source_target_pairs={{0,2},{1,3},{2,0},{3,1},{4,6},{5,7},{6,4},{7,5},{8,10},{9,11},{10,... | collective-permute-start | bytes 9437192 | tf_op jit(solution)/shard_map/ppermute | solution.py:171
  8.3 19.3 %collective-permute-start.9 = (bf16[384,8,128]{2,1,0:T(8,128)(2,1)}, bf16[384,8,128]{2,1,0:T(8,128)(2,1)}, u32[]{:S(2)}, u32[]{:S(2)}) collective-permute-start(bf16[384,8,128]{2,1,0:T(8,128)(2,1)} %get-tuple-element.32), channel_id=1, source_target_pairs={{0,4},{4,0},{8,12},{12,8},{1,5},{5,1},{9,13},{13,9},{2,6},{6,2},{1... | collective-permute-start | bytes 2359304 | tf_op jit(solution)/shard_map/ppermute | solution.py:169
  9.9 175.2 %collective-permute-start.3 = (bf16[32,384,128]{2,1,0:T(8,128)(2,1)S(1)}, bf16[32,384,128]{2,1,0:T(8,128)(2,1)}, u32[]{:S(2)}, u32[]{:S(2)}) collective-permute-start(bf16[32,384,128]{2,1,0:T(8,128)(2,1)S(1)} %bitcast.57), channel_id=1, source_target_pairs={{0,1},{1,0},{2,3},{3,2},{4,5},{5,4},{6,7},{7,6},{8,9},{9,8},{10,11... | collective-permute-start | bytes 9437192 | tf_op jit(solution)/shard_map/ppermute | solution.py:172
  74.5 111.8 %collective-permute-start.5 = (bf16[32,384,128]{2,1,0:T(8,128)(2,1)}, bf16[32,384,128]{2,1,0:T(8,128)(2,1)}, u32[]{:S(2)}, u32[]{:S(2)}) collective-permute-start(bf16[32,384,128]{2,1,0:T(8,128)(2,1)} %collective-permute-done.4.b2), channel_id=1, source_target_pairs={{0,1},{1,0},{2,3},{3,2},{4,5},{5,4},{6,7},{7,6},{8,9},{9,8},{10,11... | collective-permute-start | bytes 9437192 | tf_op jit(solution)/shard_map/ppermute | solution.py:173
  75.5 46.7 %collective-permute-start.10 = (bf16[2048,384]{1,0:T(8,128)(2,1)}, bf16[2048,384]{1,0:T(8,128)(2,1)}, u32[]{:S(2)}, u32[]{:S(2)}) collective-permute-start(bf16[2048,384]{1,0:T(8,128)(2,1)} %constant_dynamic-update-slice_fusion.held), channel_id=1, source_target_pairs={{4,8},{8,4},{5,9},{9,5},{6,10},{10,6},{7,11},{11,7},{20,24},{24,20... | collective-permute-start | bytes 4718600 | tf_op jit(solution)/shard_map/ppermute | solution.py:194
  80.0 22.2 %collective-permute-start = (bf16[1024,384]{1,0:T(8,128)(2,1)}, bf16[1024,384]{1,0:T(8,128)(2,1)}, u32[]{:S(2)}, u32[]{:S(2)}) collective-permute-start(bf16[1024,384]{1,0:T(8,128)(2,1)} %bitcast.74), channel_id=1, source_target_pairs={{0,4},{4,0},{8,12},{12,8},{1,5},{5,1},{9,13},{13,9},{2,6},{6,2},{1... | collective-permute-start | bytes 2359304 | tf_op jit(solution)/shard_map/ppermute | solution.py:170
  86.1 32.3 %collective-permute-start.18 = (bf16[1024,384]{1,0:T(8,128)(2,1)}, bf16[1024,384]{1,0:T(8,128)(2,1)S(1)}, u32[]{:S(2)}, u32[]{:S(2)}) collective-permute-start(bf16[1024,384]{1,0:T(8,128)(2,1)} %bitcast.67), channel_id=1, source_target_pairs={{0,4},{4,0},{8,12},{12,8},{1,5},{5,1},{9,13},{13,9},{2,6},{6,2},{1... | collective-permute-start | bytes 2359304 | tf_op jit(solution)/shard_map/ppermute | solution.py:170
  103.8 20.7 %collective-permute-start.1 = (bf16[1024,384]{1,0:T(8,128)(2,1)S(1)}, bf16[1024,384]{1,0:T(8,128)(2,1)S(1)}, u32[]{:S(2)}, u32[]{:S(2)}) collective-permute-start(bf16[1024,384]{1,0:T(8,128)(2,1)S(1)} %pad_maximum_fusion.held), channel_id=1, source_target_pairs={{4,8},{8,4},{5,9},{9,5},{6,10},{10,6},{7,11},{11,7},{20,24},{24,20... | collective-permute-start | bytes 2359304 | tf_op jit(solution)/shard_map/ppermute | solution.py:194
  120.4 63.4 %collective-permute-start.19 = (bf16[2048,384]{1,0:T(8,128)(2,1)}, bf16[2048,384]{1,0:T(8,128)(2,1)}, u32[]{:S(2)}, u32[]{:S(2)}) collective-permute-start(bf16[2048,384]{1,0:T(8,128)(2,1)} %constant_dynamic-update-slice_fusion.2.held), channel_id=1, source_target_pairs={{4,8},{8,4},{5,9},{9,5},{6,10},{10,6},{7,11},{11,7},{20,24},{24,20... | collective-permute-start | bytes 4718600 | tf_op jit(solution)/shard_map/ppermute | solution.py:194
  122.2 72.2 %collective-permute-start.11 = (bf16[2048,384]{1,0:T(8,128)(2,1)}, bf16[2048,384]{1,0:T(8,128)(2,1)}, u32[]{:S(2)}, u32[]{:S(2)}) collective-permute-start(bf16[2048,384]{1,0:T(8,128)(2,1)} %collective-permute-done.10.far), channel_id=1, source_target_pairs={{4,0},{8,12},{5,1},{9,13},{6,2},{10,14},{7,3},{11,15},{20,16},{24,... | collective-permute-start | bytes 4718600 | tf_op jit(solution)/shard_map/ppermute | solution.py:195
  129.7 86.7 %collective-permute-start.8 = (bf16[1024,384]{1,0:T(8,128)(2,1)}, bf16[1024,384]{1,0:T(8,128)(2,1)}, u32[]{:S(2)}, u32[]{:S(2)}) collective-permute-start(bf16[1024,384]{1,0:T(8,128)(2,1)} %bitcast.71), channel_id=1, source_target_pairs={{0,4},{4,0},{8,12},{12,8},{1,5},{5,1},{9,13},{13,9},{2,6},{6,2},{1... | collective-permute-start | bytes 2359304 | tf_op jit(solution)/shard_map/ppermute | solution.py:170
  183.8 120.2 %collective-permute-start.2 = (bf16[1024,384]{1,0:T(8,128)(2,1)}, bf16[1024,384]{1,0:T(8,128)(2,1)}, u32[]{:S(2)}, u32[]{:S(2)}) collective-permute-start(bf16[1024,384]{1,0:T(8,128)(2,1)} %copy-done.5), channel_id=1, source_target_pairs={{4,0},{8,12},{5,1},{9,13},{6,2},{10,14},{7,3},{11,15},{20,16},{24,... | collective-permute-start | bytes 2359304 | tf_op jit(solution)/shard_map/ppermute | solution.py:195
  185.1 102.4 %collective-permute-start.7 = (bf16[1024,384]{1,0:T(8,128)(2,1)}, bf16[1024,384]{1,0:T(8,128)(2,1)S(1)}, u32[]{:S(2)}, u32[]{:S(2)}) collective-permute-start(bf16[1024,384]{1,0:T(8,128)(2,1)} %collective-permute-done.6.far), channel_id=1, source_target_pairs={{4,0},{8,12},{5,1},{9,13},{6,2},{10,14},{7,3},{11,15},{20,16},{24,... | collective-permute-start | bytes 2359304 | tf_op jit(solution)/shard_map/ppermute | solution.py:195
  186.4 82.4 %collective-permute-start.20 = (bf16[2048,384]{1,0:T(8,128)(2,1)}, bf16[2048,384]{1,0:T(8,128)(2,1)S(1)}, u32[]{:S(2)}, u32[]{:S(2)}) collective-permute-start(bf16[2048,384]{1,0:T(8,128)(2,1)} %collective-permute-done.19.far), channel_id=1, source_target_pairs={{4,0},{8,12},{5,1},{9,13},{6,2},{10,14},{7,3},{11,15},{20,16},{24,... | collective-permute-start | bytes 4718600 | tf_op jit(solution)/shard_map/ppermute | solution.py:195
  217.5 96.7 %collective-permute-start.12 = (bf16[512,384]{1,0:T(8,128)(2,1)S(1)}, bf16[512,384]{1,0:T(8,128)(2,1)S(1)}, u32[]{:S(2)}, u32[]{:S(2)}) collective-permute-start(bf16[512,384]{1,0:T(8,128)(2,1)S(1)} %pad_maximum_fusion.6.held), channel_id=1, source_target_pairs={{4,8},{8,4},{5,9},{9,5},{6,10},{10,6},{7,11},{11,7},{20,24},{24,20... | collective-permute-start | bytes 1179656 | tf_op jit(solution)/shard_map/ppermute | solution.py:194
  219.4 96.1 %collective-permute-start.14 = (bf16[768,384]{1,0:T(8,128)(2,1)S(1)}, bf16[768,384]{1,0:T(8,128)(2,1)S(1)}, u32[]{:S(2)}, u32[]{:S(2)}) collective-permute-start(bf16[768,384]{1,0:T(8,128)(2,1)S(1)} %pad_maximum_fusion.2.held), channel_id=1, source_target_pairs={{4,8},{8,4},{5,9},{9,5},{6,10},{10,6},{7,11},{11,7},{20,24},{24,20... | collective-permute-start | bytes 1769480 | tf_op jit(solution)/shard_map/ppermute | solution.py:194
  268.7 33.9 %collective-permute-start.16 = (bf16[768,384]{1,0:T(8,128)(2,1)S(1)}, bf16[768,384]{1,0:T(8,128)(2,1)S(1)}, u32[]{:S(2)}, u32[]{:S(2)}) collective-permute-start(bf16[768,384]{1,0:T(8,128)(2,1)S(1)} %pad_maximum_fusion.3.held), channel_id=1, source_target_pairs={{4,8},{8,4},{5,9},{9,5},{6,10},{10,6},{7,11},{11,7},{20,24},{24,20... | collective-permute-start | bytes 1769480 | tf_op jit(solution)/shard_map/ppermute | solution.py:194
  287.5 11.5 %collective-permute-start.21 = (f32[2,256,256]{2,1,0:T(8,128)S(1)}, f32[2,256,256]{2,1,0:T(8,128)S(1)}, u32[]{:S(2)}, u32[]{:S(2)}) collective-permute-start(f32[2,256,256]{2,1,0:T(8,128)S(1)} %pad_maximum_fusion.4), channel_id=1, source_target_pairs={{1,0},{3,2},{5,4},{7,6},{9,8},{11,10},{13,12},{15,14},{17,16},{19,... | collective-permute-start | bytes 1572872 | tf_op jit(solution)/shard_map/ppermute | solution.py:182
  299.1 17.7 %collective-permute-start.22 = (f32[256,256]{1,0:T(8,128)S(1)}, f32[256,256]{1,0:T(8,128)S(1)}, u32[]{:S(2)}, u32[]{:S(2)}) collective-permute-start(f32[256,256]{1,0:T(8,128)S(1)} %dynamic-slice_bitcast_fusion.1), channel_id=1, source_target_pairs={{0,2},{2,0},{4,6},{6,4},{8,10},{10,8},{12,14},{14,12},{16,18},{18,... | collective-permute-start | bytes 786440 | tf_op jit(solution)/shard_map/ppermute | solution.py:185
  302.6 18.1 %collective-permute-start.17 = (bf16[768,384]{1,0:T(8,128)(2,1)S(1)}, bf16[768,384]{1,0:T(8,128)(2,1)S(1)}, u32[]{:S(2)}, u32[]{:S(2)}) collective-permute-start(bf16[768,384]{1,0:T(8,128)(2,1)S(1)} %collective-permute-done.16.far), channel_id=1, source_target_pairs={{4,0},{8,12},{5,1},{9,13},{6,2},{10,14},{7,3},{11,15},{20,16},{24,... | collective-permute-start | bytes 1769480 | tf_op jit(solution)/shard_map/ppermute | solution.py:195
  314.2 33.6 %collective-permute-start.13 = (bf16[512,384]{1,0:T(8,128)(2,1)S(1)}, bf16[512,384]{1,0:T(8,128)(2,1)S(1)}, u32[]{:S(2)}, u32[]{:S(2)}) collective-permute-start(bf16[512,384]{1,0:T(8,128)(2,1)S(1)} %collective-permute-done.12.far), channel_id=1, source_target_pairs={{4,0},{8,12},{5,1},{9,13},{6,2},{10,14},{7,3},{11,15},{20,16},{24,... | collective-permute-start | bytes 1179656 | tf_op jit(solution)/shard_map/ppermute | solution.py:195
  315.5 24.5 %collective-permute-start.15 = (bf16[768,384]{1,0:T(8,128)(2,1)S(1)}, bf16[768,384]{1,0:T(8,128)(2,1)S(1)}, u32[]{:S(2)}, u32[]{:S(2)}) collective-permute-start(bf16[768,384]{1,0:T(8,128)(2,1)S(1)} %collective-permute-done.14.far), channel_id=1, source_target_pairs={{4,0},{8,12},{5,1},{9,13},{6,2},{10,14},{7,3},{11,15},{20,16},{24,... | collective-permute-start | bytes 1769480 | tf_op jit(solution)/shard_map/ppermute | solution.py:195
  357.1 5.2 %collective-permute-start.26 = (f32[64,256]{1,0:T(8,128)S(1)}, f32[64,256]{1,0:T(8,128)S(1)}, u32[]{:S(2)}, u32[]{:S(2)}) collective-permute-start(f32[64,256]{1,0:T(8,128)S(1)} %get-tuple-element.43), channel_id=1, source_target_pairs={{0,8},{4,12},{8,0},{12,4},{1,9},{5,13},{9,1},{13,5},{2,10},{6,14},... | collective-permute-start | bytes 196616 | tf_op jit(solution)/shard_map/ppermute | solution.py:216
  359.3 6.1 %collective-permute-start.25 = (f32[64,256]{1,0:T(8,128)S(1)}, f32[64,256]{1,0:T(8,128)S(1)}, u32[]{:S(2)}, u32[]{:S(2)}) collective-permute-start(f32[64,256]{1,0:T(8,128)S(1)} %get-tuple-element.41), channel_id=1, source_target_pairs={{0,12},{4,8},{8,4},{12,0},{1,13},{5,9},{9,5},{13,1},{2,14},{6,10},... | collective-permute-start | bytes 196616 | tf_op jit(solution)/shard_map/ppermute | solution.py:216
  (17 other events, 288.0 us)

commit v7 on v6

--- a/solution.py
+++ b/solution.py
@@ -207,8 +207,14 @@
     for g in range(1, groups):
         work(g)
     lower = joined(0, totals[:2])
-    third, fourth, lower = lax.optimization_barrier((totals[2], totals[3], lower))
-    mine = jnp.where(core == 0, lower, joined(1, [third, fourth]))
+    third, lower = lax.optimization_barrier((totals[2], lower))
+    away = [(i, i ^ 1) for i in range(n_col) if i % 2 == 0]
+    third = third + lax.ppermute(third, "col", away)
+    fourth, third = lax.optimization_barrier((totals[3], third))
+    fourth = fourth + lax.ppermute(fourth, "col", away)
+    keep, give = jnp.where(chip == 0, third, fourth), jnp.where(chip == 0, fourth, third)
+    upper = keep + lax.ppermute(give, "col", [(i, i ^ 2) for i in range(n_col) if i % 2 == 1])
+    mine = jnp.where(core == 0, lower, upper)
     mine = mine.reshape(n_dev, b_count // n_dev * ROWS, pairs)
     out = lax.dynamic_index_in_dim(mine, dev, 0, keepdims=False)
     for mask in (3, 2, 1):

time: 372 us -> 352 us (0.946)
  waiting for transfers between devices: 157 us -> 128 us
  starting transfers between devices: 90.5 us -> 102 us
    ppermute x7, waiting for transfers between devices: 64.2 us -> 30.5 us  [send(): ready.append((g, i, c0, held, far, lax.ppermute(far, 'dev', TO_END)))]
    ppermute x3, starting transfers between devices: 57.5 us -> 68.7 us  [laddered(): lax.ppermute(own[g], 'dev', shuffled(n_dev, 1))]
    ppermute x3, waiting for transfers between devices: 29.9 us -> 33.6 us  [laddered(): lax.ppermute(own[g], 'dev', shuffled(n_dev, 1))]
    unnamed x29 -> x35, local copies, waits for them, and re-layouts: 12.6 us -> 13.7 us
  transfers between devices with their start and end apart: 28 -> 29, of which waited for: 10 -> 10; matrix products, arithmetic and copies ran while one was open for 7% -> 7% of each run, Pallas kernels for 21% -> 22%
where the time goes in v7:
time: 352 us; the launch traced here: 347 us
  waiting for transfers between devices  128 us (36%)
  starting transfers between devices  102 us (29%)
  Pallas kernels  81.9 us (23%)
  local copies, waits for them, and re-layouts  33.5 us (10%)
    pallas_call x7, Pallas kernels, block(): pl.pallas_call(functools.partial(block_kernel, first, rows, c_start), in_...  77 us
    ppermute x3, starting transfers between devices, laddered(): lax.ppermute(own[g], 'dev', shuffled(n_dev, 1))  68.7 us
    ppermute x1, waiting for transfers between devices, laddered(): across = lax.ppermute(turned_bd, 'col', shuffled(n_col, 2))  42.3 us
    ppermute x3, waiting for transfers between devices, laddered(): lax.ppermute(own[g], 'dev', shuffled(n_dev, 1))  33.6 us
    ppermute x7, waiting for transfers between devices, send(): ready.append((g, i, c0, held, far, lax.ppermute(far, 'dev', TO_END)))  30.5 us
    ppermute x1, waiting for transfers between devices, laddered(): near = [turned(lax.ppermute(first, 'dev', shuffled(n_dev, 1)))]  16.4 us
    transpose x6, local copies, waits for them, and re-layouts, turned(): x.transpose(2, 1, 0).reshape(c_count * ROWS, depth)  15.3 us
    unnamed x35, local copies, waits for them, and re-layouts  13.7 us
  transfers between devices with their start and end apart: 29, of which 10 were waited for; matrix products, arithmetic and copies ran while one was open for 7% of the time, Pallas kernels for 22%

profile of v7, /device:TPU:0, one launch (start us, length us, event | category | flops | bytes accessed | tf_op | source)
XLA Modules:
  0.0 346.8 jit_solution(801131433367628938)
XLA Ops:
  0.0 3.3 copy.18
  3.3 3.0 collective-permute-start.4
  12.5 17.6 %collective-permute-done.11 = bf16[1024,384]{1,0:T(8,128)(2,1)S(1)} collective-permute-done((bf16[1024,384]{1,0:T(8,128)(2,1)}, bf16[1024,384]{1,0:T(8,128)(2,1)S(1)}, u32[]{:S(2)}, u32[]{:S(2)}) %collective-permute-start.11) | collective-permute-done | bytes 786464 | tf_op jit(solution)/shard_map/ppermute | solution.py:170
  32.2 42.3 %collective-permute-done.4.b2 = bf16[32,384,128]{2,1,0:T(8,128)(2,1)} collective-permute-done((bf16[32,384,128]{2,1,0:T(8,128)(2,1)S(1)}, bf16[32,384,128]{2,1,0:T(8,128)(2,1)}, u32[]{:S(2)}, u32[]{:S(2)}) %collective-permute-start.4) | collective-permute-done | bytes 3145760 | tf_op jit(solution)/shard_map/ppermute | solution.py:171
  80.0 3.5 %collective-permute-start = (bf16[1024,384]{1,0:T(8,128)(2,1)}, bf16[1024,384]{1,0:T(8,128)(2,1)}, u32[]{:S(2)}, u32[]{:S(2)}) collective-permute-start(bf16[1024,384]{1,0:T(8,128)(2,1)} %bitcast.63), channel_id=1, source_target_pairs={{0,4},{4,0},{8,12},{12,8},{1,5},{5,1},{9,13},{13,9},{2,6},{6,2},{1... | collective-permute-start | bytes 2359304 | tf_op jit(solution)/shard_map/ppermute | solution.py:170
  83.5 2.7 copy.12
  86.2 16.0 %collective-permute-done = bf16[1024,384]{1,0:T(8,128)(2,1)} collective-permute-done((bf16[1024,384]{1,0:T(8,128)(2,1)}, bf16[1024,384]{1,0:T(8,128)(2,1)}, u32[]{:S(2)}, u32[]{:S(2)}) %collective-permute-start) | collective-permute-done | bytes 786464 | tf_op jit(solution)/shard_map/ppermute | solution.py:170
  102.2 16.4 %collective-permute-done.8 = bf16[384,8,128]{2,1,0:T(8,128)(2,1)} collective-permute-done((bf16[384,8,128]{2,1,0:T(8,128)(2,1)}, bf16[384,8,128]{2,1,0:T(8,128)(2,1)}, u32[]{:S(2)}, u32[]{:S(2)}) %collective-permute-start.8) | collective-permute-done | bytes 786464 | tf_op jit(solution)/shard_map/ppermute | solution.py:169
  118.6 2.7 copy.13
  135.6 63.6 %collective-permute-start.16 = (bf16[1024,384]{1,0:T(8,128)(2,1)}, bf16[1024,384]{1,0:T(8,128)(2,1)S(1)}, u32[]{:S(2)}, u32[]{:S(2)}) collective-permute-start(bf16[1024,384]{1,0:T(8,128)(2,1)} %bitcast.60), channel_id=1, source_target_pairs={{0,4},{4,0},{8,12},{12,8},{1,5},{5,1},{9,13},{13,9},{2,6},{6,2},{1... | collective-permute-start | bytes 2359304 | tf_op jit(solution)/shard_map/ppermute | solution.py:170
  203.8 4.9 %shard_map.37 = (bf16[32,1536,128]{2,1,0:T(8,128)(2,1)S(1)}, f32[8,128]{1,0:T(8,128)}) custom-call(bf16[32,384,128]{2,1,0:T(8,128)(2,1)S(1)} %bitcast.50, bf16[32,384,128]{2,1,0:T(8,128)(2,1)} %collective-permute-done.3.b1, bf16[32,384,128]{2,1,0:T(8,128)(2,1)} %collective-permute-done.4.b2, bf16[32,384,128]{2,1,0:T(8,128)(2,1)} %collective-permute-done.5.b3), custom_call_target="tpu_custom_call" | custom-call | tf_op jit(solution)/shard_map/pallas_call | solution.py:92
  208.8 3.4 copy-done
  212.1 18.7 %shard_map.41 = f32[256,256]{1,0:T(8,128)S(1)} custom-call(s32[5]{0:T(128)S(1)} %stack.36.where, bf16[2048,384]{1,0:T(8,128)(2,1)} %constant_dynamic-update-slice_fusion.2.held, bf16[2048,384]{1,0:T(8,128)(2,1)} %collective-permute-done.12.far, bf16[2048,384]{1,0:T(8,128)(2,1)} %collective-permute-done.13.end, ...), custom_call_target="tpu_custom_call" | custom-call | flops 15032385536 | bytes 24117248 | tf_op jit(solution)/shard_map/pallas_call | solution.py:115
  230.9 18.1 %shard_map.40 = f32[256,256]{1,0:T(8,128)S(1)} custom-call(s32[5]{0:T(128)S(1)} %stack.36.where, bf16[2048,384]{1,0:T(8,128)(2,1)S(1)} %copy-done.6, bf16[2048,384]{1,0:T(8,128)(2,1)} %collective-permute-done.9.far, bf16[2048,384]{1,0:T(8,128)(2,1)} %collective-permute-done.10.end, bf16[32,1536,128]{2,1,0:T(8,128)(2,1)S(1)} %get-tuple-element.20.b_ref, ...), custom_call_target="tpu_custom_call" | custom-call | flops 15032385536 | bytes 24117248 | tf_op jit(solution)/shard_map/pallas_call | solution.py:115
  254.1 12.1 %collective-permute-done.7.end = bf16[1024,384]{1,0:T(8,128)(2,1)S(1)} collective-permute-done((bf16[1024,384]{1,0:T(8,128)(2,1)}, bf16[1024,384]{1,0:T(8,128)(2,1)S(1)}, u32[]{:S(2)}, u32[]{:S(2)}) %collective-permute-start.7) | collective-permute-done | bytes 786464 | tf_op jit(solution)/shard_map/ppermute | solution.py:195
  266.9 10.1 %shard_map.38.r_ref = f32[256,256]{1,0:T(8,128)S(1)} custom-call(s32[5]{0:T(128)S(1)} %stack.36.where, bf16[1024,384]{1,0:T(8,128)(2,1)} %pad_maximum_fusion.1.held, bf16[1024,384]{1,0:T(8,128)(2,1)} %collective-permute-done.6.far, bf16[1024,384]{1,0:T(8,128)(2,1)S(1)} %collective-permute-done.7.end, bf16[32,1536,128]{2,1,0:T(8,128)(2,1)S(1)} %get-tuple-element.20.b_ref, ...), custom_call_target="tpu_custom_call" | custom-call | flops 7516192768 | bytes 18350080 | tf_op jit(solution)/shard_map/pallas_call | solution.py:115
  277.2 3.5 %collective-permute-start.15 = (f32[256,256]{1,0:T(8,128)S(1)}, f32[256,256]{1,0:T(8,128)S(1)}, u32[]{:S(2)}, u32[]{:S(2)}) collective-permute-start(f32[256,256]{1,0:T(8,128)S(1)} %dynamic-slice_bitcast_fusion), channel_id=1, source_target_pairs={{0,2},{2,0},{4,6},{6,4},{8,10},{10,8},{12,14},{14,12},{16,18},{18,... | collective-permute-start | bytes 786440 | tf_op jit(solution)/shard_map/ppermute | solution.py:185
  282.1 9.7 %shard_map.39 = f32[256,256]{1,0:T(8,128)S(1)} custom-call(s32[5]{0:T(128)S(1)} %stack.36.where, bf16[1024,384]{1,0:T(8,128)(2,1)S(1)} %copy-done.4, bf16[1024,384]{1,0:T(8,128)(2,1)S(1)} %copy-done.8, bf16[1024,384]{1,0:T(8,128)(2,1)S(1)} %collective-permute-done.2.end, bf16[32,1536,128]{2,1,0:T(8,128)(2,1)S(1)} %get-tuple-element.20.b_ref, ...), custom_call_target="tpu_custom_call" | custom-call | flops 7516192768 | bytes 18350080 | tf_op jit(solution)/shard_map/pallas_call | solution.py:115
  295.8 12.4 %collective-permute-done.22.end = bf16[768,384]{1,0:T(8,128)(2,1)S(1)} collective-permute-done((bf16[768,384]{1,0:T(8,128)(2,1)S(1)}, bf16[768,384]{1,0:T(8,128)(2,1)S(1)}, u32[]{:S(2)}, u32[]{:S(2)}) %collective-permute-start.22) | collective-permute-done | bytes 589856 | tf_op jit(solution)/shard_map/ppermute | solution.py:195
  308.2 7.5 %shard_map.42.r_ref = f32[256,256]{1,0:T(8,128)S(1)} custom-call(s32[5]{0:T(128)S(1)} %stack.36.where, bf16[768,384]{1,0:T(8,128)(2,1)S(1)} %pad_maximum_fusion.3.held, bf16[768,384]{1,0:T(8,128)(2,1)S(1)} %collective-permute-done.21.far, bf16[768,384]{1,0:T(8,128)(2,1)S(1)} %collective-permute-done.22.end, ...), custom_call_target="tpu_custom_call" | custom-call | flops 5637144576 | bytes 16908288 | tf_op jit(solution)/shard_map/pallas_call | solution.py:115
  315.7 6.1 %collective-permute-done.20.end = bf16[768,384]{1,0:T(8,128)(2,1)S(1)} collective-permute-done((bf16[768,384]{1,0:T(8,128)(2,1)S(1)}, bf16[768,384]{1,0:T(8,128)(2,1)S(1)}, u32[]{:S(2)}, u32[]{:S(2)}) %collective-permute-start.20) | collective-permute-done | bytes 589856 | tf_op jit(solution)/shard_map/ppermute | solution.py:195
  321.8 7.5 %shard_map.43.r_ref = f32[256,256]{1,0:T(8,128)S(1)} custom-call(s32[5]{0:T(128)S(1)} %stack.36.where, bf16[768,384]{1,0:T(8,128)(2,1)S(1)} %pad_maximum_fusion.2.held, bf16[768,384]{1,0:T(8,128)(2,1)S(1)} %collective-permute-done.19.far, bf16[768,384]{1,0:T(8,128)(2,1)S(1)} %collective-permute-done.20.end, ...), custom_call_target="tpu_custom_call" | custom-call | flops 5637144576 | bytes 16908288 | tf_op jit(solution)/shard_map/pallas_call | solution.py:115
  329.3 5.5 %shard_map.44 = f32[256,256]{1,0:T(8,128)S(1)} custom-call(s32[5]{0:T(128)S(1)} %stack.36.where, bf16[512,384]{1,0:T(8,128)(2,1)S(1)} %pad_maximum_fusion.5.held, bf16[512,384]{1,0:T(8,128)(2,1)S(1)} %collective-permute-done.17.far, bf16[512,384]{1,0:T(8,128)(2,1)S(1)} %collective-permute-done.18.end, bf16[32,1536,128]{2,1,0:T(8,128)(2,1)S(1)} %get-tuple-element.20.b_ref, ...), custom_call_target="tpu_custom_call" | custom-call | flops 3758096384 | bytes 15466496 | tf_op jit(solution)/shard_map/pallas_call | solution.py:115
  343.4 2.7 collective-permute-done.26
  (107 shorter events, 53.0 us)
Async XLA Ops:
  3.3 71.2 %collective-permute-start.4 = (bf16[32,384,128]{2,1,0:T(8,128)(2,1)S(1)}, bf16[32,384,128]{2,1,0:T(8,128)(2,1)}, u32[]{:S(2)}, u32[]{:S(2)}) collective-permute-start(bf16[32,384,128]{2,1,0:T(8,128)(2,1)S(1)} %bitcast.48), channel_id=1, source_target_pairs={{0,2},{1,3},{2,0},{3,1},{4,6},{5,7},{6,4},{7,5},{8,10},{9,11},{10,... | collective-permute-start | bytes 9437192 | tf_op jit(solution)/shard_map/ppermute | solution.py:171
  10.9 19.2 %collective-permute-start.11 = (bf16[1024,384]{1,0:T(8,128)(2,1)}, bf16[1024,384]{1,0:T(8,128)(2,1)S(1)}, u32[]{:S(2)}, u32[]{:S(2)}) collective-permute-start(bf16[1024,384]{1,0:T(8,128)(2,1)} %bitcast.56), channel_id=1, source_target_pairs={{0,4},{4,0},{8,12},{12,8},{1,5},{5,1},{9,13},{13,9},{2,6},{6,2},{1... | collective-permute-start | bytes 2359304 | tf_op jit(solution)/shard_map/ppermute | solution.py:170
  12.5 186.7 %collective-permute-start.3 = (bf16[32,384,128]{2,1,0:T(8,128)(2,1)S(1)}, bf16[32,384,128]{2,1,0:T(8,128)(2,1)}, u32[]{:S(2)}, u32[]{:S(2)}) collective-permute-start(bf16[32,384,128]{2,1,0:T(8,128)(2,1)S(1)} %bitcast.49), channel_id=1, source_target_pairs={{0,1},{1,0},{2,3},{3,2},{4,5},{5,4},{6,7},{7,6},{8,9},{9,8},{10,11... | collective-permute-start | bytes 9437192 | tf_op jit(solution)/shard_map/ppermute | solution.py:172
  74.5 125.9 %collective-permute-start.5 = (bf16[32,384,128]{2,1,0:T(8,128)(2,1)}, bf16[32,384,128]{2,1,0:T(8,128)(2,1)}, u32[]{:S(2)}, u32[]{:S(2)}) collective-permute-start(bf16[32,384,128]{2,1,0:T(8,128)(2,1)} %collective-permute-done.4.b2), channel_id=1, source_target_pairs={{0,1},{1,0},{2,3},{3,2},{4,5},{5,4},{6,7},{7,6},{8,9},{9,8},{10,11... | collective-permute-start | bytes 9437192 | tf_op jit(solution)/shard_map/ppermute | solution.py:173
  75.5 52.1 %collective-permute-start.12 = (bf16[2048,384]{1,0:T(8,128)(2,1)}, bf16[2048,384]{1,0:T(8,128)(2,1)}, u32[]{:S(2)}, u32[]{:S(2)}) collective-permute-start(bf16[2048,384]{1,0:T(8,128)(2,1)} %constant_dynamic-update-slice_fusion.2.held), channel_id=1, source_target_pairs={{4,8},{8,4},{5,9},{9,5},{6,10},{10,6},{7,11},{11,7},{20,24},{24,20... | collective-permute-start | bytes 4718600 | tf_op jit(solution)/shard_map/ppermute | solution.py:194
  80.0 22.2 %collective-permute-start = (bf16[1024,384]{1,0:T(8,128)(2,1)}, bf16[1024,384]{1,0:T(8,128)(2,1)}, u32[]{:S(2)}, u32[]{:S(2)}) collective-permute-start(bf16[1024,384]{1,0:T(8,128)(2,1)} %bitcast.63), channel_id=1, source_target_pairs={{0,4},{4,0},{8,12},{12,8},{1,5},{5,1},{9,13},{13,9},{2,6},{6,2},{1... | collective-permute-start | bytes 2359304 | tf_op jit(solution)/shard_map/ppermute | solution.py:170
  83.5 35.1 %collective-permute-start.8 = (bf16[384,8,128]{2,1,0:T(8,128)(2,1)}, bf16[384,8,128]{2,1,0:T(8,128)(2,1)}, u32[]{:S(2)}, u32[]{:S(2)}) collective-permute-start(bf16[384,8,128]{2,1,0:T(8,128)(2,1)} %get-tuple-element.32), channel_id=1, source_target_pairs={{0,4},{4,0},{8,12},{12,8},{1,5},{5,1},{9,13},{13,9},{2,6},{6,2},{1... | collective-permute-start | bytes 2359304 | tf_op jit(solution)/shard_map/ppermute | solution.py:169
  122.8 8.6 %collective-permute-start.9 = (bf16[2048,384]{1,0:T(8,128)(2,1)S(1)}, bf16[2048,384]{1,0:T(8,128)(2,1)}, u32[]{:S(2)}, u32[]{:S(2)}) collective-permute-start(bf16[2048,384]{1,0:T(8,128)(2,1)S(1)} %constant_dynamic-update-slice_fusion.held), channel_id=1, source_target_pairs={{4,8},{8,4},{5,9},{9,5},{6,10},{10,6},{7,11},{11,7},{20,24},{24,20... | collective-permute-start | bytes 4718600 | tf_op jit(solution)/shard_map/ppermute | solution.py:194
  127.6 81.1 %collective-permute-start.13 = (bf16[2048,384]{1,0:T(8,128)(2,1)}, bf16[2048,384]{1,0:T(8,128)(2,1)}, u32[]{:S(2)}, u32[]{:S(2)}) collective-permute-start(bf16[2048,384]{1,0:T(8,128)(2,1)} %collective-permute-done.12.far), channel_id=1, source_target_pairs={{4,0},{8,12},{5,1},{9,13},{6,2},{10,14},{7,3},{11,15},{20,16},{24,... | collective-permute-start | bytes 4718600 | tf_op jit(solution)/shard_map/ppermute | solution.py:195
  129.9 5.6 %collective-permute-start.6 = (bf16[1024,384]{1,0:T(8,128)(2,1)}, bf16[1024,384]{1,0:T(8,128)(2,1)}, u32[]{:S(2)}, u32[]{:S(2)}) collective-permute-start(bf16[1024,384]{1,0:T(8,128)(2,1)} %pad_maximum_fusion.1.held), channel_id=1, source_target_pairs={{4,8},{8,4},{5,9},{9,5},{6,10},{10,6},{7,11},{11,7},{20,24},{24,20... | collective-permute-start | bytes 2359304 | tf_op jit(solution)/shard_map/ppermute | solution.py:194
  131.5 99.3 %collective-permute-start.10 = (bf16[2048,384]{1,0:T(8,128)(2,1)}, bf16[2048,384]{1,0:T(8,128)(2,1)}, u32[]{:S(2)}, u32[]{:S(2)}) collective-permute-start(bf16[2048,384]{1,0:T(8,128)(2,1)} %collective-permute-done.9.far), channel_id=1, source_target_pairs={{4,0},{8,12},{5,1},{9,13},{6,2},{10,14},{7,3},{11,15},{20,16},{24,... | collective-permute-start | bytes 4718600 | tf_op jit(solution)/shard_map/ppermute | solution.py:195
  135.6 114.9 %collective-permute-start.16 = (bf16[1024,384]{1,0:T(8,128)(2,1)}, bf16[1024,384]{1,0:T(8,128)(2,1)S(1)}, u32[]{:S(2)}, u32[]{:S(2)}) collective-permute-start(bf16[1024,384]{1,0:T(8,128)(2,1)} %bitcast.60), channel_id=1, source_target_pairs={{0,4},{4,0},{8,12},{12,8},{1,5},{5,1},{9,13},{13,9},{2,6},{6,2},{1... | collective-permute-start | bytes 2359304 | tf_op jit(solution)/shard_map/ppermute | solution.py:170
  199.2 82.9 %collective-permute-start.2 = (bf16[1024,384]{1,0:T(8,128)(2,1)}, bf16[1024,384]{1,0:T(8,128)(2,1)S(1)}, u32[]{:S(2)}, u32[]{:S(2)}) collective-permute-start(bf16[1024,384]{1,0:T(8,128)(2,1)} %copy-done.7), channel_id=1, source_target_pairs={{4,0},{8,12},{5,1},{9,13},{6,2},{10,14},{7,3},{11,15},{20,16},{24,... | collective-permute-start | bytes 2359304 | tf_op jit(solution)/shard_map/ppermute | solution.py:195
  200.5 65.8 %collective-permute-start.7 = (bf16[1024,384]{1,0:T(8,128)(2,1)}, bf16[1024,384]{1,0:T(8,128)(2,1)S(1)}, u32[]{:S(2)}, u32[]{:S(2)}) collective-permute-start(bf16[1024,384]{1,0:T(8,128)(2,1)} %collective-permute-done.6.far), channel_id=1, source_target_pairs={{4,0},{8,12},{5,1},{9,13},{6,2},{10,14},{7,3},{11,15},{20,16},{24,... | collective-permute-start | bytes 2359304 | tf_op jit(solution)/shard_map/ppermute | solution.py:195
  249.0 28.0 %collective-permute-start.14 = (f32[2,256,256]{2,1,0:T(8,128)S(1)}, f32[2,256,256]{2,1,0:T(8,128)S(1)}, u32[]{:S(2)}, u32[]{:S(2)}) collective-permute-start(f32[2,256,256]{2,1,0:T(8,128)S(1)} %pad_maximum_fusion.4), channel_id=1, source_target_pairs={{1,0},{3,2},{5,4},{7,6},{9,8},{11,10},{13,12},{15,14},{17,16},{19,... | collective-permute-start | bytes 1572872 | tf_op jit(solution)/shard_map/ppermute | solution.py:182
  251.4 43.0 %collective-permute-start.17 = (bf16[512,384]{1,0:T(8,128)(2,1)S(1)}, bf16[512,384]{1,0:T(8,128)(2,1)S(1)}, u32[]{:S(2)}, u32[]{:S(2)}) collective-permute-start(bf16[512,384]{1,0:T(8,128)(2,1)S(1)} %pad_maximum_fusion.5.held), channel_id=1, source_target_pairs={{4,8},{8,4},{5,9},{9,5},{6,10},{10,6},{7,11},{11,7},{20,24},{24,20... | collective-permute-start | bytes 1179656 | tf_op jit(solution)/shard_map/ppermute | solution.py:194
  253.4 39.8 %collective-permute-start.19 = (bf16[768,384]{1,0:T(8,128)(2,1)S(1)}, bf16[768,384]{1,0:T(8,128)(2,1)S(1)}, u32[]{:S(2)}, u32[]{:S(2)}) collective-permute-start(bf16[768,384]{1,0:T(8,128)(2,1)S(1)} %pad_maximum_fusion.2.held), channel_id=1, source_target_pairs={{4,8},{8,4},{5,9},{9,5},{6,10},{10,6},{7,11},{11,7},{20,24},{24,20... | collective-permute-start | bytes 1769480 | tf_op jit(solution)/shard_map/ppermute | solution.py:194
  266.2 14.5 %collective-permute-start.21 = (bf16[768,384]{1,0:T(8,128)(2,1)S(1)}, bf16[768,384]{1,0:T(8,128)(2,1)S(1)}, u32[]{:S(2)}, u32[]{:S(2)}) collective-permute-start(bf16[768,384]{1,0:T(8,128)(2,1)S(1)} %pad_maximum_fusion.3.held), channel_id=1, source_target_pairs={{4,8},{8,4},{5,9},{9,5},{6,10},{10,6},{7,11},{11,7},{20,24},{24,20... | collective-permute-start | bytes 1769480 | tf_op jit(solution)/shard_map/ppermute | solution.py:194
  277.2 14.6 %collective-permute-start.15 = (f32[256,256]{1,0:T(8,128)S(1)}, f32[256,256]{1,0:T(8,128)S(1)}, u32[]{:S(2)}, u32[]{:S(2)}) collective-permute-start(f32[256,256]{1,0:T(8,128)S(1)} %dynamic-slice_bitcast_fusion), channel_id=1, source_target_pairs={{0,2},{2,0},{4,6},{6,4},{8,10},{10,8},{12,14},{14,12},{16,18},{18,... | collective-permute-start | bytes 786440 | tf_op jit(solution)/shard_map/ppermute | solution.py:185
  280.7 27.5 %collective-permute-start.22 = (bf16[768,384]{1,0:T(8,128)(2,1)S(1)}, bf16[768,384]{1,0:T(8,128)(2,1)S(1)}, u32[]{:S(2)}, u32[]{:S(2)}) collective-permute-start(bf16[768,384]{1,0:T(8,128)(2,1)S(1)} %collective-permute-done.21.far), channel_id=1, source_target_pairs={{4,0},{8,12},{5,1},{9,13},{6,2},{10,14},{7,3},{11,15},{20,16},{24,... | collective-permute-start | bytes 1769480 | tf_op jit(solution)/shard_map/ppermute | solution.py:195
  293.2 28.6 %collective-permute-start.20 = (bf16[768,384]{1,0:T(8,128)(2,1)S(1)}, bf16[768,384]{1,0:T(8,128)(2,1)S(1)}, u32[]{:S(2)}, u32[]{:S(2)}) collective-permute-start(bf16[768,384]{1,0:T(8,128)(2,1)S(1)} %collective-permute-done.19.far), channel_id=1, source_target_pairs={{4,0},{8,12},{5,1},{9,13},{6,2},{10,14},{7,3},{11,15},{20,16},{24,... | collective-permute-start | bytes 1769480 | tf_op jit(solution)/shard_map/ppermute | solution.py:195
  294.5 34.8 %collective-permute-start.18 = (bf16[512,384]{1,0:T(8,128)(2,1)S(1)}, bf16[512,384]{1,0:T(8,128)(2,1)S(1)}, u32[]{:S(2)}, u32[]{:S(2)}) collective-permute-start(bf16[512,384]{1,0:T(8,128)(2,1)S(1)} %collective-permute-done.17.far), channel_id=1, source_target_pairs={{4,0},{8,12},{5,1},{9,13},{6,2},{10,14},{7,3},{11,15},{20,16},{24,... | collective-permute-start | bytes 1179656 | tf_op jit(solution)/shard_map/ppermute | solution.py:195
  338.2 5.2 %collective-permute-start.27 = (f32[64,256]{1,0:T(8,128)S(1)}, f32[64,256]{1,0:T(8,128)S(1)}, u32[]{:S(2)}, u32[]{:S(2)}) collective-permute-start(f32[64,256]{1,0:T(8,128)S(1)} %get-tuple-element.45), channel_id=1, source_target_pairs={{0,8},{4,12},{8,0},{12,4},{1,9},{5,13},{9,1},{13,5},{2,10},{6,14},... | collective-permute-start | bytes 196616 | tf_op jit(solution)/shard_map/ppermute | solution.py:222
  340.1 6.1 %collective-permute-start.26 = (f32[64,256]{1,0:T(8,128)S(1)}, f32[64,256]{1,0:T(8,128)S(1)}, u32[]{:S(2)}, u32[]{:S(2)}) collective-permute-start(f32[64,256]{1,0:T(8,128)S(1)} %get-tuple-element.43), channel_id=1, source_target_pairs={{0,12},{4,8},{8,4},{12,0},{1,13},{5,9},{9,5},{13,1},{2,14},{6,10},... | collective-permute-start | bytes 196616 | tf_op jit(solution)/shard_map/ppermute | solution.py:222
  (21 other events, 124.2 us)

commit v8 on v7

--- a/solution.py
+++ b/solution.py
@@ -10,7 +10,7 @@
 
 F32 = jnp.float32
 ROWS = 8
-WIDE = 8
+WIDE = 16
 LIMIT = 24 * 2**20
 
 
@@ -64,7 +64,7 @@
 
     lax.fori_loop(0, b_count // WIDE, contract, 0)
     t_copy.wait()
-    group = 8
+    group = 16
     total = jnp.zeros(out_ref.shape, F32) if first else r_ref[...]
     for c in range(0, count, group):
         left = jnp.concatenate([i_v[c + m] for m in range(group)], axis=1)
@@ -235,7 +235,7 @@
         depth, a_count, c_count = factor_ac.shape
         _, b_count, width = factor_bd.shape
         fits = n_dev == 4 and n_col == 4 and width == 128 and depth % 128 == 0
-        fits = fits and a_count == ROWS * n_col and b_count % 8 == 0 and c_count % 64 == 0
+        fits = fits and a_count == ROWS * n_col and b_count % 16 == 0 and c_count % 128 == 0
         if fits:
             return laddered(n_dev, n_col, factor_ac, factor_bd, amplitudes)
         return plain(factor_ac, factor_bd, amplitudes)

time: 352 us -> 351 us (level)
  transfers between devices with their start and end apart: 29 -> 29, of which waited for: 10 -> 11; matrix products, arithmetic and copies ran while one was open for 7% -> 7% of each run, Pallas kernels for 22% -> 22%
where the time goes in v8:
time: 351 us; the launch traced here: 346 us
  waiting for transfers between devices  129 us (37%)
  starting transfers between devices  102 us (29%)
  Pallas kernels  79.6 us (23%)
  local copies, waits for them, and re-layouts  33.5 us (10%)
    pallas_call x7, Pallas kernels, block(): pl.pallas_call(functools.partial(block_kernel, first, rows, c_start), in_...  74.7 us
    ppermute x3, starting transfers between devices, laddered(): lax.ppermute(own[g], 'dev', shuffled(n_dev, 1))  68.7 us
    ppermute x1, waiting for transfers between devices, laddered(): across = lax.ppermute(turned_bd, 'col', shuffled(n_col, 2))  42.3 us
    ppermute x3, waiting for transfers between devices, laddered(): lax.ppermute(own[g], 'dev', shuffled(n_dev, 1))  33.6 us
    ppermute x7, waiting for transfers between devices, send(): ready.append((g, i, c0, held, far, lax.ppermute(far, 'dev', TO_END)))  31.4 us
    ppermute x1, waiting for transfers between devices, laddered(): near = [turned(lax.ppermute(first, 'dev', shuffled(n_dev, 1)))]  16.4 us
    transpose x6, local copies, waits for them, and re-layouts, turned(): x.transpose(2, 1, 0).reshape(c_count * ROWS, depth)  15.3 us
    unnamed x35, local copies, waits for them, and re-layouts  13.7 us
  transfers between devices with their start and end apart: 29, of which 11 were waited for; matrix products, arithmetic and copies ran while one was open for 7% of the time, Pallas kernels for 22%

profile of v8, /device:TPU:0, one launch (start us, length us, event | category | flops | bytes accessed | tf_op | source)
XLA Modules:
  0.0 345.8 jit_solution(2265833224811574407)
XLA Ops:
  0.0 3.3 copy.18
  3.3 3.0 collective-permute-start.4
  12.5 17.6 %collective-permute-done.11 = bf16[1024,384]{1,0:T(8,128)(2,1)S(1)} collective-permute-done((bf16[1024,384]{1,0:T(8,128)(2,1)}, bf16[1024,384]{1,0:T(8,128)(2,1)S(1)}, u32[]{:S(2)}, u32[]{:S(2)}) %collective-permute-start.11) | collective-permute-done | bytes 786464 | tf_op jit(solution)/shard_map/ppermute | solution.py:170
  32.2 42.3 %collective-permute-done.4.b2 = bf16[32,384,128]{2,1,0:T(8,128)(2,1)} collective-permute-done((bf16[32,384,128]{2,1,0:T(8,128)(2,1)S(1)}, bf16[32,384,128]{2,1,0:T(8,128)(2,1)}, u32[]{:S(2)}, u32[]{:S(2)}) %collective-permute-start.4) | collective-permute-done | bytes 3145760 | tf_op jit(solution)/shard_map/ppermute | solution.py:171
  80.0 3.5 %collective-permute-start = (bf16[1024,384]{1,0:T(8,128)(2,1)}, bf16[1024,384]{1,0:T(8,128)(2,1)}, u32[]{:S(2)}, u32[]{:S(2)}) collective-permute-start(bf16[1024,384]{1,0:T(8,128)(2,1)} %bitcast.63), channel_id=1, source_target_pairs={{0,4},{4,0},{8,12},{12,8},{1,5},{5,1},{9,13},{13,9},{2,6},{6,2},{1... | collective-permute-start | bytes 2359304 | tf_op jit(solution)/shard_map/ppermute | solution.py:170
  83.5 2.7 copy.12
  86.2 16.0 %collective-permute-done = bf16[1024,384]{1,0:T(8,128)(2,1)} collective-permute-done((bf16[1024,384]{1,0:T(8,128)(2,1)}, bf16[1024,384]{1,0:T(8,128)(2,1)}, u32[]{:S(2)}, u32[]{:S(2)}) %collective-permute-start) | collective-permute-done | bytes 786464 | tf_op jit(solution)/shard_map/ppermute | solution.py:170
  102.2 16.4 %collective-permute-done.8 = bf16[384,8,128]{2,1,0:T(8,128)(2,1)} collective-permute-done((bf16[384,8,128]{2,1,0:T(8,128)(2,1)}, bf16[384,8,128]{2,1,0:T(8,128)(2,1)}, u32[]{:S(2)}, u32[]{:S(2)}) %collective-permute-start.8) | collective-permute-done | bytes 786464 | tf_op jit(solution)/shard_map/ppermute | solution.py:169
  118.6 2.7 copy.13
  135.6 63.6 %collective-permute-start.16 = (bf16[1024,384]{1,0:T(8,128)(2,1)}, bf16[1024,384]{1,0:T(8,128)(2,1)S(1)}, u32[]{:S(2)}, u32[]{:S(2)}) collective-permute-start(bf16[1024,384]{1,0:T(8,128)(2,1)} %bitcast.60), channel_id=1, source_target_pairs={{0,4},{4,0},{8,12},{12,8},{1,5},{5,1},{9,13},{13,9},{2,6},{6,2},{1... | collective-permute-start | bytes 2359304 | tf_op jit(solution)/shard_map/ppermute | solution.py:170
  203.8 4.9 %shard_map.37 = (bf16[32,1536,128]{2,1,0:T(8,128)(2,1)S(1)}, f32[8,128]{1,0:T(8,128)}) custom-call(bf16[32,384,128]{2,1,0:T(8,128)(2,1)S(1)} %bitcast.50, bf16[32,384,128]{2,1,0:T(8,128)(2,1)} %collective-permute-done.3.b1, bf16[32,384,128]{2,1,0:T(8,128)(2,1)} %collective-permute-done.4.b2, bf16[32,384,128]{2,1,0:T(8,128)(2,1)} %collective-permute-done.5.b3), custom_call_target="tpu_custom_call" | custom-call | tf_op jit(solution)/shard_map/pallas_call | solution.py:92
  208.8 3.4 copy-done
  212.1 18.3 %shard_map.41 = f32[256,256]{1,0:T(8,128)S(1)} custom-call(s32[5]{0:T(128)S(1)} %stack.36.where, bf16[2048,384]{1,0:T(8,128)(2,1)} %constant_dynamic-update-slice_fusion.2.held, bf16[2048,384]{1,0:T(8,128)(2,1)} %collective-permute-done.12.far, bf16[2048,384]{1,0:T(8,128)(2,1)} %collective-permute-done.13.end, ...), custom_call_target="tpu_custom_call" | custom-call | flops 15032385536 | bytes 24117248 | tf_op jit(solution)/shard_map/pallas_call | solution.py:115
  230.5 17.8 %shard_map.40 = f32[256,256]{1,0:T(8,128)S(1)} custom-call(s32[5]{0:T(128)S(1)} %stack.36.where, bf16[2048,384]{1,0:T(8,128)(2,1)S(1)} %copy-done.6, bf16[2048,384]{1,0:T(8,128)(2,1)} %collective-permute-done.9.far, bf16[2048,384]{1,0:T(8,128)(2,1)} %collective-permute-done.10.end, bf16[32,1536,128]{2,1,0:T(8,128)(2,1)S(1)} %get-tuple-element.20.b_ref, ...), custom_call_target="tpu_custom_call" | custom-call | flops 15032385536 | bytes 24117248 | tf_op jit(solution)/shard_map/pallas_call | solution.py:115
  253.5 12.7 %collective-permute-done.7.end = bf16[1024,384]{1,0:T(8,128)(2,1)S(1)} collective-permute-done((bf16[1024,384]{1,0:T(8,128)(2,1)}, bf16[1024,384]{1,0:T(8,128)(2,1)S(1)}, u32[]{:S(2)}, u32[]{:S(2)}) %collective-permute-start.7) | collective-permute-done | bytes 786464 | tf_op jit(solution)/shard_map/ppermute | solution.py:195
  267.1 9.8 %shard_map.38.r_ref = f32[256,256]{1,0:T(8,128)S(1)} custom-call(s32[5]{0:T(128)S(1)} %stack.36.where, bf16[1024,384]{1,0:T(8,128)(2,1)} %pad_maximum_fusion.1.held, bf16[1024,384]{1,0:T(8,128)(2,1)} %collective-permute-done.6.far, bf16[1024,384]{1,0:T(8,128)(2,1)S(1)} %collective-permute-done.7.end, bf16[32,1536,128]{2,1,0:T(8,128)(2,1)S(1)} %get-tuple-element.20.b_ref, ...), custom_call_target="tpu_custom_call" | custom-call | flops 7516192768 | bytes 18350080 | tf_op jit(solution)/shard_map/pallas_call | solution.py:115
  277.1 3.5 %collective-permute-start.15 = (f32[256,256]{1,0:T(8,128)S(1)}, f32[256,256]{1,0:T(8,128)S(1)}, u32[]{:S(2)}, u32[]{:S(2)}) collective-permute-start(f32[256,256]{1,0:T(8,128)S(1)} %dynamic-slice_bitcast_fusion), channel_id=1, source_target_pairs={{0,2},{2,0},{4,6},{6,4},{8,10},{10,8},{12,14},{14,12},{16,18},{18,... | collective-permute-start | bytes 786440 | tf_op jit(solution)/shard_map/ppermute | solution.py:185
  281.9 9.2 %shard_map.39 = f32[256,256]{1,0:T(8,128)S(1)} custom-call(s32[5]{0:T(128)S(1)} %stack.36.where, bf16[1024,384]{1,0:T(8,128)(2,1)S(1)} %copy-done.4, bf16[1024,384]{1,0:T(8,128)(2,1)S(1)} %copy-done.8, bf16[1024,384]{1,0:T(8,128)(2,1)S(1)} %collective-permute-done.2.end, bf16[32,1536,128]{2,1,0:T(8,128)(2,1)S(1)} %get-tuple-element.20.b_ref, ...), custom_call_target="tpu_custom_call" | custom-call | flops 7516192768 | bytes 18350080 | tf_op jit(solution)/shard_map/pallas_call | solution.py:115
  295.1 12.8 %collective-permute-done.22.end = bf16[768,384]{1,0:T(8,128)(2,1)S(1)} collective-permute-done((bf16[768,384]{1,0:T(8,128)(2,1)S(1)}, bf16[768,384]{1,0:T(8,128)(2,1)S(1)}, u32[]{:S(2)}, u32[]{:S(2)}) %collective-permute-start.22) | collective-permute-done | bytes 589856 | tf_op jit(solution)/shard_map/ppermute | solution.py:195
  307.9 7.1 %shard_map.42.r_ref = f32[256,256]{1,0:T(8,128)S(1)} custom-call(s32[5]{0:T(128)S(1)} %stack.36.where, bf16[768,384]{1,0:T(8,128)(2,1)S(1)} %pad_maximum_fusion.3.held, bf16[768,384]{1,0:T(8,128)(2,1)S(1)} %collective-permute-done.21.far, bf16[768,384]{1,0:T(8,128)(2,1)S(1)} %collective-permute-done.22.end, ...), custom_call_target="tpu_custom_call" | custom-call | flops 5637144576 | bytes 16908288 | tf_op jit(solution)/shard_map/pallas_call | solution.py:115
  315.1 5.5 %collective-permute-done.20.end = bf16[768,384]{1,0:T(8,128)(2,1)S(1)} collective-permute-done((bf16[768,384]{1,0:T(8,128)(2,1)S(1)}, bf16[768,384]{1,0:T(8,128)(2,1)S(1)}, u32[]{:S(2)}, u32[]{:S(2)}) %collective-permute-start.20) | collective-permute-done | bytes 589856 | tf_op jit(solution)/shard_map/ppermute | solution.py:195
  320.6 7.4 %shard_map.43.r_ref = f32[256,256]{1,0:T(8,128)S(1)} custom-call(s32[5]{0:T(128)S(1)} %stack.36.where, bf16[768,384]{1,0:T(8,128)(2,1)S(1)} %pad_maximum_fusion.2.held, bf16[768,384]{1,0:T(8,128)(2,1)S(1)} %collective-permute-done.19.far, bf16[768,384]{1,0:T(8,128)(2,1)S(1)} %collective-permute-done.20.end, ...), custom_call_target="tpu_custom_call" | custom-call | flops 5637144576 | bytes 16908288 | tf_op jit(solution)/shard_map/pallas_call | solution.py:115
  328.4 5.1 %shard_map.44 = f32[256,256]{1,0:T(8,128)S(1)} custom-call(s32[5]{0:T(128)S(1)} %stack.36.where, bf16[512,384]{1,0:T(8,128)(2,1)S(1)} %pad_maximum_fusion.5.held, bf16[512,384]{1,0:T(8,128)(2,1)S(1)} %collective-permute-done.17.far, bf16[512,384]{1,0:T(8,128)(2,1)S(1)} %collective-permute-done.18.end, bf16[32,1536,128]{2,1,0:T(8,128)(2,1)S(1)} %get-tuple-element.20.b_ref, ...), custom_call_target="tpu_custom_call" | custom-call | flops 3758096384 | bytes 15466496 | tf_op jit(solution)/shard_map/pallas_call | solution.py:115
  342.4 2.7 collective-permute-done.26
  (107 shorter events, 53.8 us)
Async XLA Ops:
  3.3 71.2 %collective-permute-start.4 = (bf16[32,384,128]{2,1,0:T(8,128)(2,1)S(1)}, bf16[32,384,128]{2,1,0:T(8,128)(2,1)}, u32[]{:S(2)}, u32[]{:S(2)}) collective-permute-start(bf16[32,384,128]{2,1,0:T(8,128)(2,1)S(1)} %bitcast.48), channel_id=1, source_target_pairs={{0,2},{1,3},{2,0},{3,1},{4,6},{5,7},{6,4},{7,5},{8,10},{9,11},{10,... | collective-permute-start | bytes 9437192 | tf_op jit(solution)/shard_map/ppermute | solution.py:171
  10.9 19.2 %collective-permute-start.11 = (bf16[1024,384]{1,0:T(8,128)(2,1)}, bf16[1024,384]{1,0:T(8,128)(2,1)S(1)}, u32[]{:S(2)}, u32[]{:S(2)}) collective-permute-start(bf16[1024,384]{1,0:T(8,128)(2,1)} %bitcast.56), channel_id=1, source_target_pairs={{0,4},{4,0},{8,12},{12,8},{1,5},{5,1},{9,13},{13,9},{2,6},{6,2},{1... | collective-permute-start | bytes 2359304 | tf_op jit(solution)/shard_map/ppermute | solution.py:170
  12.5 186.7 %collective-permute-start.3 = (bf16[32,384,128]{2,1,0:T(8,128)(2,1)S(1)}, bf16[32,384,128]{2,1,0:T(8,128)(2,1)}, u32[]{:S(2)}, u32[]{:S(2)}) collective-permute-start(bf16[32,384,128]{2,1,0:T(8,128)(2,1)S(1)} %bitcast.49), channel_id=1, source_target_pairs={{0,1},{1,0},{2,3},{3,2},{4,5},{5,4},{6,7},{7,6},{8,9},{9,8},{10,11... | collective-permute-start | bytes 9437192 | tf_op jit(solution)/shard_map/ppermute | solution.py:172
  74.5 125.9 %collective-permute-start.5 = (bf16[32,384,128]{2,1,0:T(8,128)(2,1)}, bf16[32,384,128]{2,1,0:T(8,128)(2,1)}, u32[]{:S(2)}, u32[]{:S(2)}) collective-permute-start(bf16[32,384,128]{2,1,0:T(8,128)(2,1)} %collective-permute-done.4.b2), channel_id=1, source_target_pairs={{0,1},{1,0},{2,3},{3,2},{4,5},{5,4},{6,7},{7,6},{8,9},{9,8},{10,11... | collective-permute-start | bytes 9437192 | tf_op jit(solution)/shard_map/ppermute | solution.py:173
  75.5 52.1 %collective-permute-start.12 = (bf16[2048,384]{1,0:T(8,128)(2,1)}, bf16[2048,384]{1,0:T(8,128)(2,1)}, u32[]{:S(2)}, u32[]{:S(2)}) collective-permute-start(bf16[2048,384]{1,0:T(8,128)(2,1)} %constant_dynamic-update-slice_fusion.2.held), channel_id=1, source_target_pairs={{4,8},{8,4},{5,9},{9,5},{6,10},{10,6},{7,11},{11,7},{20,24},{24,20... | collective-permute-start | bytes 4718600 | tf_op jit(solution)/shard_map/ppermute | solution.py:194
  80.0 22.2 %collective-permute-start = (bf16[1024,384]{1,0:T(8,128)(2,1)}, bf16[1024,384]{1,0:T(8,128)(2,1)}, u32[]{:S(2)}, u32[]{:S(2)}) collective-permute-start(bf16[1024,384]{1,0:T(8,128)(2,1)} %bitcast.63), channel_id=1, source_target_pairs={{0,4},{4,0},{8,12},{12,8},{1,5},{5,1},{9,13},{13,9},{2,6},{6,2},{1... | collective-permute-start | bytes 2359304 | tf_op jit(solution)/shard_map/ppermute | solution.py:170
  83.5 35.1 %collective-permute-start.8 = (bf16[384,8,128]{2,1,0:T(8,128)(2,1)}, bf16[384,8,128]{2,1,0:T(8,128)(2,1)}, u32[]{:S(2)}, u32[]{:S(2)}) collective-permute-start(bf16[384,8,128]{2,1,0:T(8,128)(2,1)} %get-tuple-element.32), channel_id=1, source_target_pairs={{0,4},{4,0},{8,12},{12,8},{1,5},{5,1},{9,13},{13,9},{2,6},{6,2},{1... | collective-permute-start | bytes 2359304 | tf_op jit(solution)/shard_map/ppermute | solution.py:169
  122.8 8.6 %collective-permute-start.9 = (bf16[2048,384]{1,0:T(8,128)(2,1)S(1)}, bf16[2048,384]{1,0:T(8,128)(2,1)}, u32[]{:S(2)}, u32[]{:S(2)}) collective-permute-start(bf16[2048,384]{1,0:T(8,128)(2,1)S(1)} %constant_dynamic-update-slice_fusion.held), channel_id=1, source_target_pairs={{4,8},{8,4},{5,9},{9,5},{6,10},{10,6},{7,11},{11,7},{20,24},{24,20... | collective-permute-start | bytes 4718600 | tf_op jit(solution)/shard_map/ppermute | solution.py:194
  127.6 81.1 %collective-permute-start.13 = (bf16[2048,384]{1,0:T(8,128)(2,1)}, bf16[2048,384]{1,0:T(8,128)(2,1)}, u32[]{:S(2)}, u32[]{:S(2)}) collective-permute-start(bf16[2048,384]{1,0:T(8,128)(2,1)} %collective-permute-done.12.far), channel_id=1, source_target_pairs={{4,0},{8,12},{5,1},{9,13},{6,2},{10,14},{7,3},{11,15},{20,16},{24,... | collective-permute-start | bytes 4718600 | tf_op jit(solution)/shard_map/ppermute | solution.py:195
  129.9 5.6 %collective-permute-start.6 = (bf16[1024,384]{1,0:T(8,128)(2,1)}, bf16[1024,384]{1,0:T(8,128)(2,1)}, u32[]{:S(2)}, u32[]{:S(2)}) collective-permute-start(bf16[1024,384]{1,0:T(8,128)(2,1)} %pad_maximum_fusion.1.held), channel_id=1, source_target_pairs={{4,8},{8,4},{5,9},{9,5},{6,10},{10,6},{7,11},{11,7},{20,24},{24,20... | collective-permute-start | bytes 2359304 | tf_op jit(solution)/shard_map/ppermute | solution.py:194
  131.5 99.0 %collective-permute-start.10 = (bf16[2048,384]{1,0:T(8,128)(2,1)}, bf16[2048,384]{1,0:T(8,128)(2,1)}, u32[]{:S(2)}, u32[]{:S(2)}) collective-permute-start(bf16[2048,384]{1,0:T(8,128)(2,1)} %collective-permute-done.9.far), channel_id=1, source_target_pairs={{4,0},{8,12},{5,1},{9,13},{6,2},{10,14},{7,3},{11,15},{20,16},{24,... | collective-permute-start | bytes 4718600 | tf_op jit(solution)/shard_map/ppermute | solution.py:195
  135.6 114.2 %collective-permute-start.16 = (bf16[1024,384]{1,0:T(8,128)(2,1)}, bf16[1024,384]{1,0:T(8,128)(2,1)S(1)}, u32[]{:S(2)}, u32[]{:S(2)}) collective-permute-start(bf16[1024,384]{1,0:T(8,128)(2,1)} %bitcast.60), channel_id=1, source_target_pairs={{0,4},{4,0},{8,12},{12,8},{1,5},{5,1},{9,13},{13,9},{2,6},{6,2},{1... | collective-permute-start | bytes 2359304 | tf_op jit(solution)/shard_map/ppermute | solution.py:170
  199.2 82.8 %collective-permute-start.2 = (bf16[1024,384]{1,0:T(8,128)(2,1)}, bf16[1024,384]{1,0:T(8,128)(2,1)S(1)}, u32[]{:S(2)}, u32[]{:S(2)}) collective-permute-start(bf16[1024,384]{1,0:T(8,128)(2,1)} %copy-done.7), channel_id=1, source_target_pairs={{4,0},{8,12},{5,1},{9,13},{6,2},{10,14},{7,3},{11,15},{20,16},{24,... | collective-permute-start | bytes 2359304 | tf_op jit(solution)/shard_map/ppermute | solution.py:195
  200.5 65.8 %collective-permute-start.7 = (bf16[1024,384]{1,0:T(8,128)(2,1)}, bf16[1024,384]{1,0:T(8,128)(2,1)S(1)}, u32[]{:S(2)}, u32[]{:S(2)}) collective-permute-start(bf16[1024,384]{1,0:T(8,128)(2,1)} %collective-permute-done.6.far), channel_id=1, source_target_pairs={{4,0},{8,12},{5,1},{9,13},{6,2},{10,14},{7,3},{11,15},{20,16},{24,... | collective-permute-start | bytes 2359304 | tf_op jit(solution)/shard_map/ppermute | solution.py:195
  248.3 28.6 %collective-permute-start.14 = (f32[2,256,256]{2,1,0:T(8,128)S(1)}, f32[2,256,256]{2,1,0:T(8,128)S(1)}, u32[]{:S(2)}, u32[]{:S(2)}) collective-permute-start(f32[2,256,256]{2,1,0:T(8,128)S(1)} %pad_maximum_fusion.4), channel_id=1, source_target_pairs={{1,0},{3,2},{5,4},{7,6},{9,8},{11,10},{13,12},{15,14},{17,16},{19,... | collective-permute-start | bytes 1572872 | tf_op jit(solution)/shard_map/ppermute | solution.py:182
  250.8 43.0 %collective-permute-start.17 = (bf16[512,384]{1,0:T(8,128)(2,1)S(1)}, bf16[512,384]{1,0:T(8,128)(2,1)S(1)}, u32[]{:S(2)}, u32[]{:S(2)}) collective-permute-start(bf16[512,384]{1,0:T(8,128)(2,1)S(1)} %pad_maximum_fusion.5.held), channel_id=1, source_target_pairs={{4,8},{8,4},{5,9},{9,5},{6,10},{10,6},{7,11},{11,7},{20,24},{24,20... | collective-permute-start | bytes 1179656 | tf_op jit(solution)/shard_map/ppermute | solution.py:194
  252.7 39.8 %collective-permute-start.19 = (bf16[768,384]{1,0:T(8,128)(2,1)S(1)}, bf16[768,384]{1,0:T(8,128)(2,1)S(1)}, u32[]{:S(2)}, u32[]{:S(2)}) collective-permute-start(bf16[768,384]{1,0:T(8,128)(2,1)S(1)} %pad_maximum_fusion.2.held), channel_id=1, source_target_pairs={{4,8},{8,4},{5,9},{9,5},{6,10},{10,6},{7,11},{11,7},{20,24},{24,20... | collective-permute-start | bytes 1769480 | tf_op jit(solution)/shard_map/ppermute | solution.py:194
  266.2 14.4 %collective-permute-start.21 = (bf16[768,384]{1,0:T(8,128)(2,1)S(1)}, bf16[768,384]{1,0:T(8,128)(2,1)S(1)}, u32[]{:S(2)}, u32[]{:S(2)}) collective-permute-start(bf16[768,384]{1,0:T(8,128)(2,1)S(1)} %pad_maximum_fusion.3.held), channel_id=1, source_target_pairs={{4,8},{8,4},{5,9},{9,5},{6,10},{10,6},{7,11},{11,7},{20,24},{24,20... | collective-permute-start | bytes 1769480 | tf_op jit(solution)/shard_map/ppermute | solution.py:194
  277.1 14.0 %collective-permute-start.15 = (f32[256,256]{1,0:T(8,128)S(1)}, f32[256,256]{1,0:T(8,128)S(1)}, u32[]{:S(2)}, u32[]{:S(2)}) collective-permute-start(f32[256,256]{1,0:T(8,128)S(1)} %dynamic-slice_bitcast_fusion), channel_id=1, source_target_pairs={{0,2},{2,0},{4,6},{6,4},{8,10},{10,8},{12,14},{14,12},{16,18},{18,... | collective-permute-start | bytes 786440 | tf_op jit(solution)/shard_map/ppermute | solution.py:185
  280.6 27.3 %collective-permute-start.22 = (bf16[768,384]{1,0:T(8,128)(2,1)S(1)}, bf16[768,384]{1,0:T(8,128)(2,1)S(1)}, u32[]{:S(2)}, u32[]{:S(2)}) collective-permute-start(bf16[768,384]{1,0:T(8,128)(2,1)S(1)} %collective-permute-done.21.far), channel_id=1, source_target_pairs={{4,0},{8,12},{5,1},{9,13},{6,2},{10,14},{7,3},{11,15},{20,16},{24,... | collective-permute-start | bytes 1769480 | tf_op jit(solution)/shard_map/ppermute | solution.py:195
  292.5 28.1 %collective-permute-start.20 = (bf16[768,384]{1,0:T(8,128)(2,1)S(1)}, bf16[768,384]{1,0:T(8,128)(2,1)S(1)}, u32[]{:S(2)}, u32[]{:S(2)}) collective-permute-start(bf16[768,384]{1,0:T(8,128)(2,1)S(1)} %collective-permute-done.19.far), channel_id=1, source_target_pairs={{4,0},{8,12},{5,1},{9,13},{6,2},{10,14},{7,3},{11,15},{20,16},{24,... | collective-permute-start | bytes 1769480 | tf_op jit(solution)/shard_map/ppermute | solution.py:195
  293.8 34.6 %collective-permute-start.18 = (bf16[512,384]{1,0:T(8,128)(2,1)S(1)}, bf16[512,384]{1,0:T(8,128)(2,1)S(1)}, u32[]{:S(2)}, u32[]{:S(2)}) collective-permute-start(bf16[512,384]{1,0:T(8,128)(2,1)S(1)} %collective-permute-done.17.far), channel_id=1, source_target_pairs={{4,0},{8,12},{5,1},{9,13},{6,2},{10,14},{7,3},{11,15},{20,16},{24,... | collective-permute-start | bytes 1179656 | tf_op jit(solution)/shard_map/ppermute | solution.py:195
  337.1 5.2 %collective-permute-start.27 = (f32[64,256]{1,0:T(8,128)S(1)}, f32[64,256]{1,0:T(8,128)S(1)}, u32[]{:S(2)}, u32[]{:S(2)}) collective-permute-start(f32[64,256]{1,0:T(8,128)S(1)} %get-tuple-element.45), channel_id=1, source_target_pairs={{0,8},{4,12},{8,0},{12,4},{1,9},{5,13},{9,1},{13,5},{2,10},{6,14},... | collective-permute-start | bytes 196616 | tf_op jit(solution)/shard_map/ppermute | solution.py:222
  339.0 6.1 %collective-permute-start.26 = (f32[64,256]{1,0:T(8,128)S(1)}, f32[64,256]{1,0:T(8,128)S(1)}, u32[]{:S(2)}, u32[]{:S(2)}) collective-permute-start(f32[64,256]{1,0:T(8,128)S(1)} %get-tuple-element.43), channel_id=1, source_target_pairs={{0,12},{4,8},{8,4},{12,0},{1,13},{5,9},{9,5},{13,1},{2,14},{6,10},... | collective-permute-start | bytes 196616 | tf_op jit(solution)/shard_map/ppermute | solution.py:222
  (21 other events, 123.3 us)
